TPU v7x, 32 devices: a whole 2x2x4 slice. The times are simulated.
32 devices in a mesh: dp: 8 (over y, x, core), seq: 4 (over z).
Axes of the slice: x: 2, y: 2, z: 4, core: 2. Of those that a mesh axis runs over, the one named last changes fastest.
Arguments:
- tokens: bfloat16 [32, 1024, 768], P('dp', 'seq'), may hold values from -6 to 6
- cotangent: bfloat16 [32, 1024, 768], P('dp', 'seq'), may hold values from -6 to 6
- segments: int32 [32, 1024], P('dp'), may hold values from 0 to 4, as said below
- keep_flags: int32 [32, 8], P('dp'), may hold values 0 or 1
- first_gain: float32 [768], P('dp'), may hold values from 0.5 to 1.5
- first_shift: float32 [768], P('dp'), may hold values from -1.2 to 1.2
- joint_weight: float32 [768, 2304], P('dp'), may hold values from -0.21875 to 0.21875
- joint_bias: float32 [1536], P('dp'), may hold values from -1.2 to 1.2
- output_weight: float32 [768, 768], P('dp'), may hold values from -3 to 3
- output_bias: float32 [768], P('dp'), may hold values from -1.2 to 1.2
- second_gain: float32 [768], P('dp'), may hold values from 0.5 to 1.5
- second_shift: float32 [768], P('dp'), may hold values from -1.2 to 1.2
- expand_weight: float32 [768, 3072], P('dp'), may hold values from -0.21875 to 0.21875
- expand_bias: float32 [3072], P('dp'), may hold values from -1.2 to 1.2
- reduce_weight: float32 [3072, 768], P('dp'), may hold values from -0.109375 to 0.109375
- reduce_bias: float32 [768], P('dp'), may hold values from -1.2 to 1.2
Outputs:
- output: bfloat16 [32, 1024, 768], P('dp', 'seq')
- grad_tokens: float32 [32, 1024, 768], P('dp', 'seq')
- first_gain_grad: float32 [768], P('dp')
- first_shift_grad: float32 [768], P('dp')
- joint_weight_grad: float32 [768, 2304], P('dp')
- joint_bias_grad: float32 [1536], P('dp')
- output_weight_grad: float32 [768, 768], P('dp')
- output_bias_grad: float32 [768], P('dp')
- second_gain_grad: float32 [768], P('dp')
- second_shift_grad: float32 [768], P('dp')
- expand_weight_grad: float32 [768, 3072], P('dp')
- expand_bias_grad: float32 [3072], P('dp')
- reduce_weight_grad: float32 [3072, 768], P('dp')
- reduce_bias_grad: float32 [768], P('dp')
Inputs may be any that keep to these rules, and one draw needn't show every extreme that they name: `segments`: positions 0 to 7 of each row hold image p // 2 (class token at even p, distillation token at odd p); then the patch tokens of images 0 to 3 follow in this order, each image's patches contiguous and one or more; the rest of the row, never empty, is padding with the value 4. `keep_flags`: column i < 4 keeps the attention branch of image i, column 4 + i its feed-forward branch.
All inputs are finite; a program needn't handle non-finite values. No bound on the sum of `keep_flags` on one device may be relied on, other than what follows from the above.
Results may differ from a plain program's by a relative error of at most 0.012.
The roundings to bfloat16 on the way count: a program that leaves them out, or rounds other values in their place, can miss the bound.
Values may be sent and summed in bfloat16 or wider, within the bound.
No kernel may reach another device: no remote copies, remote signals or barrier semaphores. Data moves between devices by JAX's collectives and lax.ppermute only.
A program may use at most 192 MiB of HBM per device.

v0:
```python
import jax
import jax.numpy as jnp
from jax import lax
from jax.sharding import PartitionSpec as P

HEADS = 12
HEAD = 64


keep_ratio_inverse = 1.0 / 0.9
score_factor = 0.125
norm_epsilon = 1e-06


def normalize(inputs, gain, shift_b):
    centre = inputs - jnp.mean(inputs, axis=-1, keepdims=True)
    spread = jnp.mean(centre * centre, axis=-1, keepdims=True)
    return centre * lax.rsqrt(spread + norm_epsilon) * gain + shift_b


def gelu_exact(inputs):
    return jax.nn.gelu(inputs, approximate=False)


def matmul(left, right):
    return jnp.dot(left, right, preferred_element_type=jnp.float32)


def left_grad(inputs, grads):
    return lax.dot_general(
        inputs, grads, (((0,), (0,)), ((), ())), preferred_element_type=jnp.float32
    )


def right_grad(grads, weight):
    return lax.dot_general(
        grads, weight, (((1,), (1,)), ((), ())), preferred_element_type=jnp.float32
    )


def row_scores(queries, key_rows, seg_query, seg_key):
    raw_scores = (
        jnp.einsum("shd,lhd->hsl", queries, key_rows, preferred_element_type=jnp.float32)
        * score_factor
    )
    allowed = seg_query[:, None] == seg_key[None, :]
    return jnp.where(allowed[None, :, :], raw_scores, -1e30)


def row_forward(row_data):
    queries, key_rows, value_rows, seg_query, seg_key = row_data
    scores = row_scores(queries, key_rows, seg_query, seg_key)
    row_max = jnp.max(scores, axis=-1, keepdims=True)
    row_sum = jnp.sum(jnp.exp(scores - row_max), axis=-1, keepdims=True)
    log_total = row_max + jnp.log(row_sum)
    attention = jnp.exp(scores - log_total).astype(jnp.bfloat16)
    mixed_rows = jnp.einsum(
        "hsl,lhd->shd", attention, value_rows, preferred_element_type=jnp.float32
    )
    return (mixed_rows.astype(jnp.bfloat16), log_total)


def row_backward(row_data):
    queries, key_rows, value_rows, seg_query, seg_key, log_total, grad_mixed = row_data
    scores = row_scores(queries, key_rows, seg_query, seg_key)
    attention = jnp.exp(scores - log_total)
    grad_attention = jnp.einsum(
        "shd,lhd->hsl", grad_mixed, value_rows, preferred_element_type=jnp.float32
    )
    centre = jnp.sum(attention * grad_attention, axis=-1, keepdims=True)
    grad_scores = (attention * (grad_attention - centre)).astype(jnp.bfloat16)
    grad_queries = (
        jnp.einsum("hsl,lhd->shd", grad_scores, key_rows, preferred_element_type=jnp.float32)
        * score_factor
    )
    grad_keys = (
        jnp.einsum("hsl,shd->lhd", grad_scores, queries, preferred_element_type=jnp.float32)
        * score_factor
    )
    grad_values = jnp.einsum(
        "hsl,shd->lhd",
        attention.astype(jnp.bfloat16),
        grad_mixed,
        preferred_element_type=jnp.float32,
    )
    return (grad_queries, grad_keys, grad_values)


def shards(
    tokens,
    cotangent,
    segments,
    keep_flags,
    first_gain,
    first_shift,
    joint_weight,
    joint_bias,
    output_weight,
    output_bias,
    second_gain,
    second_shift,
    expand_weight,
    expand_bias,
    reduce_weight,
    reduce_bias,
):
    row_count, shard_len, features = tokens.shape
    row_len = segments.shape[1]
    images = keep_flags.shape[1] // 2
    token_count = row_count * shard_len
    offset_seq = lax.axis_index("seq") * shard_len
    seg_local = lax.dynamic_slice_in_dim(segments, offset_seq, shard_len, 1)
    labels = lax.broadcasted_iota(jnp.int32, (1, 1, images), 2)
    onehot = (seg_local[:, :, None] == labels).astype(jnp.float32)
    flags = keep_flags.astype(jnp.float32)
    attn_scale = (jnp.sum(onehot * flags[:, None, :images], axis=-1) * keep_ratio_inverse).reshape(
        token_count, 1
    )
    mlp_scale = (jnp.sum(onehot * flags[:, None, images:], axis=-1) * keep_ratio_inverse).reshape(
        token_count, 1
    )
    gain_a, shift_a, weight_qkv, bias_qv, weight_out, bias_out = (
        lax.all_gather(first_gain.astype(jnp.bfloat16), "dp", axis=0, tiled=True),
        lax.all_gather(first_shift.astype(jnp.bfloat16), "dp", axis=0, tiled=True),
        lax.all_gather(joint_weight.astype(jnp.bfloat16), "dp", axis=0, tiled=True),
        lax.all_gather(joint_bias.astype(jnp.bfloat16), "dp", axis=0, tiled=True),
        lax.all_gather(output_weight.astype(jnp.bfloat16), "dp", axis=0, tiled=True),
        lax.all_gather(output_bias.astype(jnp.bfloat16), "dp", axis=0, tiled=True),
    )
    flat_in = tokens.astype(jnp.float32).reshape(token_count, features)
    normed_a = normalize(flat_in, gain_a.astype(jnp.float32), shift_a.astype(jnp.float32)).astype(
        jnp.bfloat16
    )
    bias_full = jnp.concatenate(
        [
            bias_qv[:features].astype(jnp.float32),
            jnp.zeros((features,), jnp.float32),
            bias_qv[features:].astype(jnp.float32),
        ]
    )
    projected = (matmul(normed_a, weight_qkv) + bias_full).astype(jnp.bfloat16)
    queries = projected[:, :features].reshape(row_count, shard_len, HEADS, HEAD)
    key_local = projected[:, features : 2 * features].reshape(row_count, shard_len, features)
    value_local = projected[:, 2 * features :].reshape(row_count, shard_len, features)
    key_rows, value_rows = (
        lax.all_gather(key_local, "seq", axis=1, tiled=True),
        lax.all_gather(value_local, "seq", axis=1, tiled=True),
    )
    key_heads = key_rows.reshape(row_count, row_len, HEADS, HEAD)
    value_heads = value_rows.reshape(row_count, row_len, HEADS, HEAD)
    mixed_heads, log_total = lax.map(
        row_forward, (queries, key_heads, value_heads, seg_local, segments)
    )
    mixed_flat = mixed_heads.reshape(token_count, features)
    branch_a = matmul(mixed_flat, weight_out) + bias_out.astype(jnp.float32)
    middle = flat_in + attn_scale * branch_a
    gain_b, shift_bb, weight_up, bias_up, weight_down, bias_down = (
        lax.all_gather(second_gain.astype(jnp.bfloat16), "dp", axis=0, tiled=True),
        lax.all_gather(second_shift.astype(jnp.bfloat16), "dp", axis=0, tiled=True),
        lax.all_gather(expand_weight.astype(jnp.bfloat16), "dp", axis=0, tiled=True),
        lax.all_gather(expand_bias.astype(jnp.bfloat16), "dp", axis=0, tiled=True),
        lax.all_gather(reduce_weight.astype(jnp.bfloat16), "dp", axis=0, tiled=True),
        lax.all_gather(reduce_bias.astype(jnp.bfloat16), "dp", axis=0, tiled=True),
    )
    normed_b = normalize(middle, gain_b.astype(jnp.float32), shift_bb.astype(jnp.float32)).astype(
        jnp.bfloat16
    )
    pre_act = matmul(normed_b, weight_up) + bias_up.astype(jnp.float32)
    activated = gelu_exact(pre_act).astype(jnp.bfloat16)
    branch_b = matmul(activated, weight_down) + bias_down.astype(jnp.float32)
    output = (
        (middle + mlp_scale * branch_b).astype(jnp.bfloat16).reshape(row_count, shard_len, features)
    )
    grad_out = cotangent.astype(jnp.float32).reshape(token_count, features)
    grad_branch_b = (mlp_scale * grad_out).astype(jnp.bfloat16)
    g_reduce_weight = left_grad(activated, grad_branch_b)
    g_reduce_bias = jnp.sum(grad_branch_b, axis=0, dtype=jnp.float32)
    grad_activated = right_grad(grad_branch_b, weight_down)
    gelu_value, gelu_pull = jax.vjp(gelu_exact, pre_act)
    grad_pre = gelu_pull(grad_activated)[0].astype(jnp.bfloat16)
    g_expand_weight = left_grad(normed_b, grad_pre)
    g_expand_bias = jnp.sum(grad_pre, axis=0, dtype=jnp.float32)
    grad_normed_b = right_grad(grad_pre, weight_up)
    norm_value_b, norm_pull_b = jax.vjp(
        normalize, middle, gain_b.astype(jnp.float32), shift_bb.astype(jnp.float32)
    )
    grad_middle_norm, g_second_gain, g_second_shift = norm_pull_b(grad_normed_b)
    grad_middle = grad_out + grad_middle_norm
    grad_branch_a = (attn_scale * grad_middle).astype(jnp.bfloat16)
    g_output_weight = left_grad(mixed_flat, grad_branch_a)
    g_output_bias = jnp.sum(grad_branch_a, axis=0, dtype=jnp.float32)
    grad_mixed = (
        right_grad(grad_branch_a, weight_out)
        .astype(jnp.bfloat16)
        .reshape(row_count, shard_len, HEADS, HEAD)
    )
    grad_queries, grad_key_rows, grad_value_rows = lax.map(
        row_backward, (queries, key_heads, value_heads, seg_local, segments, log_total, grad_mixed)
    )
    key_sum, value_sum = (
        lax.psum_scatter(
            grad_key_rows.reshape(row_count, row_len, features),
            "seq",
            scatter_dimension=1,
            tiled=True,
        ),
        lax.psum_scatter(
            grad_value_rows.reshape(row_count, row_len, features),
            "seq",
            scatter_dimension=1,
            tiled=True,
        ),
    )
    grad_projected = jnp.concatenate(
        [
            grad_queries.reshape(token_count, features),
            key_sum.reshape(token_count, features),
            value_sum.reshape(token_count, features),
        ],
        axis=1,
    ).astype(jnp.bfloat16)
    g_joint_weight = left_grad(normed_a, grad_projected)
    column_sums = jnp.sum(grad_projected, axis=0, dtype=jnp.float32)
    g_joint_bias = jnp.concatenate([column_sums[:features], column_sums[2 * features :]])
    grad_normed_a = right_grad(grad_projected, weight_qkv)
    norm_value_a, norm_pull_a = jax.vjp(
        normalize, flat_in, gain_a.astype(jnp.float32), shift_a.astype(jnp.float32)
    )
    grad_in_norm, g_first_gain, g_first_shift = norm_pull_a(grad_normed_a)
    grad_tokens = (grad_middle + grad_in_norm).reshape(row_count, shard_len, features)
    every_shard = (
        lax.psum_scatter(g_first_gain, "dp", scatter_dimension=0, tiled=True),
        lax.psum_scatter(g_first_shift, "dp", scatter_dimension=0, tiled=True),
        lax.psum_scatter(g_joint_weight, "dp", scatter_dimension=0, tiled=True),
        lax.psum_scatter(g_joint_bias, "dp", scatter_dimension=0, tiled=True),
        lax.psum_scatter(g_output_weight, "dp", scatter_dimension=0, tiled=True),
        lax.psum_scatter(g_output_bias, "dp", scatter_dimension=0, tiled=True),
        lax.psum_scatter(g_second_gain, "dp", scatter_dimension=0, tiled=True),
        lax.psum_scatter(g_second_shift, "dp", scatter_dimension=0, tiled=True),
        lax.psum_scatter(g_expand_weight, "dp", scatter_dimension=0, tiled=True),
        lax.psum_scatter(g_expand_bias, "dp", scatter_dimension=0, tiled=True),
        lax.psum_scatter(g_reduce_weight, "dp", scatter_dimension=0, tiled=True),
        lax.psum_scatter(g_reduce_bias, "dp", scatter_dimension=0, tiled=True),
    )
    (
        s_first_gain,
        s_first_shift,
        s_joint_weight,
        s_joint_bias,
        s_output_weight,
        s_output_bias,
        s_second_gain,
        s_second_shift,
        s_expand_weight,
        s_expand_bias,
        s_reduce_weight,
        s_reduce_bias,
    ) = lax.psum(
        (
            every_shard[0],
            every_shard[1],
            every_shard[2],
            every_shard[3],
            every_shard[4],
            every_shard[5],
            every_shard[6],
            every_shard[7],
            every_shard[8],
            every_shard[9],
            every_shard[10],
            every_shard[11],
        ),
        "seq",
    )
    return (
        output,
        grad_tokens,
        s_first_gain,
        s_first_shift,
        s_joint_weight,
        s_joint_bias,
        s_output_weight,
        s_output_bias,
        s_second_gain,
        s_second_shift,
        s_expand_weight,
        s_expand_bias,
        s_reduce_weight,
        s_reduce_bias,
    )


def solution(mesh):
    return jax.shard_map(
        shards,
        mesh=mesh,
        in_specs=(
            P("dp", "seq", None),
            P("dp", "seq", None),
            P("dp", None),
            P("dp", None),
            P("dp"),
            P("dp"),
            P("dp", None),
            P("dp"),
            P("dp", None),
            P("dp"),
            P("dp"),
            P("dp"),
            P("dp", None),
            P("dp"),
            P("dp", None),
            P("dp"),
        ),
        out_specs=(
            P("dp", "seq", None),
            P("dp", "seq", None),
            P("dp"),
            P("dp"),
            P("dp", None),
            P("dp"),
            P("dp", None),
            P("dp"),
            P("dp"),
            P("dp"),
            P("dp", None),
            P("dp"),
            P("dp", None),
            P("dp"),
        ),
        check_vma=False,
    )
```

profile of v0, /device:TPU:0, one launch (start us, length us, event | category | flops | bytes accessed | tf_op | source)
XLA Modules:
  0.0 1413.0 jit_solution(12734546401829602809)
XLA Ops:
  18.1 27.3 %all-reduce.18 = (bf16[768]{0:T(1024)(128)(2,1)S(1)}, bf16[768]{0:T(1024)(128)(2,1)S(1)}, bf16[1536]{0:T(1024)(128)(2,1)S(1)}, bf16[768]{0:T(1024)(128)(2,1)S(1)...) all-reduce(bf16[768]{0:T(1024)(128)(2,1)S(1)} %dynamic-update-slice, ...), channel_id=1, replica_groups=mesh['dp'=8,'seq'=4] {'dp'}, use_global_device_ids=true, to_apply=%add.1 | all-reduce | flops 6144 | bytes 24576
  49.0 6.6 add_convert_fusion.1
  64.9 7.5 all-gather
  79.7 93.1 %all-gather.12.cloned.1.call-done = bf16[4,1024,768]{2,1,0:T(8,128)(2,1)} async-done(((bf16[4,256,768]{2,1,0:T(8,128)(2,1)}), bf16[4,1024,768]{2,1,0:T(8,128)(2,1)}) %all-gather.12.cloned.1.call-update) | async-done | bytes 6291472 | tf_op jit(solution)/shard_map/all_gather | solution.py:146
  172.8 8.7 copy.76
  181.5 106.4 %all-gather.10.cloned.1.call-done = bf16[4,1024,768]{2,1,0:T(8,128)(2,1)} async-done(((bf16[4,256,768]{2,1,0:T(8,128)(2,1)}), bf16[4,1024,768]{2,1,0:T(8,128)(2,1)}) %all-gather.10.cloned.1.call-update) | async-done | bytes 6291472 | tf_op jit(solution)/shard_map/all_gather | solution.py:147
  287.9 8.7 copy.74
  296.6 53.3 %while.26 = (s32[]{:T(128)}, bf16[4,256,12,64]{1,3,2,0:T(8,128)(2,1)}, f32[4,12,256,1]{2,1,3,0:T(8,128)S(1)}, bf16[4,1024,12,64]{1,3,2,0:T(8,128)(2,1)}, s32[4,2...) while((s32[]{:T(128)}, ...), condition=%wide.region_6.7_spmd, body=%wide.region_3.6_spmd.sunk | while | flops 840365056 | bytes 42861680 | solution.py:151
  296.9 3.7 fusion.135
  300.6 3.6 exponential_reduce_fusion.2
  304.3 5.6 fusion.136
  310.1 3.7 fusion.135
  313.8 3.6 exponential_reduce_fusion.2
  317.4 5.6 fusion.136
  323.3 3.7 fusion.135
  327.0 3.6 exponential_reduce_fusion.2
  330.6 5.6 fusion.136
  336.5 4.2 fusion.135
  340.6 3.6 exponential_reduce_fusion.2
  344.3 5.6 fusion.136
  354.0 3.5 fusion.96
  359.8 38.5 %multiply_convert_fusion.1 = (bf16[1024,3072]{1,0:T(8,128)(2,1)}, f32[1024,3072]{1,0:T(8,128)}, f32[1024,3072]{1,0:T(8,128)}) fusion(f32[3072]{0:T(1024)S(1)} %bitcast.248, bf16[768,3072]{1,0:T(8,128)(2,1)} %all-gather.16.cloned.1.call-done, f32[1024,768]{1,0:T(8,128)} %copy-done.2, f32[768]{0:T(1024)S(1)} %convert_element_type.152, ...), kind=kOutput, calls=%fused_computation.68 | convolution fusion | flops 5043388416 | bytes 39348224 | tf_op jit(solution)/shard_map/dot_general | solution.py:26
  398.4 17.4 %convert_reduce_fusion = (f32[3072]{0:T(1024)}, bf16[1024,3072]{1,0:T(8,128)(2,1)}) fusion(f32[1024,3072]{1,0:T(8,128)} %get-tuple-element.297, bf16[1024,768]{1,0:T(8,128)(2,1)S(1)} %copy-done.14, bf16[3072,768]{1,0:T(8,128)(2,1)} %all-gather.18.cloned.1.call-done, f32[1024,3072]{1,0:T(8,128)} %get-tuple-element.319, f32[3072]{0:T(1024)S(1)} %bitcast.249), kind=kOutput, calls=%fused_computation.66 | convolution fusion | flops 4885312512 | bytes 37773312 | tf_op jit(solution)/shard_map/dot_general | solution.py:36
  415.8 9.9 multiply_reduce_fusion.1
  439.8 120.7 %while.27 = (s32[]{:T(128)}, bf16[4,256,12,64]{1,3,2,0:T(8,128)(2,1)}, f32[4,1024,12,64]{1,3,2,0:T(8,128)}, f32[4,1024,12,64]{1,3,2,0:T(8,128)}, bf16[4,1024,12,...) while((s32[]{:T(128)}, ...), condition=%wide.region_14.15_spmd, body=%wide.region_12.14_spmd.sunk | while | flops 2061693952 | bytes 121487552 | solution.py:197
  440.1 3.2 fusion.145
  443.3 4.7 bitcast_dynamic-update-slice_fusion.8
  448.0 8.8 multiply_reduce_fusion.5
  456.8 6.8 multiply_convert_fusion.5
  463.7 3.4 fusion.146
  470.2 3.2 fusion.145
  473.5 4.6 bitcast_dynamic-update-slice_fusion.8
  478.1 8.8 multiply_reduce_fusion.5
  486.9 6.8 multiply_convert_fusion.5
  493.8 3.4 fusion.146
  500.3 3.2 fusion.145
  503.6 4.7 bitcast_dynamic-update-slice_fusion.8
  508.2 8.8 multiply_reduce_fusion.5
  517.1 6.8 multiply_convert_fusion.5
  523.9 3.4 fusion.146
  527.3 2.9 bitcast_dynamic-update-slice_fusion.7
  530.5 3.2 fusion.145
  533.8 4.7 bitcast_dynamic-update-slice_fusion.8
  538.5 8.8 multiply_reduce_fusion.5
  547.3 6.8 multiply_convert_fusion.5
  554.1 3.4 fusion.146
  561.3 4.8 fusion.97
  566.3 11.0 fusion.87
  577.4 9.9 fusion.98
  591.5 178.9 %reduce-scatter.9.cloned.1.call-done = f32[4,256,768]{1,2,0:T(8,128)} async-done(((f32[4,1024,768]{1,2,0:T(8,128)}), f32[4,256,768]{1,2,0:T(8,128)}) %reduce-scatter.9.cloned.1.call-update) | async-done | bytes 3145744 | tf_op jit(solution)/shard_map/reduce_scatter | solution.py:207
  770.5 3.2 convert.14
  778.8 207.0 %reduce-scatter.7.cloned.1.call-done = f32[4,256,768]{1,2,0:T(8,128)} async-done(((f32[4,1024,768]{1,2,0:T(8,128)}), f32[4,256,768]{1,2,0:T(8,128)}) %reduce-scatter.7.cloned.1.call-update) | async-done | bytes 3145744 | tf_op jit(solution)/shard_map/reduce_scatter | solution.py:201
  985.8 3.2 convert.13
  994.1 9.8 fusion.84
  1007.8 24.8 %reduce-scatter.13.cloned.1.call-done = f32[96,768]{1,0:T(8,128)} async-done(((f32[768,768]{1,0:T(8,128)}), f32[96,768]{1,0:T(8,128)}) %reduce-scatter.13.cloned.1.call-update) | async-done | bytes 294928 | tf_op jit(solution)/shard_map/reduce_scatter | solution.py:236
  1032.5 80.2 %reduce-scatter.15.cloned.1.call-done = f32[96,3072]{1,0:T(8,128)} async-done(((f32[768,3072]{1,0:T(8,128)}), f32[96,3072]{1,0:T(8,128)}) %reduce-scatter.15.cloned.1.call-update) | async-done | bytes 1179664 | tf_op jit(solution)/shard_map/reduce_scatter | solution.py:240
  1112.7 80.4 %reduce-scatter.17.cloned.1.call-done = f32[384,768]{1,0:T(8,128)} async-done(((f32[3072,768]{1,0:T(8,128)}), f32[384,768]{1,0:T(8,128)}) %reduce-scatter.17.cloned.1.call-update) | async-done | bytes 1179664 | tf_op jit(solution)/shard_map/reduce_scatter | solution.py:242
  1193.1 68.9 %reduce-scatter.11.cloned.1.call-done = f32[96,2304]{1,0:T(8,128)} async-done(((f32[768,2304]{1,0:T(8,128)}), f32[96,2304]{1,0:T(8,128)}) %reduce-scatter.11.cloned.1.call-update) | async-done | bytes 884752 | tf_op jit(solution)/shard_map/reduce_scatter | solution.py:234
  1262.0 9.7 add_convert_fusion.2
  1273.2 4.5 fusion.89
  1281.0 25.2 %all-reduce.15 = (f32[768]{0:T(1024)S(1)}, f32[768]{0:T(1024)S(1)}, f32[1536]{0:T(1024)S(1)}, f32[768]{0:T(1024)S(1)}, f32[768]{0:T(1024)S(1)}, /*index=5*/f32[7...) all-reduce(f32[768]{0:T(1024)S(1)} %get-tuple-element.218, ...), channel_id=4, replica_groups=mesh['dp'=8,'seq'=4] {'dp'}, use_global_device_ids=true, to_apply=%region_20.21.clone | all-reduce | flops 9216 | bytes 73728
  1306.8 13.4 all-reduce.16
  1320.2 4.7 add_add_fusion.2
  1324.9 74.0 %all-reduce.21.cloned.1.call-done = (f32[96,2304]{1,0:T(8,128)}, f32[96,768]{1,0:T(8,128)}, f32[96,3072]{1,0:T(8,128)}, f32[384,768]{1,0:T(8,128)}) async-done(((f32[96,2304]{1,0:T(8,128)}, f32[96,768]{1,0:T(8,128)}, f32[96,3072]{1,0:T(8,128)}, f32[384,768]{1,0:T(8,128)}), (f32[96,2304]{1,0:T(8,128)}, f32[96,768]{1,0:T(8,128)}, f32[96,3072]{1,0:T(8,128)}, ...) | async-done | bytes 3538960 | tf_op jit(solution)/shard_map/psum | solution.py:258
  (281 shorter events, 90.1 us)
Async XLA Ops:
  7.2 39.9 %copy-start = (bf16[4,256,768]{2,1,0:T(8,128)(2,1)S(1)}, bf16[4,256,768]{2,1,0:T(8,128)(2,1)}, u32[]{:S(2)}) copy-start(bf16[4,256,768]{2,1,0:T(8,128)(2,1)} %param.20) | copy-start | bytes 4718596
  7.2 41.8 %all-gather.8.cloned.1.call-start = ((), (), s32[]{:S(2)}) async-start(), calls=%async_computation.6 | async-start | bytes 3981312 | tf_op jit(solution)/shard_map/all_gather | solution.py:125
  9.3 163.4 %all-gather.12.cloned.1.call-start = ((), (), s32[]{:S(2)}) async-start(), calls=%async_computation.8 | async-start | bytes 7864320 | tf_op jit(solution)/shard_map/all_gather | solution.py:146
  45.4 2.9 copy-start.27
  48.9 6.6 copy-start.13
  55.6 3.1 copy-start.21
  57.9 6.1 copy-start.47
  57.9 6.1 copy-start.48
  57.9 6.2 copy-start.24
  57.9 230.0 %all-gather.10.cloned.1.call-start = ((), (), s32[]{:S(2)}) async-start(), calls=%async_computation.7 | async-start | bytes 7864320 | tf_op jit(solution)/shard_map/all_gather | solution.py:147
  58.0 14.5 %copy-start.6 = (bf16[4,256,768]{2,1,0:T(8,128)(2,1)S(1)}, bf16[4,256,768]{2,1,0:T(8,128)(2,1)}, u32[]{:S(2)}) copy-start(bf16[4,256,768]{2,1,0:T(8,128)(2,1)} %param.21) | copy-start | bytes 4718596
  58.7 295.4 %all-gather.14.cloned.1.call-start = ((), (), s32[]{:S(2)}) async-start(), calls=%async_computation.9 | async-start | bytes 1327104 | tf_op jit(solution)/shard_map/all_gather | solution.py:127
  59.4 300.4 %all-gather.16.cloned.1.call-start = ((), (), s32[]{:S(2)}) async-start(), calls=%async_computation.10 | async-start | bytes 5308416 | tf_op jit(solution)/shard_map/all_gather | solution.py:160
  61.6 336.7 %all-gather.18.cloned.1.call-start = ((), (), s32[]{:S(2)}) async-start(), calls=%async_computation.11 | async-start | bytes 5308416 | tf_op jit(solution)/shard_map/all_gather | solution.py:162
  63.9 706.6 %reduce-scatter.9.cloned.1.call-start = ((), (), s32[]{:S(2)}) async-start(), calls=%async_computation.13 | async-start | bytes 15728640 | tf_op jit(solution)/shard_map/reduce_scatter | solution.py:207
  64.1 361.7 %copy-start.25 = (f32[768]{0:T(1024)}, f32[768]{0:T(1024)S(1)}, u32[]{:S(2)}) copy-start(f32[768]{0:T(1024)S(1)} %convert_element_type.150) | copy-start | bytes 9220
  64.1 295.7 %copy-start.33 = (f32[768]{0:T(1024)}, f32[768]{0:T(1024)S(1)}, u32[]{:S(2)}) copy-start(f32[768]{0:T(1024)S(1)} %convert_element_type.152) | copy-start | bytes 9220
  64.9 13.2 copy-start.40
  357.6 1.7 copy-start.2
  357.6 68.2 %copy-start.19 = (f32[1024]{0:T(1024)}, f32[1024]{0:T(1024)S(1)}, u32[]{:S(2)}) copy-start(f32[1024]{0:T(1024)S(1)} %broadcast_multiply_fusion) | copy-start | bytes 12292
  359.8 66.0 %copy-start.22 = (f32[1024]{0:T(1024)}, f32[1024]{0:T(1024)S(1)}, u32[]{:S(2)}) copy-start(f32[1024]{0:T(1024)S(1)} %fusion.81) | copy-start | bytes 12292
  359.8 38.5 %copy-start.14 = (bf16[1024,768]{1,0:T(8,128)(2,1)S(1)}, bf16[1024,768]{1,0:T(8,128)(2,1)}, u32[]{:S(2)}) copy-start(bf16[1024,768]{1,0:T(8,128)(2,1)} %fusion.69) | copy-start | bytes 4718596
  398.4 17.5 %copy-start.3 = (f32[1024,768]{1,0:T(8,128)S(1)}, f32[1024,768]{1,0:T(8,128)}, u32[]{:S(2)}) copy-start(f32[1024,768]{1,0:T(8,128)} %copy-done.2) | copy-start | bytes 9437188
  425.8 3.1 copy-start.7
  427.3 1.6 copy-start.5
  427.3 4.0 copy-start.50
  427.3 6.6 copy-start.37
  456.8 6.8 copy-start.15
  467.1 2.9 copy-start.16
  486.9 6.8 copy-start.15
  497.2 2.9 copy-start.16
  517.1 6.8 copy-start.15
  527.3 2.9 copy-start.16
  547.3 6.8 copy-start.15
  557.6 2.9 copy-start.16
  560.5 425.3 %reduce-scatter.7.cloned.1.call-start = ((), (), s32[]{:S(2)}) async-start(), calls=%async_computation.12 | async-start | bytes 15728640 | tf_op jit(solution)/shard_map/reduce_scatter | solution.py:201
  561.2 5.0 copy-start.4
  561.3 5.0 copy-start.20
  561.3 5.0 copy-start.23
  561.3 5.0 copy-start.26
  561.3 5.0 copy-start.34
  561.3 471.2 %reduce-scatter.13.cloned.1.call-start = ((), (), s32[]{:S(2)}) async-start(), calls=%async_computation.15 | async-start | bytes 2654208 | tf_op jit(solution)/shard_map/reduce_scatter | solution.py:236
  566.2 546.5 %reduce-scatter.15.cloned.1.call-start = ((), (), s32[]{:S(2)}) async-start(), calls=%async_computation.16 | async-start | bytes 10616832 | tf_op jit(solution)/shard_map/reduce_scatter | solution.py:240
  577.3 615.7 %reduce-scatter.17.cloned.1.call-start = ((), (), s32[]{:S(2)}) async-start(), calls=%async_computation.17 | async-start | bytes 10616832 | tf_op jit(solution)/shard_map/reduce_scatter | solution.py:242
  587.3 674.7 %reduce-scatter.11.cloned.1.call-start = ((), (), s32[]{:S(2)}) async-start(), calls=%async_computation.14 | async-start | bytes 7962624 | tf_op jit(solution)/shard_map/reduce_scatter | solution.py:234
  1003.9 2.0 copy-start.46
  1003.9 2.0 copy-start.39
  1003.9 258.1 %copy-start.41 = (f32[1,2,4,128]{3,1,2,0:T(2,128)S(1)}, f32[1,2,4,128]{3,1,2,0:T(2,128)}, u32[]{:S(2)}) copy-start(f32[1,2,4,128]{3,1,2,0:T(2,128)} %copy-done.40) | copy-start | bytes 12292
  1004.0 395.0 %all-reduce.21.cloned.1.call-start = ((), (), s32[]{:S(2)}) async-start(), calls=%async_computation.18 | async-start | bytes 7077888 | tf_op jit(solution)/shard_map/psum | solution.py:258
  1262.0 9.8 copy-start.10
  1262.0 9.8 copy-start.11
  1262.0 9.7 copy-start.12
  1262.0 10.6 copy-start.49
  1271.8 1.4 copy-start.1
  1273.2 4.6 copy-start.36
  1273.2 6.2 copy-start.32
  1277.7 1.7 copy-start.9
  1277.7 3.3 copy-start.42
  1277.7 3.3 copy-start.43
  1277.8 3.3 copy-start.44
  1277.8 3.3 copy-start.45
  1277.8 42.5 %copy-start.8 = (bf16[4,256,768]{2,1,0:T(8,128)(2,1)S(1)}, bf16[4,256,768]{2,1,0:T(8,128)(2,1)}, u32[]{:S(2)}) copy-start(bf16[4,256,768]{2,1,0:T(8,128)(2,1)} %param.21) | copy-start | bytes 4718596
  1277.8 42.5 %copy-start.38 = (f32[1024]{0:T(1024)S(1)}, f32[1024]{0:T(1024)}, u32[]{:S(2)}) copy-start(f32[1024]{0:T(1024)} %copy-done.37) | copy-start | bytes 12292
  1398.9 6.3 copy-start.18
  (6 other events, 6.3 us)
Sparse Core Ops, SparseCore 0:
  10.5 36.7 all-gather.7
  58.0 114.7 all-gather.11
  174.4 113.5 all-gather.9
  290.2 22.0 all-gather.13
  314.7 38.8 all-gather.15
  355.9 38.7 all-gather.17
  560.6 209.7 reduce-scatter.8
  772.8 212.9 reduce-scatter.6
  989.1 43.3 reduce-scatter.12
  1035.9 76.7 reduce-scatter.14
  1116.2 76.8 reduce-scatter.16
  1196.4 65.4 reduce-scatter.10
  1264.6 134.2 all-reduce.20
where the time goes:
time: 1420 us; the launch traced here: 1410 us
  waiting for transfers between devices  915 us (64%)
  matrix products  258 us (18%)
  other arithmetic  78.9 us (6%)
  blocking collectives  73.4 us (5%)
  local copies, waits for them, and re-layouts  68.1 us (5%)
  between operations  18.2 us (1%)
    reduce_scatter x1, waiting for transfers between devices, shards(): lax.psum_scatter(grad_key_rows.reshape(row_count, row_len, features), 'se...  207 us
    reduce_scatter x1, waiting for transfers between devices, shards(): lax.psum_scatter(grad_value_rows.reshape(row_count, row_len, features), '...  179 us
    all_gather x1, waiting for transfers between devices, shards(): lax.all_gather(value_local, 'seq', axis=1, tiled=True)  106 us
    all_gather x1, waiting for transfers between devices, shards(): lax.all_gather(key_local, 'seq', axis=1, tiled=True)  93.1 us
    reduce_scatter x1, waiting for transfers between devices, shards(): lax.psum_scatter(g_reduce_weight, 'dp', scatter_dimension=0, tiled=True)  80.4 us
    reduce_scatter x1, waiting for transfers between devices, shards(): lax.psum_scatter(g_expand_weight, 'dp', scatter_dimension=0, tiled=True)  80.2 us
    psum x1, waiting for transfers between devices, shards(): lax.psum((every_shard[0], every_shard[1], every_shard[2], every_shard[3],...  74 us
    reduce_scatter x1, waiting for transfers between devices, shards(): lax.psum_scatter(g_joint_weight, 'dp', scatter_dimension=0, tiled=True)  68.9 us
  transfers between devices with their start and end apart: 13, of which 9 were waited for; matrix products, arithmetic and copies ran while one was open for 16% of the time, Pallas kernels for 0%

commit v1 on v0

v1 whole, which is shorter than its diff:
```python
import functools

import jax
import jax.numpy as jnp
from jax import lax
from jax.experimental import pallas as pl
from jax.experimental.pallas import tpu as pltpu
from jax.sharding import PartitionSpec as P

HEAD = 64
PAIR = 2 * HEAD
VIRTUAL = 8
keep_ratio_inverse = 1.0 / 0.9
norm_epsilon = 1e-06
F32 = jnp.float32
BF16 = jnp.bfloat16


def dot_nn(left, right):
    return lax.dot_general(left, right, (((1,), (0,)), ((), ())), preferred_element_type=F32)


def dot_nt(left, right):
    return lax.dot_general(left, right, (((1,), (1,)), ((), ())), preferred_element_type=F32)


def dot_tn(left, right):
    return lax.dot_general(left, right, (((0,), (0,)), ((), ())), preferred_element_type=F32)


def whole(shape):
    return pl.BlockSpec(shape, lambda *_: (0,) * len(shape))


SMEM = pl.BlockSpec(memory_space=pltpu.SMEM)
ANY = pl.BlockSpec(memory_space=pl.ANY)


def branch_scale(segment_column, flags_ref, first, images):
    scale = jnp.zeros(segment_column.shape, F32)
    for image in range(images):
        flag = flags_ref[first + image].astype(F32) * keep_ratio_inverse
        scale = jnp.where(segment_column == image, flag, scale)
    return scale


def norm_parts(inputs):
    centre = inputs - jnp.mean(inputs, axis=-1, keepdims=True)
    spread = jnp.mean(centre * centre, axis=-1, keepdims=True)
    inverse = lax.rsqrt(spread + norm_epsilon)
    return centre * inverse, inverse


def norm_backward(normal, inverse, grads, gain):
    scaled = grads * gain
    mean_scaled = jnp.mean(scaled, axis=-1, keepdims=True)
    mean_product = jnp.mean(scaled * normal, axis=-1, keepdims=True)
    return (scaled - mean_scaled - normal * mean_product) * inverse


def accumulate(step, ref, value):
    @pl.when(step == 0)
    def _():
        ref[...] = value

    @pl.when(step > 0)
    def _():
        ref[...] += value


def joint_kernel(rows, place_ref, x_ref, gain_ref, shift_ref, bias_ref, *refs):
    pieces = refs[:VIRTUAL]
    proj_ref, normed_t_ref, weight_ref, sems = refs[VIRTUAL:]

    @pl.when(pl.program_id(0) == 0)
    def _():
        copies = []
        for k in range(VIRTUAL):
            start = pl.multiple_of((place_ref[0] ^ k) * rows, 16)
            copies.append(
                pltpu.make_async_copy(
                    pieces[k].at[pl.ds(0, rows)], weight_ref.at[pl.ds(start, rows)], sems.at[k]
                )
            )
        for copy in copies:
            copy.start()
        for copy in copies:
            copy.wait()

    normal, _ = norm_parts(x_ref[...].astype(F32))
    normed = (normal * gain_ref[...] + shift_ref[...]).astype(BF16)
    normed_t_ref[...] = normed.T
    proj_ref[...] = (dot_nn(normed, weight_ref[...]) + bias_ref[...]).astype(BF16)


def joint_forward(place, x, gain, shift, bias, pieces, rows, tile=256):
    tokens, features = x.shape
    width = bias.shape[1]
    return pl.pallas_call(
        functools.partial(joint_kernel, rows),
        grid=(tokens // tile,),
        in_specs=[
            SMEM,
            pl.BlockSpec((tile, features), lambda t: (t, 0)),
            whole((1, features)),
            whole((1, features)),
            whole((1, width)),
        ]
        + [ANY] * VIRTUAL,
        out_specs=[
            pl.BlockSpec((tile, width), lambda t: (t, 0)),
            pl.BlockSpec((features, tile), lambda t: (0, t)),
            whole((features, width)),
        ],
        out_shape=[
            jax.ShapeDtypeStruct((tokens, width), BF16),
            jax.ShapeDtypeStruct((features, tokens), BF16),
            jax.ShapeDtypeStruct((features, width), BF16),
        ],
        scratch_shapes=[pltpu.SemaphoreType.DMA((VIRTUAL,))],
        compiler_params=pltpu.CompilerParams(vmem_limit_bytes=48 << 20),
        cost_estimate=pl.CostEstimate(
            flops=2 * tokens * features * width, bytes_accessed=14 << 20, transcendentals=0
        ),
        name="joint_forward",
    )(place, x, gain, shift, bias, *pieces)


def attention_forward_kernel(q_ref, k_ref, v_ref, segq_ref, segk_ref, mixed_ref, total_ref):
    queries = q_ref[...] * jnp.asarray(0.125, BF16)
    keys = k_ref[...]
    values_t = v_ref[...].T
    allowed = segk_ref[...] == segq_ref[...]
    lane = lax.broadcasted_iota(jnp.int32, queries.shape, 1)
    mixed, totals = [], []
    for h in range(2):
        mine = jnp.where((lane // HEAD) == h, queries, jnp.zeros_like(queries))
        scores = jnp.where(allowed, dot_nt(keys, mine), -1e30)
        top = jnp.max(scores, axis=0, keepdims=True)
        weights = jnp.exp(scores - top)
        total = jnp.sum(weights, axis=0, keepdims=True)
        probs = (weights * (1.0 / total)).astype(BF16)
        mixed.append(dot_nn(values_t[h * HEAD : (h + 1) * HEAD], probs))
        totals.append(top + jnp.log(total))
    mixed_ref[...] = jnp.concatenate(mixed, axis=0).T.astype(BF16)
    totals.append(jnp.zeros((6,) + totals[0].shape[1:], F32))
    total_ref[0] = jnp.concatenate(totals, axis=0)


def attention_forward(proj, seg_row, seg_column, tile=256):
    tokens, width = proj.shape
    features = width // 3
    pairs = features // PAIR
    return pl.pallas_call(
        attention_forward_kernel,
        grid=(pairs, tokens // tile),
        in_specs=[
            pl.BlockSpec((tile, PAIR), lambda h, i: (i, h)),
            pl.BlockSpec((tokens, PAIR), lambda h, i: (0, pairs + h)),
            pl.BlockSpec((tokens, PAIR), lambda h, i: (0, 2 * pairs + h)),
            pl.BlockSpec((1, tile), lambda h, i: (0, i)),
            whole((tokens, 1)),
        ],
        out_specs=[
            pl.BlockSpec((tile, PAIR), lambda h, i: (i, h)),
            pl.BlockSpec((1, 8, tile), lambda h, i: (h, 0, i)),
        ],
        out_shape=[
            jax.ShapeDtypeStruct((tokens, features), BF16),
            jax.ShapeDtypeStruct((pairs, 8, tokens), F32),
        ],
        compiler_params=pltpu.CompilerParams(vmem_limit_bytes=48 << 20),
        cost_estimate=pl.CostEstimate(
            flops=16 * tokens * tokens * features,
            bytes_accessed=8 << 20,
            transcendentals=tokens * tokens * features // HEAD,
        ),
        name="attention_forward",
    )(proj, proj, proj, seg_row, seg_column)


def attention_backward_kernel(
    q_tiles, q_ref, k_ref, v_ref, g_ref, segq_ref, segk_ref, total_ref, dq_ref, dk_ref, dv_ref, dk_sum, dv_sum
):
    step = pl.program_id(1)
    queries = q_ref[...] * jnp.asarray(0.125, BF16)
    keys, values, grads = k_ref[...], v_ref[...], g_ref[...]
    keys_t = keys.T
    allowed = segk_ref[...] == segq_ref[...]
    lane = lax.broadcasted_iota(jnp.int32, queries.shape, 1)
    grad_q, grad_k, grad_v = [], 0.0, 0.0
    for h in range(2):
        mine = (lane // HEAD) == h
        query = jnp.where(mine, queries, jnp.zeros_like(queries))
        grad = jnp.where(mine, grads, jnp.zeros_like(grads))
        scores = jnp.where(allowed, dot_nt(keys, query), -1e30)
        probs = jnp.exp(scores - total_ref[0, h : h + 1, :])
        grad_probs = dot_nt(values, grad)
        centre = jnp.sum(probs * grad_probs, axis=0, keepdims=True)
        grad_scores = (probs * (grad_probs - centre)).astype(BF16)
        grad_v += dot_nn(probs.astype(BF16), grad)
        grad_k += dot_nn(grad_scores, query)
        grad_q.append(dot_nn(keys_t[h * HEAD : (h + 1) * HEAD], grad_scores))
    dq_ref[...] = (jnp.concatenate(grad_q, axis=0).T * 0.125).astype(BF16)
    accumulate(step, dk_sum, grad_k)
    accumulate(step, dv_sum, grad_v)

    @pl.when(step == q_tiles - 1)
    def _():
        dk_ref[...] = dk_sum[...].astype(BF16)
        dv_ref[...] = dv_sum[...].astype(BF16)


def attention_backward(proj, grad_mixed, seg_row, seg_column, totals, tile=256):
    tokens, width = proj.shape
    features = width // 3
    pairs = features // PAIR
    q_tiles = tokens // tile
    return pl.pallas_call(
        functools.partial(attention_backward_kernel, q_tiles),
        grid=(pairs, q_tiles),
        in_specs=[
            pl.BlockSpec((tile, PAIR), lambda h, i: (i, h)),
            pl.BlockSpec((tokens, PAIR), lambda h, i: (0, pairs + h)),
            pl.BlockSpec((tokens, PAIR), lambda h, i: (0, 2 * pairs + h)),
            pl.BlockSpec((tile, PAIR), lambda h, i: (i, h)),
            pl.BlockSpec((1, tile), lambda h, i: (0, i)),
            whole((tokens, 1)),
            pl.BlockSpec((1, 8, tile), lambda h, i: (h, 0, i)),
        ],
        out_specs=[
            pl.BlockSpec((tile, PAIR), lambda h, i: (i, h)),
            pl.BlockSpec((tokens, PAIR), lambda h, i: (0, h)),
            pl.BlockSpec((tokens, PAIR), lambda h, i: (0, h)),
        ],
        out_shape=[jax.ShapeDtypeStruct((tokens, features), BF16)] * 3,
        scratch_shapes=[pltpu.VMEM((tokens, PAIR), F32)] * 2,
        compiler_params=pltpu.CompilerParams(vmem_limit_bytes=56 << 20),
        cost_estimate=pl.CostEstimate(
            flops=24 * tokens * tokens * features,
            bytes_accessed=14 << 20,
            transcendentals=tokens * tokens * features // HEAD,
        ),
        name="attention_backward",
    )(proj, proj, proj, grad_mixed, seg_row, seg_column, totals)


def middle_kernel(rows, images, place_ref, flags_ref, mixed_ref, x_ref, cot_ref, seg_ref, bias_ref, gain_ref, shift_ref, *refs):
    pieces = refs[:VIRTUAL]
    middle_ref, normed_ref, normed_t_ref, grad_ref, weight_ref, sems = refs[VIRTUAL:]
    features = x_ref.shape[1]

    @pl.when(pl.program_id(0) == 0)
    def _():
        copies = []
        for k in range(VIRTUAL):
            start = pl.multiple_of((place_ref[0] ^ k) * rows, 16)
            copies.append(
                pltpu.make_async_copy(
                    pieces[k].at[:, pl.ds(0, features)],
                    weight_ref.at[pl.ds(start, rows)],
                    sems.at[k],
                )
            )
        for copy in copies:
            copy.start()
        for copy in copies:
            copy.wait()

    branch = dot_nn(mixed_ref[...], weight_ref[...]) + bias_ref[...]
    segment = seg_ref[...]
    middle = x_ref[...].astype(F32) + branch_scale(segment, flags_ref, 0, images) * branch
    middle_ref[...] = middle
    normal, _ = norm_parts(middle)
    normed = (normal * gain_ref[...] + shift_ref[...]).astype(BF16)
    normed_ref[...] = normed
    normed_t_ref[...] = normed.T
    mlp_scale = branch_scale(segment, flags_ref, images, images)
    grad_ref[...] = (mlp_scale * cot_ref[...].astype(F32)).astype(BF16)


def middle_forward(place, flags, mixed, x, cot, seg_column, bias, gain, shift, pieces, rows, tile=256):
    tokens, features = x.shape
    images = flags.shape[0] // 2
    row_block = pl.BlockSpec((tile, features), lambda t: (t, 0))
    return pl.pallas_call(
        functools.partial(middle_kernel, rows, images),
        grid=(tokens // tile,),
        in_specs=[SMEM, SMEM, row_block, row_block, row_block, pl.BlockSpec((tile, 1), lambda t: (t, 0))]
        + [whole((1, features))] * 3
        + [ANY] * VIRTUAL,
        out_specs=[
            row_block,
            row_block,
            pl.BlockSpec((features, tile), lambda t: (0, t)),
            row_block,
            whole((features, features)),
        ],
        out_shape=[
            jax.ShapeDtypeStruct((tokens, features), F32),
            jax.ShapeDtypeStruct((tokens, features), BF16),
            jax.ShapeDtypeStruct((features, tokens), BF16),
            jax.ShapeDtypeStruct((tokens, features), BF16),
            jax.ShapeDtypeStruct((features, features), BF16),
        ],
        scratch_shapes=[pltpu.SemaphoreType.DMA((VIRTUAL,))],
        compiler_params=pltpu.CompilerParams(vmem_limit_bytes=48 << 20),
        cost_estimate=pl.CostEstimate(
            flops=2 * tokens * features * features, bytes_accessed=16 << 20, transcendentals=0
        ),
        name="middle_forward",
    )(place, flags, mixed, x, cot, seg_column, bias, gain, shift, *pieces)


def split_shards(rows, place, source_ref, keep_ref, send_ref):
    for pair in range(VIRTUAL // 2):
        slot = pair ^ (place >> 1)
        stay = pl.multiple_of((2 * pair + (place & 1)) * rows, 16)
        leave = pl.multiple_of((2 * pair + 1 - (place & 1)) * rows, 16)
        keep_ref[slot] = source_ref[pl.ds(stay, rows), :]
        send_ref[slot] = source_ref[pl.ds(leave, rows), :]


root_half = 0.7071067811865476
root_two_pi_inverse = 0.3989422804014327


def mlp_kernel(rows, tiles, block, place_ref, normed_ref, normed_t_ref, g_ref, bias_ref, *refs):
    pieces = refs[:VIRTUAL]
    (out_ref, gn_ref, keep1_ref, send1_ref, keep2_ref, send2_ref, db_ref) = refs[VIRTUAL : VIRTUAL + 7]
    w1_s, w2_s, act_s, gp_s, dw_s, sems = refs[VIRTUAL + 7 :]
    f = pl.program_id(0)
    place = place_ref[0]
    tokens, features = normed_ref.shape
    hidden = w1_s.shape[1]
    parts = hidden // features

    @pl.when(f == 0)
    def _():
        copies = []
        for k in range(VIRTUAL):
            start = pl.multiple_of((place ^ k) * rows, 16)
            copies.append(
                pltpu.make_async_copy(
                    pieces[k].at[:, pl.ds(features, hidden)], w1_s.at[pl.ds(start, rows)], sems.at[0, k]
                )
            )
            for part in range(parts):
                start = pl.multiple_of(((place ^ k) * parts + part) * rows, 16)
                copies.append(
                    pltpu.make_async_copy(
                        pieces[k].at[:, pl.ds(features + hidden + part * features, features)],
                        w2_s.at[pl.ds(start, rows)],
                        sems.at[1 + part, k],
                    )
                )
        for copy in copies:
            copy.start()
        for copy in copies:
            copy.wait()

    first = pl.multiple_of(f * block, block)
    w1 = w1_s[:, pl.ds(first, block)]
    w2 = w2_s[pl.ds(first, block), :]
    bias = bias_ref[...]
    step = tokens // tiles
    db = jnp.zeros((1, block), F32)
    for t in range(tiles):
        part = slice(t * step, (t + 1) * step)
        pre = dot_nn(normed_ref[part, :], w1) + bias
        cdf = 0.5 * (1.0 + lax.erf(pre * root_half))
        act = (pre * cdf).astype(BF16)
        slope = cdf + pre * (jnp.exp(-0.5 * pre * pre) * root_two_pi_inverse)
        gp = (dot_nt(g_ref[part, :], w2) * slope).astype(BF16)
        db += jnp.sum(gp.astype(F32), axis=0, keepdims=True)
        act_s[part, :] = act
        gp_s[part, :] = gp
        out = dot_nn(act, w2)
        gn = dot_nt(gp, w1)

        @pl.when(f == 0)
        def _():
            out_ref[part, :] = out
            gn_ref[part, :] = gn

        @pl.when(f > 0)
        def _():
            out_ref[part, :] += out
            gn_ref[part, :] += gn

    db_ref[...] = db
    dw_s[...] = dot_nn(normed_t_ref[...], gp_s[...]).astype(BF16)
    split_shards(rows, place, dw_s, keep1_ref, send1_ref)
    dw_s[...] = dot_tn(act_s[...], g_ref[...]).astype(BF16)
    slot = f ^ (place >> 1)
    for part in range(parts):
        stay = pl.multiple_of(((place & 1) * parts + part) * rows, 16)
        leave = pl.multiple_of(((1 - (place & 1)) * parts + part) * rows, 16)
        columns = slice(part * features, (part + 1) * features)
        keep2_ref[slot, :, columns] = dw_s[pl.ds(stay, rows), :]
        send2_ref[slot, :, columns] = dw_s[pl.ds(leave, rows), :]


def mlp(place, normed, normed_t, grads, bias, pieces, rows, tiles=4):
    tokens, features = normed.shape
    hidden = bias.shape[1]
    parts = hidden // features
    block = 2 * hidden // VIRTUAL
    assert block == features
    half = VIRTUAL // 2
    columns = pl.BlockSpec((half, rows, block), lambda f: (0, 0, f))
    shards = jax.ShapeDtypeStruct((half, rows, hidden), BF16)
    return pl.pallas_call(
        functools.partial(mlp_kernel, rows, tiles, block),
        grid=(hidden // block,),
        in_specs=[
            SMEM,
            whole((tokens, features)),
            whole((features, tokens)),
            whole((tokens, features)),
            pl.BlockSpec((1, block), lambda f: (0, f)),
        ]
        + [ANY] * VIRTUAL,
        out_specs=[
            whole((tokens, features)),
            whole((tokens, features)),
            columns,
            columns,
            whole((half, rows, hidden)),
            whole((half, rows, hidden)),
            pl.BlockSpec((1, block), lambda f: (0, f)),
        ],
        out_shape=[jax.ShapeDtypeStruct((tokens, features), F32)] * 2
        + [shards] * 4
        + [jax.ShapeDtypeStruct((1, hidden), F32)],
        scratch_shapes=[
            pltpu.VMEM((features, hidden), BF16),
            pltpu.VMEM((hidden, features), BF16),
            pltpu.VMEM((tokens, block), BF16),
            pltpu.VMEM((tokens, block), BF16),
            pltpu.VMEM((features, block), BF16),
            pltpu.SemaphoreType.DMA((1 + parts, VIRTUAL)),
        ],
        compiler_params=pltpu.CompilerParams(vmem_limit_bytes=62 << 20),
        cost_estimate=pl.CostEstimate(
            flops=12 * tokens * features * hidden,
            bytes_accessed=30 << 20,
            transcendentals=2 * tokens * hidden,
        ),
        name="mlp",
    )(place, normed, normed_t, grads, bias, *pieces)


def output_backward_kernel(
    rows, images, steps, place_ref, flags_ref, middle_ref, gn_ref, branch_ref, cot_ref, mixed_ref, seg_ref,
    gain_ref, bias_ref, weight_ref, out_ref, gm_ref, gx_ref, keep_ref, send_ref, sums_ref, dw_sum, dw_s,
):
    step = pl.program_id(0)
    segment = seg_ref[...]
    attn_scale = branch_scale(segment, flags_ref, 0, images)
    mlp_scale = branch_scale(segment, flags_ref, images, images)
    middle = middle_ref[...]
    cot = cot_ref[...].astype(F32)
    out_ref[...] = (middle + mlp_scale * (branch_ref[...] + bias_ref[...])).astype(BF16)
    grad_b = (mlp_scale * cot).astype(BF16)
    gn = gn_ref[...]
    normal, inverse = norm_parts(middle)
    grad_middle = cot + norm_backward(normal, inverse, gn, gain_ref[...])
    gm_ref[...] = grad_middle
    grad_a = (attn_scale * grad_middle).astype(BF16)
    gx_ref[...] = dot_nt(grad_a, weight_ref[...]).astype(BF16)
    accumulate(step, dw_sum, dot_tn(mixed_ref[...], grad_a))
    total = lambda v: jnp.sum(v, axis=0, keepdims=True)
    sums = [total(gn * normal), total(gn), total(grad_a.astype(F32)), total(grad_b.astype(F32))]
    accumulate(step, sums_ref, jnp.concatenate(sums + [jnp.zeros((4,) + sums[0].shape[1:], F32)], axis=0))

    @pl.when(step == steps - 1)
    def _():
        dw_s[...] = dw_sum[...].astype(BF16)
        split_shards(rows, place_ref[0], dw_s, keep_ref, send_ref)


def output_backward(place, flags, middle, gn, branch, cot, mixed, seg_column, gain, bias, weight, rows, tile=256):
    tokens, features = middle.shape
    images = flags.shape[0] // 2
    half = VIRTUAL // 2
    steps = tokens // tile
    row_block = pl.BlockSpec((tile, features), lambda t: (t, 0))
    shards = jax.ShapeDtypeStruct((half, rows, features), BF16)
    return pl.pallas_call(
        functools.partial(output_backward_kernel, rows, images, steps),
        grid=(steps,),
        in_specs=[SMEM, SMEM]
        + [row_block] * 5
        + [pl.BlockSpec((tile, 1), lambda t: (t, 0)), whole((1, features)), whole((1, features)), whole((features, features))],
        out_specs=[row_block, row_block, row_block, whole((half, rows, features)), whole((half, rows, features)), whole((8, features))],
        out_shape=[
            jax.ShapeDtypeStruct((tokens, features), BF16),
            jax.ShapeDtypeStruct((tokens, features), F32),
            jax.ShapeDtypeStruct((tokens, features), BF16),
            shards,
            shards,
            jax.ShapeDtypeStruct((8, features), F32),
        ],
        scratch_shapes=[pltpu.VMEM((features, features), F32), pltpu.VMEM((features, features), BF16)],
        compiler_params=pltpu.CompilerParams(vmem_limit_bytes=56 << 20),
        cost_estimate=pl.CostEstimate(
            flops=4 * tokens * features * features, bytes_accessed=22 << 20, transcendentals=0
        ),
        name="output_backward",
    )(place, flags, middle, gn, branch, cot, mixed, seg_column, gain, bias, weight)


def joint_weight_kernel(rows, place_ref, normed_t_ref, dq_ref, dk_ref, dv_ref, keep_ref, send_ref, sums_ref, dw_s):
    step = pl.program_id(0)

    def block(ref):
        grads = ref[...]
        dw_s[...] = dot_nn(normed_t_ref[...], grads).astype(BF16)
        sums_ref[...] = jnp.sum(grads.astype(F32), axis=0, keepdims=True)

    for index, ref in enumerate((dq_ref, dk_ref, dv_ref)):
        pl.when(step == index)(functools.partial(block, ref))
    split_shards(rows, place_ref[0], dw_s, keep_ref, send_ref)


def joint_weight_grad(place, normed_t, dq, dk, dv, rows):
    features, tokens = normed_t.shape
    half = VIRTUAL // 2
    columns = pl.BlockSpec((half, rows, features), lambda c: (0, 0, c))
    shards = jax.ShapeDtypeStruct((half, rows, 3 * features), BF16)
    return pl.pallas_call(
        functools.partial(joint_weight_kernel, rows),
        grid=(3,),
        in_specs=[SMEM, whole((features, tokens))] + [whole((tokens, features))] * 3,
        out_specs=[columns, columns, pl.BlockSpec((1, features), lambda c: (0, c))],
        out_shape=[shards, shards, jax.ShapeDtypeStruct((1, 3 * features), F32)],
        scratch_shapes=[pltpu.VMEM((features, features), BF16)],
        compiler_params=pltpu.CompilerParams(vmem_limit_bytes=48 << 20),
        cost_estimate=pl.CostEstimate(
            flops=6 * tokens * features * features, bytes_accessed=10 << 20, transcendentals=0
        ),
        name="joint_weight_grad",
    )(place, normed_t, dq, dk, dv)


def joint_backward_kernel(dq_ref, dk_ref, dv_ref, weight_ref, x_ref, gm_ref, gain_ref, gt_ref, sums_ref):
    features = x_ref.shape[1]
    gn = dot_nt(dq_ref[...], weight_ref[:, :features])
    gn += dot_nt(dk_ref[...], weight_ref[:, features : 2 * features])
    gn += dot_nt(dv_ref[...], weight_ref[:, 2 * features :])
    normal, inverse = norm_parts(x_ref[...].astype(F32))
    gt_ref[...] = (gm_ref[...] + norm_backward(normal, inverse, gn, gain_ref[...])).astype(BF16)
    total = lambda v: jnp.sum(v, axis=0, keepdims=True)
    sums = [total(gn * normal), total(gn)]
    accumulate(
        pl.program_id(0), sums_ref, jnp.concatenate(sums + [jnp.zeros((6, features), F32)], axis=0)
    )


def joint_backward(dq, dk, dv, weight, x, gm, gain, tile=256):
    tokens, features = x.shape
    row_block = pl.BlockSpec((tile, features), lambda t: (t, 0))
    return pl.pallas_call(
        joint_backward_kernel,
        grid=(tokens // tile,),
        in_specs=[row_block] * 3 + [whole((features, 3 * features)), row_block, row_block, whole((1, features))],
        out_specs=[row_block, whole((8, features))],
        out_shape=[jax.ShapeDtypeStruct((tokens, features), BF16), jax.ShapeDtypeStruct((8, features), F32)],
        compiler_params=pltpu.CompilerParams(vmem_limit_bytes=48 << 20),
        cost_estimate=pl.CostEstimate(
            flops=6 * tokens * features * features, bytes_accessed=15 << 20, transcendentals=0
        ),
        name="joint_backward",
    )(dq, dk, dv, weight, x, gm, gain)


def after(value, *others):
    return lax.optimization_barrier((value,) + others)[0]


def dp_swap(value, bit):
    return lax.ppermute(value, "dp", [(i, i ^ bit) for i in range(VIRTUAL)])


def seq_exchange(value, parts):
    me = lax.axis_index("seq")

    def block(place):
        return lax.dynamic_index_in_dim(value, place % parts, 0, keepdims=False)

    order = sorted(range(1, parts), key=lambda k: abs(k - parts / 2))
    got = [
        (k, lax.ppermute(block(me + k), "seq", [(i, (i + k) % parts) for i in range(parts)]))
        for k in order
    ]
    out = lax.dynamic_update_index_in_dim(jnp.zeros_like(value), block(me), me, 0)
    for k, arrived in got:
        out = lax.dynamic_update_index_in_dim(out, arrived, (me - k) % parts, 0)
    return out


def gather_shards(own, first):
    far_x, far_y = dp_swap(own, 2), dp_swap(own, 4)
    corner = dp_swap(far_x, 4) if first == 2 else dp_swap(far_y, 2)
    mine = (own, far_x, far_y, corner)
    other = [dp_swap(piece, 1) for piece in mine]
    return [piece for both in zip(mine, other) for piece in both]


def add(left, right):
    return left.astype(F32) + right.astype(F32)


def scatter_rest(half, first):
    if first == 2:
        one = add(half[0::2], dp_swap(half[1::2], 2)).astype(BF16)
        return add(one[0], dp_swap(one[1], 4))
    one = add(half[:2], dp_swap(half[2:], 4)).astype(BF16)
    return add(one[0], dp_swap(one[1], 2))


def seq_sum(value, parts):
    rows = value.shape[0] // parts
    cut = value.astype(BF16).reshape(parts, rows, value.shape[1])
    arrived = seq_exchange(cut, parts)
    total = jnp.sum(arrived.astype(F32), axis=0).astype(BF16)
    me = lax.axis_index("seq")
    out = lax.dynamic_update_index_in_dim(jnp.zeros_like(cut), total, me, 0)
    for k in range(1, parts):
        got = lax.ppermute(total, "seq", [(i, (i + k) % parts) for i in range(parts)])
        out = lax.dynamic_update_index_in_dim(out, got, (me - k) % parts, 0)
    return out.astype(F32).reshape(value.shape)


def sum_everywhere(value, parts):
    for bit in (1, 2, 4):
        value = value + dp_swap(value, bit)
    if parts & (parts - 1):
        return lax.psum(value, "seq")
    bit = 1
    while bit < parts:
        value = value + lax.ppermute(value, "seq", [(i, i ^ bit) for i in range(parts)])
        bit *= 2
    return value


def pack_rows(matrix, rows):
    groups = matrix.shape[0] // rows
    return jnp.concatenate([matrix[g * rows : (g + 1) * rows] for g in range(groups)], axis=1)


def unpack_rows(matrix, features):
    groups = matrix.shape[1] // features
    return jnp.concatenate([matrix[:, g * features : (g + 1) * features] for g in range(groups)], axis=0)


def shards(
    ndp,
    nseq,
    tokens,
    cotangent,
    segments,
    keep_flags,
    first_gain,
    first_shift,
    joint_weight,
    joint_bias,
    output_weight,
    output_bias,
    second_gain,
    second_shift,
    expand_weight,
    expand_bias,
    reduce_weight,
    reduce_bias,
):
    row_count, shard_len, features = tokens.shape
    assert row_count == nseq
    row_len = segments.shape[1]
    hidden = expand_weight.shape[1]
    rows = features // VIRTUAL
    me_seq = lax.axis_index("seq")
    me_dp = lax.axis_index("dp")
    exact = ndp == VIRTUAL

    smalls = (first_gain, first_shift, joint_bias, output_bias, second_gain, second_shift, expand_bias, reduce_bias)
    widths = [s.shape[0] * ndp for s in smalls]

    x = seq_exchange(tokens, nseq).reshape(row_len, features)

    if exact:
        place = me_dp.astype(jnp.int32).reshape(1)
        row = jnp.concatenate([s.astype(BF16) for s in smalls])
        width = 3 * features
        row = jnp.pad(row, (0, width - row.shape[0])).reshape(1, width)
        piece = jnp.concatenate([joint_weight.astype(BF16), jnp.pad(row, ((0, 15), (0, 0)))], axis=0)
        joint_pieces = gather_shards(piece, 2)
        small_slots = jnp.stack([p[rows, : sum(w // ndp for w in widths)] for p in joint_pieces]).astype(F32)
        slot = lax.broadcasted_iota(jnp.int32, (VIRTUAL, VIRTUAL, 1), 1)
        home = lax.broadcasted_iota(jnp.int32, (VIRTUAL, VIRTUAL, 1), 0)
        ordered = jnp.sum(jnp.where(slot == (home ^ me_dp), small_slots[None], 0.0), axis=1)
        params, start = [], 0
        for w in widths:
            params.append(ordered[:, start : start + w // ndp].reshape(1, w))
            start += w // ndp
        piece = jnp.concatenate(
            [output_weight.astype(BF16), expand_weight.astype(BF16), pack_rows(reduce_weight.astype(BF16), rows)],
            axis=1,
        )
        piece = after(piece, joint_pieces[2], joint_pieces[4])
        rest_pieces = gather_shards(piece, 4)
    else:
        place = jnp.zeros((1,), jnp.int32)
        full = lambda w: lax.all_gather(w.astype(BF16), "dp", axis=0, tiled=True)
        params = [full(s).astype(F32).reshape(1, -1) for s in smalls]
        joint = full(joint_weight)
        out_w, up_w, down_w = full(output_weight), full(expand_weight), full(reduce_weight)
        joint_pieces = [joint[k * rows : (k + 1) * rows] for k in range(VIRTUAL)]
        group = hidden // VIRTUAL
        rest_pieces = [
            jnp.concatenate(
                [
                    out_w[k * rows : (k + 1) * rows],
                    up_w[k * rows : (k + 1) * rows],
                    pack_rows(down_w[k * group : (k + 1) * group], rows),
                ],
                axis=1,
            )
            for k in range(VIRTUAL)
        ]
    gain_a, shift_a, bias_qv, bias_out, gain_b, shift_b, bias_up, bias_down = params
    bias_joint = jnp.concatenate([bias_qv[:, :features], jnp.zeros((1, features), F32), bias_qv[:, features:]], axis=1)

    seg = lax.dynamic_index_in_dim(segments, me_seq, 0, keepdims=False)
    flags = lax.dynamic_index_in_dim(keep_flags, me_seq, 0, keepdims=False)
    seg_row, seg_column = seg.reshape(1, row_len), seg.reshape(row_len, 1)

    cot = seq_exchange(after(cotangent, x), nseq).reshape(row_len, features)

    proj, normed_a_t, weight_joint = joint_forward(place, x, gain_a, shift_a, bias_joint, joint_pieces, rows)
    mixed, totals = attention_forward(proj, seg_row, seg_column)
    middle, normed_b, normed_b_t, grad_b, weight_out = middle_forward(
        place, flags, mixed, x, cot, seg_column, bias_out, gain_b, shift_b, rest_pieces, rows
    )
    branch, gn, keep_up, send_up, keep_down, send_down, g_bias_up = mlp(
        place, normed_b, normed_b_t, grad_b, bias_up, rest_pieces, rows
    )
    output, grad_middle, grad_mixed, keep_out, send_out, sums_b = output_backward(
        place, flags, middle, gn, branch, cot, mixed, seg_column, gain_b, bias_down, weight_out, rows
    )
    dq, dk, dv = attention_backward(proj, grad_mixed, seg_row, seg_column, totals)
    keep_joint, send_joint, sums_joint = joint_weight_grad(place, normed_a_t, dq, dk, dv, rows)
    grad_in, sums_a = joint_backward(dq, dk, dv, weight_joint, x, grad_middle, gain_a)

    output = seq_exchange(output.reshape(nseq, shard_len, features), nseq)
    grad_tokens = seq_exchange(grad_in.reshape(nseq, shard_len, features), nseq).astype(F32)

    late = jnp.concatenate([sums_a[0], sums_a[1], sums_joint[0, :features], sums_joint[0, 2 * features :]])
    early = jnp.concatenate([sums_b[2], sums_b[0], sums_b[1], g_bias_up[0], sums_b[3]])
    if exact:
        early = sum_everywhere(early.reshape(-1, 128), nseq).reshape(-1)
        late = sum_everywhere(late.reshape(-1, 128), nseq).reshape(-1)
        half_up = add(keep_up, dp_swap(send_up, 1)).astype(BF16)
        half_down = add(keep_down, dp_swap(send_down, 1)).astype(BF16)
        half_out = add(keep_out, dp_swap(send_out, 1)).astype(BF16)
        first = jnp.concatenate(
            [scatter_rest(half_up, 2), scatter_rest(half_down, 4), scatter_rest(half_out, 2)], axis=1
        )
        first = seq_sum(first, nseq)
        g_up = first[:, :hidden]
        g_down = unpack_rows(first[:, hidden : 2 * hidden], features)
        g_out = first[:, 2 * hidden :]
        arrived = dp_swap(send_joint, 1)
        cut = 3 * features // 2
        half_a = add(keep_joint[:, :, :cut], arrived[:, :, :cut]).astype(BF16)
        half_b = add(keep_joint[:, :, cut:], arrived[:, :, cut:]).astype(BF16)
        g_joint = seq_sum(jnp.concatenate([scatter_rest(half_a, 2), scatter_rest(half_b, 4)], axis=1), nseq)
    else:
        early, late = lax.psum((early, late), ("dp", "seq"))

        def total(keep, send):
            return jnp.stack([keep, send], axis=1).reshape(features, keep.shape[2])

        def reduce(matrix):
            part = lax.psum_scatter(matrix.astype(F32), "dp", scatter_dimension=0, tiled=True)
            return lax.psum(part, "seq")

        g_up = reduce(total(keep_up, send_up))
        g_out = reduce(total(keep_out, send_out))
        g_joint = reduce(total(keep_joint, send_joint))
        down = jnp.stack([keep_down, send_down], axis=1).reshape(VIRTUAL, rows, hidden)
        g_down = reduce(jnp.concatenate([unpack_rows(down[k], features) for k in range(VIRTUAL)], axis=0))

    def mine(vector, start, size):
        piece = size // ndp
        return lax.dynamic_slice_in_dim(vector, start + me_dp * piece, piece, 0)

    g_first_gain = mine(late, 0, features)
    g_first_shift = mine(late, features, features)
    g_joint_bias = mine(late, 2 * features, 2 * features)
    g_output_bias = mine(early, 0, features)
    g_second_gain = mine(early, features, features)
    g_second_shift = mine(early, 2 * features, features)
    g_expand_bias = mine(early, 3 * features, hidden)
    g_reduce_bias = mine(early, 3 * features + hidden, features)
    return (
        output,
        grad_tokens,
        g_first_gain,
        g_first_shift,
        g_joint,
        g_joint_bias,
        g_out,
        g_output_bias,
        g_second_gain,
        g_second_shift,
        g_up,
        g_expand_bias,
        g_down,
        g_reduce_bias,
    )


def solution(mesh):
    vector, matrix = P("dp"), P("dp", None)
    token_spec = P("dp", "seq", None)
    params = (vector, vector, matrix, vector, matrix, vector, vector, vector, matrix, vector, matrix, vector)
    return jax.shard_map(
        functools.partial(shards, mesh.shape["dp"], mesh.shape["seq"]),
        mesh=mesh,
        in_specs=(token_spec, token_spec, matrix, matrix) + params,
        out_specs=(token_spec, token_spec) + params,
        check_vma=False,
    )
```

time: 1420 us -> 552 us (0.39)
  waiting for transfers between devices: 915 us -> 226 us
  matrix products: 258 us -> 0 us
  Pallas kernels: 0 us -> 193 us
  blocking collectives: 73.4 us -> 0 us
  starting transfers between devices: 0.53 us -> 69.2 us
  other arithmetic: 78.9 us -> 18.5 us
  local copies, waits for them, and re-layouts: 68.1 us -> 36.2 us
  between operations: 18.2 us -> 1.97 us
    reduce_scatter x6 -> x0, waiting for transfers between devices: 640 us -> none  [the longest x1 207 us: shards(): lax.psum_scatter(grad_key_rows.reshape(row_count, row_len, features), 'se...]
    dot_general x40 -> x0, matrix products: 258 us -> none  [the longest x4 58.4 us: matmul(): return jnp.dot(left, right, preferred_element_type=jnp.float32)]
    ppermute x0 -> x62, waiting for transfers between devices: none -> 226 us  [the longest x18 104 us: seq_exchange(): lax.ppermute(block(me + k), 'seq', [(i, (i + k) % parts) for i in range(p...]
    all_gather x6 -> x0, waiting for transfers between devices: 200 us -> none  [the longest x1 106 us: shards(): lax.all_gather(value_local, 'seq', axis=1, tiled=True)]
    pallas_call x0 -> x8, Pallas kernels: none -> 193 us  [the longest x1 51.9 us: attention_backward(): pl.pallas_call(functools.partial(attention_backward_kernel, q_tiles), gri...]
    psum x1 -> x0, waiting for transfers between devices: 74 us -> none  [shards(): lax.psum((every_shard[0], every_shard[1], every_shard[2], every_shard[3],...]
    ppermute x0 -> x62, starting transfers between devices: none -> 69.2 us  [the longest x18 28.1 us: seq_exchange(): lax.ppermute(block(me + k), 'seq', [(i, (i + k) % parts) for i in range(p...]
    unnamed x2 -> x0, blocking collectives: 52.4 us -> none
  transfers between devices with their start and end apart: 13 -> 62, of which waited for: 9 -> 34; matrix products, arithmetic and copies ran while one was open for 16% -> 5% of each run, Pallas kernels for 0% -> 25%
where the time goes in v1:
time: 552 us; the launch traced here: 545 us
  waiting for transfers between devices  226 us (41%)
  Pallas kernels  193 us (35%)
  starting transfers between devices  69.2 us (13%)
  local copies, waits for them, and re-layouts  36.2 us (7%)
  other arithmetic  18.5 us (3%)
    ppermute x18, waiting for transfers between devices, seq_exchange(): lax.ppermute(block(me + k), 'seq', [(i, (i + k) % parts) for i in range(p...  104 us
    ppermute x34, waiting for transfers between devices, dp_swap(): return lax.ppermute(value, 'dp', [(i, i ^ bit) for i in range(VIRTUAL)])  75.6 us
    pallas_call x1, Pallas kernels, attention_backward(): pl.pallas_call(functools.partial(attention_backward_kernel, q_tiles), gri...  51.9 us
    pallas_call x1, Pallas kernels, attention_forward(): pl.pallas_call(attention_forward_kernel, grid=(pairs, tokens // tile), in...  47.4 us
    pallas_call x1, Pallas kernels, mlp(): pl.pallas_call(functools.partial(mlp_kernel, rows, tiles, block), grid=(h...  46.6 us
    ppermute x18, starting transfers between devices, seq_exchange(): lax.ppermute(block(me + k), 'seq', [(i, (i + k) % parts) for i in range(p...  28.1 us
    ppermute x4, waiting for transfers between devices, sum_everywhere(): lax.ppermute(value, 'seq', [(i, i ^ bit) for i in range(parts)])  25.8 us
    ppermute x34, starting transfers between devices, dp_swap(): return lax.ppermute(value, 'dp', [(i, i ^ bit) for i in range(VIRTUAL)])  23.3 us
  transfers between devices with their start and end apart: 62, of which 34 were waited for; matrix products, arithmetic and copies ran while one was open for 5% of the time, Pallas kernels for 25%

profile of v1, /device:TPU:0, one launch (start us, length us, event | category | flops | bytes accessed | tf_op | source)
XLA Modules:
  0.0 545.3 jit_solution(16585500262187759574)
XLA Ops:
  7.4 3.0 collective-permute-start.4
  10.4 1.5 collective-permute-start.6
  13.1 2.7 collective-permute-start
  15.7 1.6 collective-permute-start.1
  18.0 24.7 %collective-permute-done = bf16[256,768]{1,0:T(8,128)(2,1)} collective-permute-done((bf16[256,768]{1,0:T(8,128)(2,1)}, bf16[256,768]{1,0:T(8,128)(2,1)}, u32[]{:S(2)}, u32[]{:S(2)}) %collective-permute-start) | collective-permute-done | bytes 393248 | tf_op jit(solution)/shard_map/ppermute | solution.py:594
  42.8 1.8 bitcast_dynamic-update-slice_fusion.11
  45.1 1.8 bitcast_dynamic-update-slice_fusion.10
  46.9 6.5 %collective-permute-done.2 = bf16[256,768]{1,0:T(8,128)(2,1)S(1)} collective-permute-done((bf16[256,768]{1,0:T(8,128)(2,1)S(1)}, bf16[256,768]{1,0:T(8,128)(2,1)S(1)}, u32[]{:S(2)}, u32[]{:S(2)}) %collective-permute-start.2) | collective-permute-done | bytes 393248 | tf_op jit(solution)/shard_map/ppermute | solution.py:594
  55.0 2.6 collective-permute-start.11
  61.2 20.9 %collective-permute-done.10 = bf16[256,768]{1,0:T(8,128)(2,1)S(1)} collective-permute-done((bf16[256,768]{1,0:T(8,128)(2,1)S(1)}, bf16[256,768]{1,0:T(8,128)(2,1)S(1)}, u32[]{:S(2)}, u32[]{:S(2)}) %collective-permute-start.10) | collective-permute-done | bytes 393248 | tf_op jit(solution)/shard_map/ppermute | solution.py:594
  82.7 3.7 collective-permute-done.8.refs_6_
  87.0 1.5 collective-permute-start.18
  98.6 10.5 %joint_forward.1 = (bf16[1024,2304]{1,0:T(8,128)(2,1)}, bf16[768,1024]{1,0:T(8,128)(2,1)S(1)}, bf16[768,2304]{1,0:T(8,128)(2,1)}) custom-call(s32[1]{0:T(128)} %bitcast.place_ref, bf16[1024,768]{1,0:T(8,128)(2,1)} %bitcast.163, f32[1,768]{1,0:T(1,128)S(1)} %reshape.205.gain_ref, f32[1,768]{1,0:T(1,128)S(1)} %reshape.206.shift_ref, ...), custom_call_target="tpu_custom_call" | custom-call | flops 3623878656 | bytes 14680064 | tf_op jit(solution)/shard_map/joint_forward/pallas_call | solution.py:99
  110.5 8.1 %collective-permute-done.14.refs_2_ = bf16[96,6912]{1,0:T(8,128)(2,1)S(1)} collective-permute-done((bf16[96,6912]{1,0:T(8,128)(2,1)S(1)}, bf16[96,6912]{1,0:T(8,128)(2,1)S(1)}, u32[]{:S(2)}, u32[]{:S(2)}) %collective-permute-start.14) | collective-permute-done | bytes 1327136 | tf_op jit(solution)/shard_map/ppermute | solution.py:583
  118.5 28.1 %collective-permute-done.18.refs_6_ = bf16[96,6912]{1,0:T(8,128)(2,1)} collective-permute-done((bf16[96,6912]{1,0:T(8,128)(2,1)}, bf16[96,6912]{1,0:T(8,128)(2,1)}, u32[]{:S(2)}, u32[]{:S(2)}) %collective-permute-start.18) | collective-permute-done | bytes 1327136 | tf_op jit(solution)/shard_map/ppermute | solution.py:583
  148.0 47.4 %attention_forward.1 = (bf16[1024,768]{1,0:T(8,128)(2,1)S(1)}, f32[6,8,1024]{2,1,0:T(8,128)S(1)}) custom-call(bf16[1024,2304]{1,0:T(8,128)(2,1)} %get-tuple-element.47.q_ref.k_ref.v_ref, bf16[1024,2304]{1,0:T(8,128)(2,1)} %get-tuple-element.47.q_ref.k_ref.v_ref, bf16[1024,2304]{1,0:T(8,128)(2,1)} %get-tuple-element.47.q_ref.k_ref.v_ref, ...), custom_call_target="tpu_custom_call" | custom-call | flops 12884901888 | bytes 8388608 | tf_op jit(solution)/shard_map/attention_forward/pallas_call | solution.py:154
  196.6 8.4 %middle_forward.1 = (f32[1024,768]{1,0:T(8,128)}, bf16[1024,768]{1,0:T(8,128)(2,1)}, bf16[768,1024]{1,0:T(8,128)(2,1)}, bf16[1024,768]{1,0:T(8,128)(2,1)}, bf16[768,768]{1,0:T(8,128)(2,1)S(1)}) custom-call(s32[1]{0:T(128)} %bitcast.place_ref, s32[8]{0:T(128)S(1)} %fusion.16.flags_ref, bf16[1024,768]{1,0:T(8,128)(2,1)} %copy-done.2, ...), custom_call_target="tpu_custom_call" | custom-call | flops 1207959552 | bytes 16777216 | tf_op jit(solution)/shard_map/middle_forward/pallas_call | solution.py:286
  206.0 46.6 %mlp.1 = (f32[1024,768]{1,0:T(8,128)}, f32[1024,768]{1,0:T(8,128)}, bf16[4,96,3072]{2,1,0:T(8,128)(2,1)}, bf16[4,96,3072]{2,1,0:T(8,128)(2,1)}, bf16[4,96,3072]{...) custom-call(s32[1]{0:T(128)} %bitcast.place_ref, bf16[1024,768]{1,0:T(8,128)(2,1)} %get-tuple-element.52.normed_ref, ...), custom_call_target="tpu_custom_call" | custom-call | flops 28991029248 | bytes 31457280 | tf_op jit(solution)/shard_map/mlp/pallas_call | solution.py:413
  253.3 12.8 %output_backward.1 = (bf16[1024,768]{1,0:T(8,128)(2,1)}, f32[1024,768]{1,0:T(8,128)}, bf16[1024,768]{1,0:T(8,128)(2,1)}, bf16[4,96,768]{2,1,0:T(8,128)(2,1)}, bf...) custom-call(s32[1]{0:T(128)} %bitcast.place_ref, s32[8]{0:T(128)} %copy-done.11, f32[1024,768]{1,0:T(8,128)} %get-tuple-element.51.middle_ref, ...), custom_call_target="tpu_custom_call" | custom-call | flops 2415919104 | bytes 23068672 | tf_op jit(solution)/shard_map/output_backward/pallas_call | solution.py:490
  267.2 51.9 %attention_backward.1 = (bf16[1024,768]{1,0:T(8,128)(2,1)}, bf16[1024,768]{1,0:T(8,128)(2,1)}, bf16[1024,768]{1,0:T(8,128)(2,1)}) custom-call(bf16[1024,2304]{1,0:T(8,128)(2,1)} %get-tuple-element.47.q_ref.k_ref.v_ref, bf16[1024,2304]{1,0:T(8,128)(2,1)} %get-tuple-element.47.q_ref.k_ref.v_ref, bf16[1024,2304]{1,0:T(8,128)(2,1)} %get-tuple-element.47.q_ref.k_ref.v_ref, ...), custom_call_target="tpu_custom_call" | custom-call | flops 19327352832 | bytes 14680064 | tf_op jit(solution)/shard_map/attention_backward/pallas_call | solution.py:219
  319.1 1.4 copy-done.22
  320.5 1.4 copy-done.24
  321.9 7.1 %joint_weight_grad.1 = (bf16[4,96,2304]{2,1,0:T(8,128)(2,1)}, bf16[4,96,2304]{2,1,0:T(8,128)(2,1)}, f32[1,2304]{1,0:T(1,128)S(1)}) custom-call(s32[1]{0:T(128)} %bitcast.place_ref, bf16[768,1024]{1,0:T(8,128)(2,1)S(1)} %copy-done.27, bf16[1024,768]{1,0:T(8,128)(2,1)S(1)} %copy-done.22, bf16[1024,768]{1,0:T(8,128)(2,1)S(1)} %copy-done.24, ...), custom_call_target="tpu_custom_call" | custom-call | flops 3623878656 | bytes 10485760 | tf_op jit(solution)/shard_map/joint_weight_grad/pallas_call | solution.py:532
  329.1 8.4 %joint_backward.1 = (bf16[1024,768]{1,0:T(8,128)(2,1)S(1)}, f32[8,768]{1,0:T(8,128)S(1)}) custom-call(bf16[1024,768]{1,0:T(8,128)(2,1)S(1)} %copy-done.23, bf16[1024,768]{1,0:T(8,128)(2,1)S(1)} %copy-done.25, bf16[1024,768]{1,0:T(8,128)(2,1)} %get-tuple-element.63.dv_ref, bf16[768,2304]{1,0:T(8,128)(2,1)} %get-tuple-element.64.weight_ref, ...), custom_call_target="tpu_custom_call" | custom-call | flops 3623878656 | bytes 15728640 | tf_op jit(solution)/shard_map/joint_backward/pallas_call | solution.py:564
  339.5 1.5 collective-permute-start.58
  341.1 1.6 collective-permute-done.27
  343.4 2.9 collective-permute-done.28
  346.4 4.1 collective-permute-start.29
  350.4 1.6 collective-permute-start.59
  352.1 2.9 collective-permute-start.30
  355.4 9.2 %collective-permute-done.30 = f32[24,128]{1,0:T(8,128)S(1)} collective-permute-done((f32[24,128]{1,0:T(8,128)S(1)}, f32[24,128]{1,0:T(8,128)S(1)}, u32[]{:S(2)}, u32[]{:S(2)}) %collective-permute-start.30) | collective-permute-done | bytes 12320 | tf_op jit(solution)/shard_map/ppermute | solution.py:643
  364.6 8.7 %collective-permute-done.60 = f32[48,128]{1,0:T(8,128)S(1)} collective-permute-done((f32[48,128]{1,0:T(8,128)S(1)}, f32[48,128]{1,0:T(8,128)S(1)}, u32[]{:S(2)}, u32[]{:S(2)}) %collective-permute-start.60) | collective-permute-done | bytes 24608 | tf_op jit(solution)/shard_map/ppermute | solution.py:643
  374.5 7.8 %collective-permute-done.61 = f32[48,128]{1,0:T(8,128)S(1)} collective-permute-done((f32[48,128]{1,0:T(8,128)S(1)}, f32[48,128]{1,0:T(8,128)S(1)}, u32[]{:S(2)}, u32[]{:S(2)}) %collective-permute-start.61) | collective-permute-done | bytes 24608 | tf_op jit(solution)/shard_map/ppermute | solution.py:643
  383.6 3.8 collective-permute-start.25
  387.5 4.6 collective-permute-done.24
  392.1 3.5 collective-permute-done.25
  395.6 3.6 collective-permute-start.20
  399.6 20.7 %collective-permute-done.20 = bf16[256,768]{1,0:T(8,128)(2,1)S(1)} collective-permute-done((bf16[256,768]{1,0:T(8,128)(2,1)S(1)}, bf16[256,768]{1,0:T(8,128)(2,1)S(1)}, u32[]{:S(2)}, u32[]{:S(2)}) %collective-permute-start.20) | collective-permute-done | bytes 393248 | tf_op jit(solution)/shard_map/ppermute | solution.py:594
  420.9 1.9 convert_element_type.208
  422.9 5.1 collective-permute-done.49
  430.8 1.6 collective-permute-done.22
  432.5 2.4 collective-permute-done.50
  435.7 5.7 %collective-permute-done.34 = bf16[2,96,1152]{2,1,0:T(8,128)(2,1)S(1)} collective-permute-done((bf16[2,96,1152]{2,1,0:T(8,128)(2,1)S(1)}, bf16[2,96,1152]{2,1,0:T(8,128)(2,1)S(1)}, u32[]{:S(2)}, u32[]{:S(2)}) %collective-permute-start.34) | collective-permute-done | bytes 442400 | tf_op jit(solution)/shard_map/ppermute | solution.py:583
  442.3 3.2 collective-permute-done.32
  452.8 1.4 copy-done.30
  456.5 2.3 collective-permute-start.37
  458.8 1.5 collective-permute-start.38
  460.4 3.9 collective-permute-done.37
  464.3 3.3 collective-permute-done.38
  468.9 2.7 collective-permute-start.41
  471.6 2.8 collective-permute-done.39
  474.5 2.0 collective-permute-done.40
  476.5 1.8 add_convert_fusion.3
  479.2 3.5 collective-permute-done.46
  482.7 1.7 add_convert_fusion.2
  485.1 5.6 %collective-permute-done.44 = bf16[96,3072]{1,0:T(8,128)(2,1)S(1)} collective-permute-done((bf16[96,3072]{1,0:T(8,128)(2,1)S(1)}, bf16[96,3072]{1,0:T(8,128)(2,1)S(1)}, u32[]{:S(2)}, u32[]{:S(2)}) %collective-permute-start.44) | collective-permute-done | bytes 589856 | tf_op jit(solution)/shard_map/ppermute | solution.py:583
  490.8 3.5 collective-permute-done.47
  494.8 4.5 collective-permute-start.51
  500.3 3.8 collective-permute-start.53
  504.1 14.4 %collective-permute-done.51 = bf16[24,6912]{1,0:T(8,128)(2,1)S(1)} collective-permute-done((bf16[24,6912]{1,0:T(8,128)(2,1)S(1)}, bf16[24,6912]{1,0:T(8,128)(2,1)S(1)}, u32[]{:S(2)}, u32[]{:S(2)}) %collective-permute-start.51) | collective-permute-done | bytes 331808 | tf_op jit(solution)/shard_map/ppermute | solution.py:594
  518.9 4.5 collective-permute-start.54
  523.5 2.4 collective-permute-start.56
  526.0 5.6 %collective-permute-done.54 = bf16[24,6912]{1,0:T(8,128)(2,1)S(1)} collective-permute-done((bf16[24,6912]{1,0:T(8,128)(2,1)S(1)}, bf16[24,6912]{1,0:T(8,128)(2,1)S(1)}, u32[]{:S(2)}, u32[]{:S(2)}) %collective-permute-start.54) | collective-permute-done | bytes 331808 | tf_op jit(solution)/shard_map/ppermute | solution.py:631
  531.7 9.7 %collective-permute-done.55 = bf16[24,6912]{1,0:T(8,128)(2,1)S(1)} collective-permute-done((bf16[24,6912]{1,0:T(8,128)(2,1)S(1)}, bf16[24,6912]{1,0:T(8,128)(2,1)S(1)}, u32[]{:S(2)}, u32[]{:S(2)}) %collective-permute-start.55) | collective-permute-done | bytes 331808 | tf_op jit(solution)/shard_map/ppermute | solution.py:631
  (314 shorter events, 61.5 us)
Async XLA Ops:
  7.4 37.1 %collective-permute-start.4 = (bf16[112,2304]{1,0:T(8,128)(2,1)S(1)}, bf16[112,2304]{1,0:T(8,128)(2,1)}, u32[]{:S(2)}, u32[]{:S(2)}) collective-permute-start(bf16[112,2304]{1,0:T(8,128)(2,1)S(1)} %fusion.3.refs_0_), channel_id=1, source_target_pairs={{0,8},{4,12},{8,0},{12,4},{16,24},{20,28},{24,16},{28,20},{1,9},{5... | collective-permute-start | bytes 1548296 | tf_op jit(solution)/shard_map/ppermute | solution.py:583
  10.4 34.1 %collective-permute-start.6 = (bf16[112,2304]{1,0:T(8,128)(2,1)S(1)}, bf16[112,2304]{1,0:T(8,128)(2,1)}, u32[]{:S(2)}, u32[]{:S(2)}) collective-permute-start(bf16[112,2304]{1,0:T(8,128)(2,1)S(1)} %fusion.3.refs_0_), channel_id=1, source_target_pairs={{0,16},{4,20},{8,24},{12,28},{16,0},{20,4},{24,8},{28,12},{1,17},{... | collective-permute-start | bytes 1548296 | tf_op jit(solution)/shard_map/ppermute | solution.py:583
  11.9 48.0 %collective-permute-start.3 = (bf16[112,2304]{1,0:T(8,128)(2,1)S(1)}, bf16[112,2304]{1,0:T(8,128)(2,1)S(1)}, u32[]{:S(2)}, u32[]{:S(2)}) collective-permute-start(bf16[112,2304]{1,0:T(8,128)(2,1)S(1)} %fusion.3.refs_0_), channel_id=1, source_target_pairs={{0,4},{4,0},{8,12},{12,8},{16,20},{20,16},{24,28},{28,24},{1,5},{5... | collective-permute-start | bytes 1548296 | tf_op jit(solution)/shard_map/ppermute | solution.py:583
  13.1 29.7 %collective-permute-start = (bf16[256,768]{1,0:T(8,128)(2,1)}, bf16[256,768]{1,0:T(8,128)(2,1)}, u32[]{:S(2)}, u32[]{:S(2)}) collective-permute-start(bf16[256,768]{1,0:T(8,128)(2,1)} %get-tuple-element.108), channel_id=1, source_target_pairs={{0,2},{1,3},{2,0},{3,1},{4,6},{5,7},{6,4},{7,5},{8,10},{9,11},{10,... | collective-permute-start | bytes 1179656 | tf_op jit(solution)/shard_map/ppermute | solution.py:594
  15.7 29.4 %collective-permute-start.1 = (bf16[256,768]{1,0:T(8,128)(2,1)}, bf16[256,768]{1,0:T(8,128)(2,1)}, u32[]{:S(2)}, u32[]{:S(2)}) collective-permute-start(bf16[256,768]{1,0:T(8,128)(2,1)} %get-tuple-element.110), channel_id=1, source_target_pairs={{0,1},{1,2},{2,3},{3,0},{4,5},{5,6},{6,7},{7,4},{8,9},{9,10},{10,1... | collective-permute-start | bytes 1179656 | tf_op jit(solution)/shard_map/ppermute | solution.py:594
  17.6 178.9 %copy-start.4 = (bf16[96,6912]{1,0:T(8,128)(2,1)}, bf16[96,6912]{1,0:T(8,128)(2,1)S(1)}, u32[]{:S(2)}) copy-start(bf16[96,6912]{1,0:T(8,128)(2,1)S(1)} %slice_dynamic-update-slice_fusion.refs_0_) | copy-start | bytes 3981316
  17.9 178.6 %copy-start.3 = (s32[1024,1]{1,0:T(8,128)}, s32[1024,1]{1,0:T(8,128)S(1)}, u32[]{:S(2)}) copy-start(s32[1024,1]{1,0:T(8,128)S(1)} %copy.34.segk_ref.seg_ref) | copy-start | bytes 12292
  42.8 10.7 %collective-permute-start.2 = (bf16[256,768]{1,0:T(8,128)(2,1)S(1)}, bf16[256,768]{1,0:T(8,128)(2,1)S(1)}, u32[]{:S(2)}, u32[]{:S(2)}) collective-permute-start(bf16[256,768]{1,0:T(8,128)(2,1)S(1)} %get-tuple-element.107), channel_id=1, source_target_pairs={{0,3},{1,0},{2,1},{3,2},{4,7},{5,4},{6,5},{7,6},{8,11},{9,8},{10,9... | collective-permute-start | bytes 1179656 | tf_op jit(solution)/shard_map/ppermute | solution.py:594
  44.5 42.5 %collective-permute-start.16 = (bf16[96,6912]{1,0:T(8,128)(2,1)S(1)}, bf16[96,6912]{1,0:T(8,128)(2,1)}, u32[]{:S(2)}, u32[]{:S(2)}) collective-permute-start(bf16[96,6912]{1,0:T(8,128)(2,1)S(1)} %slice_dynamic-update-slice_fusion.refs_0_), channel_id=1, source_target_pairs={{0,16},{4,20},{8,24},{12,28},{16,0},{20,4},{24,8},{28,12},{1,17},{... | collective-permute-start | bytes 3981320 | tf_op jit(solution)/shard_map/ppermute | solution.py:583
  54.2 32.1 %collective-permute-start.8 = (bf16[112,2304]{1,0:T(8,128)(2,1)}, bf16[112,2304]{1,0:T(8,128)(2,1)S(1)}, u32[]{:S(2)}, u32[]{:S(2)}) collective-permute-start(bf16[112,2304]{1,0:T(8,128)(2,1)} %collective-permute-done.4.refs_2_), channel_id=1, source_target_pairs={{0,16},{4,20},{8,24},{12,28},{16,0},{20,4},{24,8},{28,12},{1,17},{... | collective-permute-start | bytes 1548296 | tf_op jit(solution)/shard_map/ppermute | solution.py:583
  55.0 27.2 %collective-permute-start.10 = (bf16[256,768]{1,0:T(8,128)(2,1)S(1)}, bf16[256,768]{1,0:T(8,128)(2,1)S(1)}, u32[]{:S(2)}, u32[]{:S(2)}) collective-permute-start(bf16[256,768]{1,0:T(8,128)(2,1)S(1)} %get-tuple-element.105), channel_id=1, source_target_pairs={{0,2},{1,3},{2,0},{3,1},{4,6},{5,7},{6,4},{7,5},{8,10},{9,11},{10,... | collective-permute-start | bytes 1179656 | tf_op jit(solution)/shard_map/ppermute | solution.py:594
  55.0 27.1 %collective-permute-start.11 = (bf16[256,768]{1,0:T(8,128)(2,1)S(1)}, bf16[256,768]{1,0:T(8,128)(2,1)S(1)}, u32[]{:S(2)}, u32[]{:S(2)}) collective-permute-start(bf16[256,768]{1,0:T(8,128)(2,1)S(1)} %get-tuple-element.104), channel_id=1, source_target_pairs={{0,1},{1,2},{2,3},{3,0},{4,5},{5,6},{6,7},{7,4},{8,9},{9,10},{10,1... | collective-permute-start | bytes 1179656 | tf_op jit(solution)/shard_map/ppermute | solution.py:594
  59.9 26.5 %collective-permute-start.12 = (bf16[256,768]{1,0:T(8,128)(2,1)S(1)}, bf16[256,768]{1,0:T(8,128)(2,1)S(1)}, u32[]{:S(2)}, u32[]{:S(2)}) collective-permute-start(bf16[256,768]{1,0:T(8,128)(2,1)S(1)} %get-tuple-element.103), channel_id=1, source_target_pairs={{0,3},{1,0},{2,1},{3,2},{4,7},{5,4},{6,5},{7,6},{8,11},{9,8},{10,9... | collective-permute-start | bytes 1179656 | tf_op jit(solution)/shard_map/ppermute | solution.py:594
  82.2 6.4 %collective-permute-start.5 = (bf16[112,2304]{1,0:T(8,128)(2,1)}, bf16[112,2304]{1,0:T(8,128)(2,1)S(1)}, u32[]{:S(2)}, u32[]{:S(2)}) collective-permute-start(bf16[112,2304]{1,0:T(8,128)(2,1)} %collective-permute-done.4.refs_2_), channel_id=1, source_target_pairs={{0,4},{4,0},{8,12},{12,8},{16,20},{20,16},{24,28},{28,24},{1,5},{5... | collective-permute-start | bytes 1548296 | tf_op jit(solution)/shard_map/ppermute | solution.py:583
  82.2 7.7 %collective-permute-start.7 = (bf16[112,2304]{1,0:T(8,128)(2,1)}, bf16[112,2304]{1,0:T(8,128)(2,1)S(1)}, u32[]{:S(2)}, u32[]{:S(2)}) collective-permute-start(bf16[112,2304]{1,0:T(8,128)(2,1)} %collective-permute-done.6.refs_4_), channel_id=1, source_target_pairs={{0,4},{4,0},{8,12},{12,8},{16,20},{20,16},{24,28},{28,24},{1,5},{5... | collective-permute-start | bytes 1548296 | tf_op jit(solution)/shard_map/ppermute | solution.py:583
  86.3 4.3 collective-permute-start.9
  86.4 32.1 %collective-permute-start.14 = (bf16[96,6912]{1,0:T(8,128)(2,1)S(1)}, bf16[96,6912]{1,0:T(8,128)(2,1)S(1)}, u32[]{:S(2)}, u32[]{:S(2)}) collective-permute-start(bf16[96,6912]{1,0:T(8,128)(2,1)S(1)} %slice_dynamic-update-slice_fusion.refs_0_), channel_id=1, source_target_pairs={{0,8},{4,12},{8,0},{12,4},{16,24},{20,28},{24,16},{28,20},{1,9},{5... | collective-permute-start | bytes 3981320 | tf_op jit(solution)/shard_map/ppermute | solution.py:583
  87.0 59.5 %collective-permute-start.18 = (bf16[96,6912]{1,0:T(8,128)(2,1)}, bf16[96,6912]{1,0:T(8,128)(2,1)}, u32[]{:S(2)}, u32[]{:S(2)}) collective-permute-start(bf16[96,6912]{1,0:T(8,128)(2,1)} %collective-permute-done.16.refs_4_), channel_id=1, source_target_pairs={{0,8},{4,12},{8,0},{12,4},{16,24},{20,28},{24,16},{28,20},{1,9},{5... | collective-permute-start | bytes 3981320 | tf_op jit(solution)/shard_map/ppermute | solution.py:583
  88.6 107.9 %collective-permute-start.13 = (bf16[96,6912]{1,0:T(8,128)(2,1)S(1)}, bf16[96,6912]{1,0:T(8,128)(2,1)}, u32[]{:S(2)}, u32[]{:S(2)}) collective-permute-start(bf16[96,6912]{1,0:T(8,128)(2,1)S(1)} %slice_dynamic-update-slice_fusion.refs_0_), channel_id=1, source_target_pairs={{0,4},{4,0},{8,12},{12,8},{16,20},{20,16},{24,28},{28,24},{1,5},{5... | collective-permute-start | bytes 3981320 | tf_op jit(solution)/shard_map/ppermute | solution.py:583
  110.3 86.2 %collective-permute-start.17 = (bf16[96,6912]{1,0:T(8,128)(2,1)}, bf16[96,6912]{1,0:T(8,128)(2,1)}, u32[]{:S(2)}, u32[]{:S(2)}) collective-permute-start(bf16[96,6912]{1,0:T(8,128)(2,1)} %collective-permute-done.16.refs_4_), channel_id=1, source_target_pairs={{0,4},{4,0},{8,12},{12,8},{16,20},{20,16},{24,28},{28,24},{1,5},{5... | collective-permute-start | bytes 3981320 | tf_op jit(solution)/shard_map/ppermute | solution.py:583
  118.5 78.0 %collective-permute-start.15 = (bf16[96,6912]{1,0:T(8,128)(2,1)S(1)}, bf16[96,6912]{1,0:T(8,128)(2,1)}, u32[]{:S(2)}, u32[]{:S(2)}) collective-permute-start(bf16[96,6912]{1,0:T(8,128)(2,1)S(1)} %collective-permute-done.14.refs_2_), channel_id=1, source_target_pairs={{0,4},{4,0},{8,12},{12,8},{16,20},{20,16},{24,28},{28,24},{1,5},{5... | collective-permute-start | bytes 3981320 | tf_op jit(solution)/shard_map/ppermute | solution.py:583
  146.6 49.9 %collective-permute-start.19 = (bf16[96,6912]{1,0:T(8,128)(2,1)}, bf16[96,6912]{1,0:T(8,128)(2,1)}, u32[]{:S(2)}, u32[]{:S(2)}) collective-permute-start(bf16[96,6912]{1,0:T(8,128)(2,1)} %collective-permute-done.18.refs_6_), channel_id=1, source_target_pairs={{0,4},{4,0},{8,12},{12,8},{16,20},{20,16},{24,28},{28,24},{1,5},{5... | collective-permute-start | bytes 3981320 | tf_op jit(solution)/shard_map/ppermute | solution.py:583
  252.6 194.3 %collective-permute-start.42 = (bf16[4,96,3072]{2,1,0:T(8,128)(2,1)}, bf16[4,96,3072]{2,1,0:T(8,128)(2,1)S(1)}, u32[]{:S(2)}, u32[]{:S(2)}) collective-permute-start(bf16[4,96,3072]{2,1,0:T(8,128)(2,1)} %get-tuple-element.73), channel_id=1, source_target_pairs={{0,4},{4,0},{8,12},{12,8},{16,20},{20,16},{24,28},{28,24},{1,5},{5... | collective-permute-start | bytes 7077896 | tf_op jit(solution)/shard_map/ppermute | solution.py:583
  266.1 133.2 %collective-permute-start.48 = (bf16[4,96,768]{2,1,0:T(8,128)(2,1)}, bf16[4,96,768]{2,1,0:T(8,128)(2,1)S(1)}, u32[]{:S(2)}, u32[]{:S(2)}) collective-permute-start(bf16[4,96,768]{2,1,0:T(8,128)(2,1)} %get-tuple-element.77), channel_id=1, source_target_pairs={{0,4},{4,0},{8,12},{12,8},{16,20},{20,16},{24,28},{28,24},{1,5},{5... | collective-permute-start | bytes 1769480 | tf_op jit(solution)/shard_map/ppermute | solution.py:583
  337.5 1.4 collective-permute-start.26
  338.1 1.4 collective-permute-start.57
  338.2 91.3 %collective-permute-start.31 = (bf16[4,96,2304]{2,1,0:T(8,128)(2,1)S(1)}, bf16[4,96,2304]{2,1,0:T(8,128)(2,1)S(1)}, u32[]{:S(2)}, u32[]{:S(2)}) collective-permute-start(bf16[4,96,2304]{2,1,0:T(8,128)(2,1)S(1)} %copy-done.47), channel_id=1, source_target_pairs={{0,4},{4,0},{8,12},{12,8},{16,20},{20,16},{24,28},{28,24},{1,5},{5... | collective-permute-start | bytes 5308424 | tf_op jit(solution)/shard_map/ppermute | solution.py:583
  338.9 3.8 collective-permute-start.27
  339.5 10.9 %collective-permute-start.58 = (f32[48,128]{1,0:T(8,128)S(1)}, f32[48,128]{1,0:T(8,128)S(1)}, u32[]{:S(2)}, u32[]{:S(2)}) collective-permute-start(f32[48,128]{1,0:T(8,128)S(1)} %bitcast_add_fusion), channel_id=1, source_target_pairs={{0,8},{4,12},{8,0},{12,4},{16,24},{20,28},{24,16},{28,20},{1,9},{5... | collective-permute-start | bytes 73736 | tf_op jit(solution)/shard_map/ppermute | solution.py:583
  342.7 3.7 collective-permute-start.28
  346.4 5.7 %collective-permute-start.29 = (f32[24,128]{1,0:T(8,128)S(1)}, f32[24,128]{1,0:T(8,128)S(1)}, u32[]{:S(2)}, u32[]{:S(2)}) collective-permute-start(f32[24,128]{1,0:T(8,128)S(1)} %add.317), channel_id=1, source_target_pairs={{0,1},{1,0},{2,3},{3,2},{4,5},{5,4},{6,7},{7,6},{8,9},{9,8},{10,11... | collective-permute-start | bytes 36872 | tf_op jit(solution)/shard_map/ppermute | solution.py:643
  350.4 4.8 collective-permute-start.59
  352.1 12.4 %collective-permute-start.30 = (f32[24,128]{1,0:T(8,128)S(1)}, f32[24,128]{1,0:T(8,128)S(1)}, u32[]{:S(2)}, u32[]{:S(2)}) collective-permute-start(f32[24,128]{1,0:T(8,128)S(1)} %add.318), channel_id=1, source_target_pairs={{0,2},{1,3},{2,0},{3,1},{4,6},{5,7},{6,4},{7,5},{8,10},{9,11},{10,... | collective-permute-start | bytes 36872 | tf_op jit(solution)/shard_map/ppermute | solution.py:643
  355.2 28.4 %collective-permute-start.23 = (bf16[256,768]{1,0:T(8,128)(2,1)S(1)}, bf16[256,768]{1,0:T(8,128)(2,1)S(1)}, u32[]{:S(2)}, u32[]{:S(2)}) collective-permute-start(bf16[256,768]{1,0:T(8,128)(2,1)S(1)} %get-tuple-element.97), channel_id=1, source_target_pairs={{0,2},{1,3},{2,0},{3,1},{4,6},{5,7},{6,4},{7,5},{8,10},{9,11},{10,... | collective-permute-start | bytes 1179656 | tf_op jit(solution)/shard_map/ppermute | solution.py:594
  364.6 8.7 %collective-permute-start.60 = (f32[48,128]{1,0:T(8,128)S(1)}, f32[48,128]{1,0:T(8,128)S(1)}, u32[]{:S(2)}, u32[]{:S(2)}) collective-permute-start(f32[48,128]{1,0:T(8,128)S(1)} %add.342), channel_id=1, source_target_pairs={{0,1},{1,0},{2,3},{3,2},{4,5},{5,4},{6,7},{7,6},{8,9},{9,8},{10,11... | collective-permute-start | bytes 73736 | tf_op jit(solution)/shard_map/ppermute | solution.py:643
  373.3 9.1 %collective-permute-start.61 = (f32[48,128]{1,0:T(8,128)S(1)}, f32[48,128]{1,0:T(8,128)S(1)}, u32[]{:S(2)}, u32[]{:S(2)}) collective-permute-start(f32[48,128]{1,0:T(8,128)S(1)} %add.343), channel_id=1, source_target_pairs={{0,2},{1,3},{2,0},{3,1},{4,6},{5,7},{6,4},{7,5},{8,10},{9,11},{10,... | collective-permute-start | bytes 73736 | tf_op jit(solution)/shard_map/ppermute | solution.py:643
  382.4 9.7 %collective-permute-start.24 = (bf16[256,768]{1,0:T(8,128)(2,1)S(1)}, bf16[256,768]{1,0:T(8,128)(2,1)S(1)}, u32[]{:S(2)}, u32[]{:S(2)}) collective-permute-start(bf16[256,768]{1,0:T(8,128)(2,1)S(1)} %get-tuple-element.96), channel_id=1, source_target_pairs={{0,1},{1,2},{2,3},{3,0},{4,5},{5,6},{6,7},{7,4},{8,9},{9,10},{10,1... | collective-permute-start | bytes 1179656 | tf_op jit(solution)/shard_map/ppermute | solution.py:594
  383.6 12.0 %collective-permute-start.25 = (bf16[256,768]{1,0:T(8,128)(2,1)S(1)}, bf16[256,768]{1,0:T(8,128)(2,1)S(1)}, u32[]{:S(2)}, u32[]{:S(2)}) collective-permute-start(bf16[256,768]{1,0:T(8,128)(2,1)S(1)} %get-tuple-element.95), channel_id=1, source_target_pairs={{0,3},{1,0},{2,1},{3,2},{4,7},{5,4},{6,5},{7,6},{8,11},{9,8},{10,9... | collective-permute-start | bytes 1179656 | tf_op jit(solution)/shard_map/ppermute | solution.py:594
  392.1 59.8 %collective-permute-start.45 = (bf16[4,96,3072]{2,1,0:T(8,128)(2,1)S(1)}, bf16[4,96,3072]{2,1,0:T(8,128)(2,1)S(1)}, u32[]{:S(2)}, u32[]{:S(2)}) collective-permute-start(bf16[4,96,3072]{2,1,0:T(8,128)(2,1)S(1)} %copy-done.46), channel_id=1, source_target_pairs={{0,4},{4,0},{8,12},{12,8},{16,20},{20,16},{24,28},{28,24},{1,5},{5... | collective-permute-start | bytes 7077896 | tf_op jit(solution)/shard_map/ppermute | solution.py:583
  395.6 24.7 %collective-permute-start.20 = (bf16[256,768]{1,0:T(8,128)(2,1)S(1)}, bf16[256,768]{1,0:T(8,128)(2,1)S(1)}, u32[]{:S(2)}, u32[]{:S(2)}) collective-permute-start(bf16[256,768]{1,0:T(8,128)(2,1)S(1)} %get-tuple-element.101), channel_id=1, source_target_pairs={{0,2},{1,3},{2,0},{3,1},{4,6},{5,7},{6,4},{7,5},{8,10},{9,11},{10,... | collective-permute-start | bytes 1179656 | tf_op jit(solution)/shard_map/ppermute | solution.py:594
  399.3 23.6 %collective-permute-start.21 = (bf16[256,768]{1,0:T(8,128)(2,1)S(1)}, bf16[256,768]{1,0:T(8,128)(2,1)S(1)}, u32[]{:S(2)}, u32[]{:S(2)}) collective-permute-start(bf16[256,768]{1,0:T(8,128)(2,1)S(1)} %get-tuple-element.100), channel_id=1, source_target_pairs={{0,1},{1,2},{2,3},{3,0},{4,5},{5,6},{6,7},{7,4},{8,9},{9,10},{10,1... | collective-permute-start | bytes 1179656 | tf_op jit(solution)/shard_map/ppermute | solution.py:594
  420.3 7.8 %collective-permute-start.49 = (bf16[2,96,768]{2,1,0:T(8,128)(2,1)S(1)}, bf16[2,96,768]{2,1,0:T(8,128)(2,1)S(1)}, u32[]{:S(2)}, u32[]{:S(2)}) collective-permute-start(bf16[2,96,768]{2,1,0:T(8,128)(2,1)S(1)} %slice.233), channel_id=1, source_target_pairs={{0,8},{4,12},{8,0},{12,4},{16,24},{20,28},{24,16},{28,20},{1,9},{5... | collective-permute-start | bytes 884744 | tf_op jit(solution)/shard_map/ppermute | solution.py:583
  422.9 9.6 %collective-permute-start.22 = (bf16[256,768]{1,0:T(8,128)(2,1)S(1)}, bf16[256,768]{1,0:T(8,128)(2,1)S(1)}, u32[]{:S(2)}, u32[]{:S(2)}) collective-permute-start(bf16[256,768]{1,0:T(8,128)(2,1)S(1)} %get-tuple-element.99), channel_id=1, source_target_pairs={{0,3},{1,0},{2,1},{3,2},{4,7},{5,4},{6,5},{7,6},{8,11},{9,8},{10,9... | collective-permute-start | bytes 1179656 | tf_op jit(solution)/shard_map/ppermute | solution.py:594
  428.2 6.8 %collective-permute-start.50 = (bf16[96,768]{1,0:T(8,128)(2,1)S(1)}, bf16[96,768]{1,0:T(8,128)(2,1)S(1)}, u32[]{:S(2)}, u32[]{:S(2)}) collective-permute-start(bf16[96,768]{1,0:T(8,128)(2,1)S(1)} %slice_bitcast_fusion.8), channel_id=1, source_target_pairs={{0,16},{4,20},{8,24},{12,28},{16,0},{20,4},{24,8},{28,12},{1,17},{... | collective-permute-start | bytes 442376 | tf_op jit(solution)/shard_map/ppermute | solution.py:583
  430.0 11.4 %collective-permute-start.34 = (bf16[2,96,1152]{2,1,0:T(8,128)(2,1)S(1)}, bf16[2,96,1152]{2,1,0:T(8,128)(2,1)S(1)}, u32[]{:S(2)}, u32[]{:S(2)}) collective-permute-start(bf16[2,96,1152]{2,1,0:T(8,128)(2,1)S(1)} %slice.273), channel_id=1, source_target_pairs={{0,16},{4,20},{8,24},{12,28},{16,0},{20,4},{24,8},{28,12},{1,17},{... | collective-permute-start | bytes 1327112 | tf_op jit(solution)/shard_map/ppermute | solution.py:583
  435.0 10.4 %collective-permute-start.32 = (bf16[2,96,1152]{2,1,0:T(8,128)(2,1)S(1)}, bf16[2,96,1152]{2,1,0:T(8,128)(2,1)S(1)}, u32[]{:S(2)}, u32[]{:S(2)}) collective-permute-start(bf16[2,96,1152]{2,1,0:T(8,128)(2,1)S(1)} %slice.215), channel_id=1, source_target_pairs={{0,8},{4,12},{8,0},{12,4},{16,24},{20,28},{24,16},{28,20},{1,9},{5... | collective-permute-start | bytes 1327112 | tf_op jit(solution)/shard_map/ppermute | solution.py:583
  441.6 8.6 %collective-permute-start.35 = (bf16[96,1152]{1,0:T(8,128)(2,1)S(1)}, bf16[96,1152]{1,0:T(8,128)(2,1)S(1)}, u32[]{:S(2)}, u32[]{:S(2)}) collective-permute-start(bf16[96,1152]{1,0:T(8,128)(2,1)S(1)} %slice_bitcast_fusion.4), channel_id=1, source_target_pairs={{0,8},{4,12},{8,0},{12,4},{16,24},{20,28},{24,16},{28,20},{1,9},{5... | collective-permute-start | bytes 663560 | tf_op jit(solution)/shard_map/ppermute | solution.py:583
  445.6 6.0 %collective-permute-start.33 = (bf16[96,1152]{1,0:T(8,128)(2,1)S(1)}, bf16[96,1152]{1,0:T(8,128)(2,1)S(1)}, u32[]{:S(2)}, u32[]{:S(2)}) collective-permute-start(bf16[96,1152]{1,0:T(8,128)(2,1)S(1)} %slice_bitcast_fusion.6), channel_id=1, source_target_pairs={{0,16},{4,20},{8,24},{12,28},{16,0},{20,4},{24,8},{28,12},{1,17},{... | collective-permute-start | bytes 663560 | tf_op jit(solution)/shard_map/ppermute | solution.py:583
  449.0 27.5 %collective-permute-start.43 = (bf16[2,96,3072]{2,1,0:T(8,128)(2,1)}, bf16[2,96,3072]{2,1,0:T(8,128)(2,1)}, u32[]{:S(2)}, u32[]{:S(2)}) collective-permute-start(bf16[2,96,3072]{2,1,0:T(8,128)(2,1)} %slice.225), channel_id=1, source_target_pairs={{0,8},{4,12},{8,0},{12,4},{16,24},{20,28},{24,16},{28,20},{1,9},{5... | collective-permute-start | bytes 3538952 | tf_op jit(solution)/shard_map/ppermute | solution.py:583
  451.7 8.6 %collective-permute-start.36 = (bf16[24,2304]{1,0:T(8,128)(2,1)S(1)}, bf16[24,2304]{1,0:T(8,128)(2,1)S(1)}, u32[]{:S(2)}, u32[]{:S(2)}) collective-permute-start(bf16[24,2304]{1,0:T(8,128)(2,1)S(1)} %get-tuple-element.117), channel_id=1, source_target_pairs={{0,2},{1,3},{2,0},{3,1},{4,6},{5,7},{6,4},{7,5},{8,10},{9,11},{10,... | collective-permute-start | bytes 331784 | tf_op jit(solution)/shard_map/ppermute | solution.py:594
  455.2 27.4 %collective-permute-start.46 = (bf16[2,96,3072]{2,1,0:T(8,128)(2,1)}, bf16[2,96,3072]{2,1,0:T(8,128)(2,1)}, u32[]{:S(2)}, u32[]{:S(2)}) collective-permute-start(bf16[2,96,3072]{2,1,0:T(8,128)(2,1)} %slice.279), channel_id=1, source_target_pairs={{0,16},{4,20},{8,24},{12,28},{16,0},{20,4},{24,8},{28,12},{1,17},{... | collective-permute-start | bytes 3538952 | tf_op jit(solution)/shard_map/ppermute | solution.py:583
  456.5 7.7 %collective-permute-start.37 = (bf16[24,2304]{1,0:T(8,128)(2,1)S(1)}, bf16[24,2304]{1,0:T(8,128)(2,1)S(1)}, u32[]{:S(2)}, u32[]{:S(2)}) collective-permute-start(bf16[24,2304]{1,0:T(8,128)(2,1)S(1)} %get-tuple-element.118), channel_id=1, source_target_pairs={{0,1},{1,2},{2,3},{3,0},{4,5},{5,6},{6,7},{7,4},{8,9},{9,10},{10,1... | collective-permute-start | bytes 331784 | tf_op jit(solution)/shard_map/ppermute | solution.py:594
  458.8 8.8 %collective-permute-start.38 = (bf16[24,2304]{1,0:T(8,128)(2,1)S(1)}, bf16[24,2304]{1,0:T(8,128)(2,1)S(1)}, u32[]{:S(2)}, u32[]{:S(2)}) collective-permute-start(bf16[24,2304]{1,0:T(8,128)(2,1)S(1)} %get-tuple-element.115), channel_id=1, source_target_pairs={{0,3},{1,0},{2,1},{3,2},{4,7},{5,4},{6,5},{7,6},{8,11},{9,8},{10,9... | collective-permute-start | bytes 331784 | tf_op jit(solution)/shard_map/ppermute | solution.py:594
  467.7 6.8 %collective-permute-start.39 = (bf16[24,2304]{1,0:T(8,128)(2,1)S(1)}, bf16[24,2304]{1,0:T(8,128)(2,1)S(1)}, u32[]{:S(2)}, u32[]{:S(2)}) collective-permute-start(bf16[24,2304]{1,0:T(8,128)(2,1)S(1)} %reduce_sum.34), channel_id=1, source_target_pairs={{0,1},{1,2},{2,3},{3,0},{4,5},{5,6},{6,7},{7,4},{8,9},{9,10},{10,1... | collective-permute-start | bytes 331784 | tf_op jit(solution)/shard_map/ppermute | solution.py:631
  468.4 8.0 %collective-permute-start.40 = (bf16[24,2304]{1,0:T(8,128)(2,1)S(1)}, bf16[24,2304]{1,0:T(8,128)(2,1)S(1)}, u32[]{:S(2)}, u32[]{:S(2)}) collective-permute-start(bf16[24,2304]{1,0:T(8,128)(2,1)S(1)} %reduce_sum.34), channel_id=1, source_target_pairs={{0,2},{1,3},{2,0},{3,1},{4,6},{5,7},{6,4},{7,5},{8,10},{9,11},{10,... | collective-permute-start | bytes 331784 | tf_op jit(solution)/shard_map/ppermute | solution.py:631
  468.9 7.6 %collective-permute-start.41 = (bf16[24,2304]{1,0:T(8,128)(2,1)S(1)}, bf16[24,2304]{1,0:T(8,128)(2,1)S(1)}, u32[]{:S(2)}, u32[]{:S(2)}) collective-permute-start(bf16[24,2304]{1,0:T(8,128)(2,1)S(1)} %reduce_sum.34), channel_id=1, source_target_pairs={{0,3},{1,0},{2,1},{3,2},{4,7},{5,4},{6,5},{7,6},{8,11},{9,8},{10,9... | collective-permute-start | bytes 331784 | tf_op jit(solution)/shard_map/ppermute | solution.py:631
  478.4 12.3 %collective-permute-start.44 = (bf16[96,3072]{1,0:T(8,128)(2,1)S(1)}, bf16[96,3072]{1,0:T(8,128)(2,1)S(1)}, u32[]{:S(2)}, u32[]{:S(2)}) collective-permute-start(bf16[96,3072]{1,0:T(8,128)(2,1)S(1)} %slice_bitcast_fusion.2), channel_id=1, source_target_pairs={{0,16},{4,20},{8,24},{12,28},{16,0},{20,4},{24,8},{28,12},{1,17},{... | collective-permute-start | bytes 1769480 | tf_op jit(solution)/shard_map/ppermute | solution.py:583
  484.4 9.9 %collective-permute-start.47 = (bf16[96,3072]{1,0:T(8,128)(2,1)S(1)}, bf16[96,3072]{1,0:T(8,128)(2,1)S(1)}, u32[]{:S(2)}, u32[]{:S(2)}) collective-permute-start(bf16[96,3072]{1,0:T(8,128)(2,1)S(1)} %slice_bitcast_fusion), channel_id=1, source_target_pairs={{0,8},{4,12},{8,0},{12,4},{16,24},{20,28},{24,16},{28,20},{1,9},{5... | collective-permute-start | bytes 1769480 | tf_op jit(solution)/shard_map/ppermute | solution.py:583
  494.8 23.6 %collective-permute-start.51 = (bf16[24,6912]{1,0:T(8,128)(2,1)S(1)}, bf16[24,6912]{1,0:T(8,128)(2,1)S(1)}, u32[]{:S(2)}, u32[]{:S(2)}) collective-permute-start(bf16[24,6912]{1,0:T(8,128)(2,1)S(1)} %get-tuple-element.113), channel_id=1, source_target_pairs={{0,2},{1,3},{2,0},{3,1},{4,6},{5,7},{6,4},{7,5},{8,10},{9,11},{10,... | collective-permute-start | bytes 995336 | tf_op jit(solution)/shard_map/ppermute | solution.py:594
  500.3 18.2 %collective-permute-start.52 = (bf16[24,6912]{1,0:T(8,128)(2,1)S(1)}, bf16[24,6912]{1,0:T(8,128)(2,1)S(1)}, u32[]{:S(2)}, u32[]{:S(2)}) collective-permute-start(bf16[24,6912]{1,0:T(8,128)(2,1)S(1)} %get-tuple-element.112), channel_id=1, source_target_pairs={{0,1},{1,2},{2,3},{3,0},{4,5},{5,6},{6,7},{7,4},{8,9},{9,10},{10,1... | collective-permute-start | bytes 995336 | tf_op jit(solution)/shard_map/ppermute | solution.py:594
  500.3 18.3 %collective-permute-start.53 = (bf16[24,6912]{1,0:T(8,128)(2,1)S(1)}, bf16[24,6912]{1,0:T(8,128)(2,1)S(1)}, u32[]{:S(2)}, u32[]{:S(2)}) collective-permute-start(bf16[24,6912]{1,0:T(8,128)(2,1)S(1)} %get-tuple-element.111), channel_id=1, source_target_pairs={{0,3},{1,0},{2,1},{3,2},{4,7},{5,4},{6,5},{7,6},{8,11},{9,8},{10,9... | collective-permute-start | bytes 995336 | tf_op jit(solution)/shard_map/ppermute | solution.py:594
  518.9 12.7 %collective-permute-start.54 = (bf16[24,6912]{1,0:T(8,128)(2,1)S(1)}, bf16[24,6912]{1,0:T(8,128)(2,1)S(1)}, u32[]{:S(2)}, u32[]{:S(2)}) collective-permute-start(bf16[24,6912]{1,0:T(8,128)(2,1)S(1)} %reduce_sum.35), channel_id=1, source_target_pairs={{0,1},{1,2},{2,3},{3,0},{4,5},{5,6},{6,7},{7,4},{8,9},{9,10},{10,1... | collective-permute-start | bytes 995336 | tf_op jit(solution)/shard_map/ppermute | solution.py:631
  523.5 17.9 %collective-permute-start.55 = (bf16[24,6912]{1,0:T(8,128)(2,1)S(1)}, bf16[24,6912]{1,0:T(8,128)(2,1)S(1)}, u32[]{:S(2)}, u32[]{:S(2)}) collective-permute-start(bf16[24,6912]{1,0:T(8,128)(2,1)S(1)} %reduce_sum.35), channel_id=1, source_target_pairs={{0,2},{1,3},{2,0},{3,1},{4,6},{5,7},{6,4},{7,5},{8,10},{9,11},{10,... | collective-permute-start | bytes 995336 | tf_op jit(solution)/shard_map/ppermute | solution.py:631
  523.5 18.4 %collective-permute-start.56 = (bf16[24,6912]{1,0:T(8,128)(2,1)S(1)}, bf16[24,6912]{1,0:T(8,128)(2,1)S(1)}, u32[]{:S(2)}, u32[]{:S(2)}) collective-permute-start(bf16[24,6912]{1,0:T(8,128)(2,1)S(1)} %reduce_sum.35), channel_id=1, source_target_pairs={{0,3},{1,0},{2,1},{3,2},{4,7},{5,4},{6,5},{7,6},{8,11},{9,8},{10,9... | collective-permute-start | bytes 995336 | tf_op jit(solution)/shard_map/ppermute | solution.py:631
  (47 other events, 790.5 us)

commit v2 on v1

--- a/solution.py
+++ b/solution.py
@@ -30,6 +30,10 @@
 
 def whole(shape):
     return pl.BlockSpec(shape, lambda *_: (0,) * len(shape))
+
+
+def once(shape):
+    return pl.BlockSpec(shape, lambda *_: (0,) * len(shape), pipeline_mode=pl.Buffered(1))
 
 
 SMEM = pl.BlockSpec(memory_space=pltpu.SMEM)
@@ -147,17 +151,19 @@
     total_ref[0] = jnp.concatenate(totals, axis=0)
 
 
-def attention_forward(proj, seg_row, seg_column, tile=256):
+def attention_forward(proj, seg_row, seg_column, part, parts, tile=256):
     tokens, width = proj.shape
-    features = width // 3
-    pairs = features // PAIR
+    every = width // 3 // PAIR
+    pairs = every // parts
+    features = pairs * PAIR
+    base = part * pairs
     return pl.pallas_call(
         attention_forward_kernel,
         grid=(pairs, tokens // tile),
         in_specs=[
-            pl.BlockSpec((tile, PAIR), lambda h, i: (i, h)),
-            pl.BlockSpec((tokens, PAIR), lambda h, i: (0, pairs + h)),
-            pl.BlockSpec((tokens, PAIR), lambda h, i: (0, 2 * pairs + h)),
+            pl.BlockSpec((tile, PAIR), lambda h, i: (i, base + h)),
+            pl.BlockSpec((tokens, PAIR), lambda h, i: (0, every + base + h)),
+            pl.BlockSpec((tokens, PAIR), lambda h, i: (0, 2 * every + base + h)),
             pl.BlockSpec((1, tile), lambda h, i: (0, i)),
             whole((tokens, 1)),
         ],
@@ -211,19 +217,21 @@
         dv_ref[...] = dv_sum[...].astype(BF16)
 
 
-def attention_backward(proj, grad_mixed, seg_row, seg_column, totals, tile=256):
+def attention_backward(proj, grad_mixed, seg_row, seg_column, totals, part, parts, tile=256):
     tokens, width = proj.shape
-    features = width // 3
-    pairs = features // PAIR
+    every = width // 3 // PAIR
+    pairs = every // parts
+    features = pairs * PAIR
+    base = part * pairs
     q_tiles = tokens // tile
     return pl.pallas_call(
         functools.partial(attention_backward_kernel, q_tiles),
         grid=(pairs, q_tiles),
         in_specs=[
-            pl.BlockSpec((tile, PAIR), lambda h, i: (i, h)),
-            pl.BlockSpec((tokens, PAIR), lambda h, i: (0, pairs + h)),
-            pl.BlockSpec((tokens, PAIR), lambda h, i: (0, 2 * pairs + h)),
-            pl.BlockSpec((tile, PAIR), lambda h, i: (i, h)),
+            pl.BlockSpec((tile, PAIR), lambda h, i: (i, base + h)),
+            pl.BlockSpec((tokens, PAIR), lambda h, i: (0, every + base + h)),
+            pl.BlockSpec((tokens, PAIR), lambda h, i: (0, 2 * every + base + h)),
+            pl.BlockSpec((tile, PAIR), lambda h, i: (i, base + h)),
             pl.BlockSpec((1, tile), lambda h, i: (0, i)),
             whole((tokens, 1)),
             pl.BlockSpec((1, 8, tile), lambda h, i: (h, 0, i)),
@@ -245,7 +253,7 @@
     )(proj, proj, proj, grad_mixed, seg_row, seg_column, totals)
 
 
-def middle_kernel(rows, images, place_ref, flags_ref, mixed_ref, x_ref, cot_ref, seg_ref, bias_ref, gain_ref, shift_ref, *refs):
+def middle_kernel(rows, images, place_ref, flags_ref, mixed0_ref, mixed1_ref, x_ref, cot_ref, seg_ref, bias_ref, gain_ref, shift_ref, *refs):
     pieces = refs[:VIRTUAL]
     middle_ref, normed_ref, normed_t_ref, grad_ref, weight_ref, sems = refs[VIRTUAL:]
     features = x_ref.shape[1]
@@ -267,7 +275,8 @@
         for copy in copies:
             copy.wait()
 
-    branch = dot_nn(mixed_ref[...], weight_ref[...]) + bias_ref[...]
+    half = features // 2
+    branch = dot_nn(mixed0_ref[...], weight_ref[:half]) + dot_nn(mixed1_ref[...], weight_ref[half:]) + bias_ref[...]
     segment = seg_ref[...]
     middle = x_ref[...].astype(F32) + branch_scale(segment, flags_ref, 0, images) * branch
     middle_ref[...] = middle
@@ -283,10 +292,11 @@
     tokens, features = x.shape
     images = flags.shape[0] // 2
     row_block = pl.BlockSpec((tile, features), lambda t: (t, 0))
+    half_block = pl.BlockSpec((tile, features // 2), lambda t: (t, 0))
     return pl.pallas_call(
         functools.partial(middle_kernel, rows, images),
         grid=(tokens // tile,),
-        in_specs=[SMEM, SMEM, row_block, row_block, row_block, pl.BlockSpec((tile, 1), lambda t: (t, 0))]
+        in_specs=[SMEM, SMEM, half_block, half_block, row_block, row_block, pl.BlockSpec((tile, 1), lambda t: (t, 0))]
         + [whole((1, features))] * 3
         + [ANY] * VIRTUAL,
         out_specs=[
@@ -309,7 +319,7 @@
             flops=2 * tokens * features * features, bytes_accessed=16 << 20, transcendentals=0
         ),
         name="middle_forward",
-    )(place, flags, mixed, x, cot, seg_column, bias, gain, shift, *pieces)
+    )(place, flags, *mixed, x, cot, seg_column, bias, gain, shift, *pieces)
 
 
 def split_shards(rows, place, source_ref, keep_ref, send_ref):
@@ -325,10 +335,12 @@
 root_two_pi_inverse = 0.3989422804014327
 
 
-def mlp_kernel(rows, tiles, block, place_ref, normed_ref, normed_t_ref, g_ref, bias_ref, *refs):
+def mlp_kernel(
+    rows, tiles, block, images, place_ref, flags_ref, normed_ref, normed_t_ref, g_ref, middle_ref, seg_ref, bias_out_ref, bias_ref, *refs
+):
     pieces = refs[:VIRTUAL]
     (out_ref, gn_ref, keep1_ref, send1_ref, keep2_ref, send2_ref, db_ref) = refs[VIRTUAL : VIRTUAL + 7]
-    w1_s, w2_s, act_s, gp_s, dw_s, sems = refs[VIRTUAL + 7 :]
+    w1_s, w2_s, act_s, gp_s, dw_s, branch_s, sems = refs[VIRTUAL + 7 :]
     f = pl.program_id(0)
     place = place_ref[0]
     tokens, features = normed_ref.shape
@@ -380,13 +392,18 @@
 
         @pl.when(f == 0)
         def _():
-            out_ref[part, :] = out
+            branch_s[part, :] = out
             gn_ref[part, :] = gn
 
         @pl.when(f > 0)
         def _():
-            out_ref[part, :] += out
+            branch_s[part, :] += out
             gn_ref[part, :] += gn
+
+    @pl.when(f == pl.num_programs(0) - 1)
+    def _():
+        scale = branch_scale(seg_ref[...], flags_ref, images, images)
+        out_ref[...] = (middle_ref[...] + scale * (branch_s[...] + bias_out_ref[...])).astype(BF16)
 
     db_ref[...] = db
     dw_s[...] = dot_nn(normed_t_ref[...], gp_s[...]).astype(BF16)
@@ -401,7 +418,7 @@
         send2_ref[slot, :, columns] = dw_s[pl.ds(leave, rows), :]
 
 
-def mlp(place, normed, normed_t, grads, bias, pieces, rows, tiles=4):
+def mlp(place, flags, normed, normed_t, grads, middle, seg_column, bias_out, bias, pieces, rows, tiles=4):
     tokens, features = normed.shape
     hidden = bias.shape[1]
     parts = hidden // features
@@ -410,14 +427,19 @@
     half = VIRTUAL // 2
     columns = pl.BlockSpec((half, rows, block), lambda f: (0, 0, f))
     shards = jax.ShapeDtypeStruct((half, rows, hidden), BF16)
+    images = flags.shape[0] // 2
     return pl.pallas_call(
-        functools.partial(mlp_kernel, rows, tiles, block),
+        functools.partial(mlp_kernel, rows, tiles, block, images),
         grid=(hidden // block,),
         in_specs=[
             SMEM,
-            whole((tokens, features)),
-            whole((features, tokens)),
-            whole((tokens, features)),
+            SMEM,
+            once((tokens, features)),
+            once((features, tokens)),
+            once((tokens, features)),
+            once((tokens, features)),
+            once((tokens, 1)),
+            whole((1, features)),
             pl.BlockSpec((1, block), lambda f: (0, f)),
         ]
         + [ANY] * VIRTUAL,
@@ -430,7 +452,7 @@
             whole((half, rows, hidden)),
             pl.BlockSpec((1, block), lambda f: (0, f)),
         ],
-        out_shape=[jax.ShapeDtypeStruct((tokens, features), F32)] * 2
+        out_shape=[jax.ShapeDtypeStruct((tokens, features), BF16), jax.ShapeDtypeStruct((tokens, features), F32)]
         + [shards] * 4
         + [jax.ShapeDtypeStruct((1, hidden), F32)],
         scratch_shapes=[
@@ -439,6 +461,7 @@
             pltpu.VMEM((tokens, block), BF16),
             pltpu.VMEM((tokens, block), BF16),
             pltpu.VMEM((features, block), BF16),
+            pltpu.VMEM((tokens, features), F32),
             pltpu.SemaphoreType.DMA((1 + parts, VIRTUAL)),
         ],
         compiler_params=pltpu.CompilerParams(vmem_limit_bytes=62 << 20),
@@ -448,12 +471,12 @@
             transcendentals=2 * tokens * hidden,
         ),
         name="mlp",
-    )(place, normed, normed_t, grads, bias, *pieces)
+    )(place, flags, normed, normed_t, grads, middle, seg_column, bias_out, bias, *pieces)
 
 
 def output_backward_kernel(
-    rows, images, steps, place_ref, flags_ref, middle_ref, gn_ref, branch_ref, cot_ref, mixed_ref, seg_ref,
-    gain_ref, bias_ref, weight_ref, out_ref, gm_ref, gx_ref, keep_ref, send_ref, sums_ref, dw_sum, dw_s,
+    rows, images, steps, place_ref, flags_ref, middle_ref, gn_ref, cot_ref, mixed0_ref, mixed1_ref, seg_ref,
+    gain_ref, weight_ref, gm_ref, gx_ref, keep_ref, send_ref, sums_ref, dw_sum, dw_s,
 ):
     step = pl.program_id(0)
     segment = seg_ref[...]
@@ -461,7 +484,6 @@
     mlp_scale = branch_scale(segment, flags_ref, images, images)
     middle = middle_ref[...]
     cot = cot_ref[...].astype(F32)
-    out_ref[...] = (middle + mlp_scale * (branch_ref[...] + bias_ref[...])).astype(BF16)
     grad_b = (mlp_scale * cot).astype(BF16)
     gn = gn_ref[...]
     normal, inverse = norm_parts(middle)
@@ -469,7 +491,9 @@
     gm_ref[...] = grad_middle
     grad_a = (attn_scale * grad_middle).astype(BF16)
     gx_ref[...] = dot_nt(grad_a, weight_ref[...]).astype(BF16)
-    accumulate(step, dw_sum, dot_tn(mixed_ref[...], grad_a))
+    half = mixed0_ref.shape[1]
+    accumulate(step, dw_sum.at[:half], dot_tn(mixed0_ref[...], grad_a))
+    accumulate(step, dw_sum.at[half:], dot_tn(mixed1_ref[...], grad_a))
     total = lambda v: jnp.sum(v, axis=0, keepdims=True)
     sums = [total(gn * normal), total(gn), total(grad_a.astype(F32)), total(grad_b.astype(F32))]
     accumulate(step, sums_ref, jnp.concatenate(sums + [jnp.zeros((4,) + sums[0].shape[1:], F32)], axis=0))
@@ -480,22 +504,23 @@
         split_shards(rows, place_ref[0], dw_s, keep_ref, send_ref)
 
 
-def output_backward(place, flags, middle, gn, branch, cot, mixed, seg_column, gain, bias, weight, rows, tile=256):
+def output_backward(place, flags, middle, gn, cot, mixed, seg_column, gain, weight, rows, tile=256):
     tokens, features = middle.shape
     images = flags.shape[0] // 2
     half = VIRTUAL // 2
     steps = tokens // tile
     row_block = pl.BlockSpec((tile, features), lambda t: (t, 0))
+    half_block = pl.BlockSpec((tile, features // 2), lambda t: (t, 0))
     shards = jax.ShapeDtypeStruct((half, rows, features), BF16)
     return pl.pallas_call(
         functools.partial(output_backward_kernel, rows, images, steps),
         grid=(steps,),
         in_specs=[SMEM, SMEM]
-        + [row_block] * 5
-        + [pl.BlockSpec((tile, 1), lambda t: (t, 0)), whole((1, features)), whole((1, features)), whole((features, features))],
-        out_specs=[row_block, row_block, row_block, whole((half, rows, features)), whole((half, rows, features)), whole((8, features))],
+        + [row_block] * 3
+        + [half_block] * 2
+        + [pl.BlockSpec((tile, 1), lambda t: (t, 0)), whole((1, features)), whole((features, features))],
+        out_specs=[row_block, row_block, whole((half, rows, features)), whole((half, rows, features)), whole((8, features))],
         out_shape=[
-            jax.ShapeDtypeStruct((tokens, features), BF16),
             jax.ShapeDtypeStruct((tokens, features), F32),
             jax.ShapeDtypeStruct((tokens, features), BF16),
             shards,
@@ -508,7 +533,7 @@
             flops=4 * tokens * features * features, bytes_accessed=22 << 20, transcendentals=0
         ),
         name="output_backward",
-    )(place, flags, middle, gn, branch, cot, mixed, seg_column, gain, bias, weight)
+    )(place, flags, middle, gn, cot, *mixed, seg_column, gain, weight)
 
 
 def joint_weight_kernel(rows, place_ref, normed_t_ref, dq_ref, dk_ref, dv_ref, keep_ref, send_ref, sums_ref, dw_s):
@@ -526,29 +551,35 @@
 
 def joint_weight_grad(place, normed_t, dq, dk, dv, rows):
     features, tokens = normed_t.shape
+    width = dq.shape[1]
     half = VIRTUAL // 2
-    columns = pl.BlockSpec((half, rows, features), lambda c: (0, 0, c))
-    shards = jax.ShapeDtypeStruct((half, rows, 3 * features), BF16)
+    columns = pl.BlockSpec((half, rows, width), lambda c: (0, 0, c))
+    shards = jax.ShapeDtypeStruct((half, rows, 3 * width), BF16)
     return pl.pallas_call(
         functools.partial(joint_weight_kernel, rows),
         grid=(3,),
-        in_specs=[SMEM, whole((features, tokens))] + [whole((tokens, features))] * 3,
-        out_specs=[columns, columns, pl.BlockSpec((1, features), lambda c: (0, c))],
-        out_shape=[shards, shards, jax.ShapeDtypeStruct((1, 3 * features), F32)],
-        scratch_shapes=[pltpu.VMEM((features, features), BF16)],
+        in_specs=[SMEM, whole((features, tokens))] + [whole((tokens, width))] * 3,
+        out_specs=[columns, columns, pl.BlockSpec((1, width), lambda c: (0, c))],
+        out_shape=[shards, shards, jax.ShapeDtypeStruct((1, 3 * width), F32)],
+        scratch_shapes=[pltpu.VMEM((features, width), BF16)],
         compiler_params=pltpu.CompilerParams(vmem_limit_bytes=48 << 20),
         cost_estimate=pl.CostEstimate(
-            flops=6 * tokens * features * features, bytes_accessed=10 << 20, transcendentals=0
+            flops=6 * tokens * features * width, bytes_accessed=6 << 20, transcendentals=0
         ),
         name="joint_weight_grad",
     )(place, normed_t, dq, dk, dv)
 
 
-def joint_backward_kernel(dq_ref, dk_ref, dv_ref, weight_ref, x_ref, gm_ref, gain_ref, gt_ref, sums_ref):
+def joint_backward_kernel(*refs):
+    grads = refs[:6]
+    weight_ref, x_ref, gm_ref, gain_ref, gt_ref, sums_ref = refs[6:]
     features = x_ref.shape[1]
-    gn = dot_nt(dq_ref[...], weight_ref[:, :features])
-    gn += dot_nt(dk_ref[...], weight_ref[:, features : 2 * features])
-    gn += dot_nt(dv_ref[...], weight_ref[:, 2 * features :])
+    width = features // 2
+    gn = jnp.zeros(x_ref.shape, F32)
+    for part in range(2):
+        for index in range(3):
+            start = index * features + part * width
+            gn += dot_nt(grads[3 * part + index][...], weight_ref[:, start : start + width])
     normal, inverse = norm_parts(x_ref[...].astype(F32))
     gt_ref[...] = (gm_ref[...] + norm_backward(normal, inverse, gn, gain_ref[...])).astype(BF16)
     total = lambda v: jnp.sum(v, axis=0, keepdims=True)
@@ -558,13 +589,14 @@
     )
 
 
-def joint_backward(dq, dk, dv, weight, x, gm, gain, tile=256):
+def joint_backward(grads, weight, x, gm, gain, tile=256):
     tokens, features = x.shape
     row_block = pl.BlockSpec((tile, features), lambda t: (t, 0))
+    half_block = pl.BlockSpec((tile, features // 2), lambda t: (t, 0))
     return pl.pallas_call(
         joint_backward_kernel,
         grid=(tokens // tile,),
-        in_specs=[row_block] * 3 + [whole((features, 3 * features)), row_block, row_block, whole((1, features))],
+        in_specs=[half_block] * 6 + [whole((features, 3 * features)), row_block, row_block, whole((1, features))],
         out_specs=[row_block, whole((8, features))],
         out_shape=[jax.ShapeDtypeStruct((tokens, features), BF16), jax.ShapeDtypeStruct((8, features), F32)],
         compiler_params=pltpu.CompilerParams(vmem_limit_bytes=48 << 20),
@@ -572,39 +604,43 @@
             flops=6 * tokens * features * features, bytes_accessed=15 << 20, transcendentals=0
         ),
         name="joint_backward",
-    )(dq, dk, dv, weight, x, gm, gain)
+    )(*grads, weight, x, gm, gain)
 
 
 def after(value, *others):
-    return lax.optimization_barrier((value,) + others)[0]
+    return lax.optimization_barrier((value, others))[0]
 
 
 def dp_swap(value, bit):
     return lax.ppermute(value, "dp", [(i, i ^ bit) for i in range(VIRTUAL)])
 
 
-def seq_exchange(value, parts):
+def pick(value, place, parts):
+    return lax.dynamic_index_in_dim(value, place % parts, 0, keepdims=False)
+
+
+def seq_send(value, parts):
     me = lax.axis_index("seq")
-
-    def block(place):
-        return lax.dynamic_index_in_dim(value, place % parts, 0, keepdims=False)
-
     order = sorted(range(1, parts), key=lambda k: abs(k - parts / 2))
-    got = [
-        (k, lax.ppermute(block(me + k), "seq", [(i, (i + k) % parts) for i in range(parts)]))
+    return [
+        (k, lax.ppermute(pick(value, me + k, parts), "seq", [(i, (i + k) % parts) for i in range(parts)]))
         for k in order
     ]
-    out = lax.dynamic_update_index_in_dim(jnp.zeros_like(value), block(me), me, 0)
+
+
+def seq_exchange(value, parts):
+    return seq_place(value, seq_send(value, parts), parts)
+
+
+def seq_place(value, got, parts):
+    me = lax.axis_index("seq")
+    out = lax.dynamic_update_index_in_dim(jnp.zeros_like(value), pick(value, me, parts), me, 0)
     for k, arrived in got:
         out = lax.dynamic_update_index_in_dim(out, arrived, (me - k) % parts, 0)
     return out
 
 
-def gather_shards(own, first):
-    far_x, far_y = dp_swap(own, 2), dp_swap(own, 4)
-    corner = dp_swap(far_x, 4) if first == 2 else dp_swap(far_y, 2)
-    mine = (own, far_x, far_y, corner)
-    other = [dp_swap(piece, 1) for piece in mine]
+def interleave(mine, other):
     return [piece for both in zip(mine, other) for piece in both]
 
 
@@ -612,25 +648,17 @@
     return left.astype(F32) + right.astype(F32)
 
 
-def scatter_rest(half, first):
-    if first == 2:
-        one = add(half[0::2], dp_swap(half[1::2], 2)).astype(BF16)
-        return add(one[0], dp_swap(one[1], 4))
-    one = add(half[:2], dp_swap(half[2:], 4)).astype(BF16)
-    return add(one[0], dp_swap(one[1], 2))
-
-
-def seq_sum(value, parts):
-    rows = value.shape[0] // parts
-    cut = value.astype(BF16).reshape(parts, rows, value.shape[1])
-    arrived = seq_exchange(cut, parts)
-    total = jnp.sum(arrived.astype(F32), axis=0).astype(BF16)
+def seq_move(value, moves):
+    return lax.ppermute(value, "seq", moves)
+
+
+def chain_sum(value):
+    value = value.astype(BF16)
+    inner = add(value, seq_move(value, [(0, 1), (3, 2)])).astype(BF16)
+    total = add(inner, seq_move(inner, [(1, 2), (2, 1)])).astype(BF16)
+    back = seq_move(total, [(1, 0), (2, 3)])
     me = lax.axis_index("seq")
-    out = lax.dynamic_update_index_in_dim(jnp.zeros_like(cut), total, me, 0)
-    for k in range(1, parts):
-        got = lax.ppermute(total, "seq", [(i, (i + k) % parts) for i in range(parts)])
-        out = lax.dynamic_update_index_in_dim(out, got, (me - k) % parts, 0)
-    return out.astype(F32).reshape(value.shape)
+    return jnp.where((me == 1) | (me == 2), total, back).astype(F32)
 
 
 def sum_everywhere(value, parts):
@@ -682,7 +710,7 @@
     rows = features // VIRTUAL
     me_seq = lax.axis_index("seq")
     me_dp = lax.axis_index("dp")
-    exact = ndp == VIRTUAL
+    exact = ndp == VIRTUAL and nseq == 4
 
     smalls = (first_gain, first_shift, joint_bias, output_bias, second_gain, second_shift, expand_bias, reduce_bias)
     widths = [s.shape[0] * ndp for s in smalls]
@@ -695,7 +723,9 @@
         width = 3 * features
         row = jnp.pad(row, (0, width - row.shape[0])).reshape(1, width)
         piece = jnp.concatenate([joint_weight.astype(BF16), jnp.pad(row, ((0, 15), (0, 0)))], axis=0)
-        joint_pieces = gather_shards(piece, 2)
+        near = (dp_swap(piece, 2), dp_swap(piece, 4))
+        own = [piece, near[0], near[1], dp_swap(near[0], 4)]
+        joint_pieces = interleave(own, [dp_swap(p, 1) for p in own])
         small_slots = jnp.stack([p[rows, : sum(w // ndp for w in widths)] for p in joint_pieces]).astype(F32)
         slot = lax.broadcasted_iota(jnp.int32, (VIRTUAL, VIRTUAL, 1), 1)
         home = lax.broadcasted_iota(jnp.int32, (VIRTUAL, VIRTUAL, 1), 0)
@@ -708,8 +738,9 @@
             [output_weight.astype(BF16), expand_weight.astype(BF16), pack_rows(reduce_weight.astype(BF16), rows)],
             axis=1,
         )
-        piece = after(piece, joint_pieces[2], joint_pieces[4])
-        rest_pieces = gather_shards(piece, 4)
+        piece = after(piece, joint_pieces)
+        own = [piece, dp_swap(piece, 2), dp_swap(piece, 4), dp_swap(piece, 6)]
+        rest_pieces = interleave(own, [dp_swap(p, 1) for p in own])
     else:
         place = jnp.zeros((1,), jnp.int32)
         full = lambda w: lax.all_gather(w.astype(BF16), "dp", axis=0, tiled=True)
@@ -739,43 +770,74 @@
     cot = seq_exchange(after(cotangent, x), nseq).reshape(row_len, features)
 
     proj, normed_a_t, weight_joint = joint_forward(place, x, gain_a, shift_a, bias_joint, joint_pieces, rows)
-    mixed, totals = attention_forward(proj, seg_row, seg_column)
+    first, totals_a = attention_forward(proj, seg_row, seg_column, 0, 2)
+    if exact:
+        proj_b = after(proj, first, own[1], own[2])
+    else:
+        proj_b = proj
+    second, totals_b = attention_forward(proj_b, seg_row, seg_column, 1, 2)
+    mixed = (first, second)
     middle, normed_b, normed_b_t, grad_b, weight_out = middle_forward(
         place, flags, mixed, x, cot, seg_column, bias_out, gain_b, shift_b, rest_pieces, rows
     )
-    branch, gn, keep_up, send_up, keep_down, send_down, g_bias_up = mlp(
-        place, normed_b, normed_b_t, grad_b, bias_up, rest_pieces, rows
+    output, gn, keep_up, send_up, keep_down, send_down, g_bias_up = mlp(
+        place, flags, normed_b, normed_b_t, grad_b, middle, seg_column, bias_down, bias_up, rest_pieces, rows
     )
-    output, grad_middle, grad_mixed, keep_out, send_out, sums_b = output_backward(
-        place, flags, middle, gn, branch, cot, mixed, seg_column, gain_b, bias_down, weight_out, rows
+    blocks_out = output.reshape(nseq, shard_len, features)
+    sent_out = seq_send(blocks_out, nseq)
+    if exact:
+        moved_up, moved_down = dp_swap(send_up, 1), dp_swap(send_down, 1)
+    grad_middle, grad_mixed, keep_out, send_out, sums_b = output_backward(
+        place, flags, middle, gn, cot, mixed, seg_column, gain_b, weight_out, rows
     )
-    dq, dk, dv = attention_backward(proj, grad_mixed, seg_row, seg_column, totals)
-    keep_joint, send_joint, sums_joint = joint_weight_grad(place, normed_a_t, dq, dk, dv, rows)
-    grad_in, sums_a = joint_backward(dq, dk, dv, weight_joint, x, grad_middle, gain_a)
-
-    output = seq_exchange(output.reshape(nseq, shard_len, features), nseq)
+    early = jnp.concatenate([sums_b[2], sums_b[0], sums_b[1], g_bias_up[0], sums_b[3]])
+    if exact:
+        half_up = add(keep_up, moved_up).astype(BF16)
+        half_down = add(keep_down, moved_down).astype(BF16)
+        grad_mixed = after(grad_mixed, half_up, half_down)
+        far_up, far_down = dp_swap(half_up[1::2], 2), dp_swap(half_down[2:], 4)
+    grads_a = attention_backward(proj, grad_mixed, seg_row, seg_column, totals_a, 0, 2)
+    keep_a, send_a, sums_joint_a = joint_weight_grad(place, normed_a_t, *grads_a, rows)
+    if exact:
+        one_up = add(half_up[0::2], far_up).astype(BF16)
+        one_down = add(half_down[:2], far_down).astype(BF16)
+        grad_mixed = after(grad_mixed, keep_a, one_up, one_down, sent_out)
+        far_up, far_down = dp_swap(one_up[1], 4), dp_swap(one_down[1], 2)
+        send_a = jnp.concatenate([send_a, send_out], axis=2)
+        moved_a = dp_swap(send_a, 1)
+    grads_b = attention_backward(proj, grad_mixed, seg_row, seg_column, totals_b, 1, 2)
+    keep_b, send_b, sums_joint_b = joint_weight_grad(place, normed_a_t, *grads_b, rows)
+    grads = grads_a + grads_b
+    if exact:
+        up = add(one_up[0], far_up)
+        down = add(one_down[0], far_down)
+        half_a = add(jnp.concatenate([keep_a, keep_out], axis=2), moved_a).astype(BF16)
+        send_b = after(send_b, up, down, half_a)
+        moved_b = dp_swap(send_b, 1)
+        far_a = dp_swap(half_a[1::2], 2)
+    grad_in, sums_a = joint_backward(grads, weight_joint, x, grad_middle, gain_a)
+
+    output = seq_place(blocks_out, sent_out, nseq)
     grad_tokens = seq_exchange(grad_in.reshape(nseq, shard_len, features), nseq).astype(F32)
 
-    late = jnp.concatenate([sums_a[0], sums_a[1], sums_joint[0, :features], sums_joint[0, 2 * features :]])
-    early = jnp.concatenate([sums_b[2], sums_b[0], sums_b[1], g_bias_up[0], sums_b[3]])
+    width = features // 2
+    sums_joint = [s[0, index * width : (index + 1) * width] for index in (0, 2) for s in (sums_joint_a, sums_joint_b)]
+    late = jnp.concatenate([sums_a[0], sums_a[1]] + sums_joint)
     if exact:
         early = sum_everywhere(early.reshape(-1, 128), nseq).reshape(-1)
         late = sum_everywhere(late.reshape(-1, 128), nseq).reshape(-1)
-        half_up = add(keep_up, dp_swap(send_up, 1)).astype(BF16)
-        half_down = add(keep_down, dp_swap(send_down, 1)).astype(BF16)
-        half_out = add(keep_out, dp_swap(send_out, 1)).astype(BF16)
-        first = jnp.concatenate(
-            [scatter_rest(half_up, 2), scatter_rest(half_down, 4), scatter_rest(half_out, 2)], axis=1
-        )
-        first = seq_sum(first, nseq)
+        first = chain_sum(jnp.concatenate([up, down], axis=1))
         g_up = first[:, :hidden]
-        g_down = unpack_rows(first[:, hidden : 2 * hidden], features)
-        g_out = first[:, 2 * hidden :]
-        arrived = dp_swap(send_joint, 1)
-        cut = 3 * features // 2
-        half_a = add(keep_joint[:, :, :cut], arrived[:, :, :cut]).astype(BF16)
-        half_b = add(keep_joint[:, :, cut:], arrived[:, :, cut:]).astype(BF16)
-        g_joint = seq_sum(jnp.concatenate([scatter_rest(half_a, 2), scatter_rest(half_b, 4)], axis=1), nseq)
+        g_down = unpack_rows(first[:, hidden:], features)
+        half_b = add(keep_b, moved_b).astype(BF16)
+        one_a = add(half_a[0::2], far_a).astype(BF16)
+        part_a = add(one_a[0], dp_swap(one_a[1], 4))
+        one_b = add(half_b[:2], dp_swap(half_b[2:], 4)).astype(BF16)
+        part_b = add(one_b[0], dp_swap(one_b[1], 2))
+        last = chain_sum(jnp.concatenate([part_a, part_b], axis=1))
+        g_out = last[:, 3 * width : 3 * width + features]
+        blocks = [last[:, c * width : (c + 1) * width] for c in (0, 5, 1, 6, 2, 7)]
+        g_joint = jnp.concatenate(blocks, axis=1)
     else:
         early, late = lax.psum((early, late), ("dp", "seq"))
 
@@ -788,7 +850,9 @@
 
         g_up = reduce(total(keep_up, send_up))
         g_out = reduce(total(keep_out, send_out))
-        g_joint = reduce(total(keep_joint, send_joint))
+        joint_a, joint_b = total(keep_a, send_a), total(keep_b, send_b)
+        blocks = [j[:, c * width : (c + 1) * width] for c in range(3) for j in (joint_a, joint_b)]
+        g_joint = reduce(jnp.concatenate(blocks, axis=1))
         down = jnp.stack([keep_down, send_down], axis=1).reshape(VIRTUAL, rows, hidden)
         g_down = reduce(jnp.concatenate([unpack_rows(down[k], features) for k in range(VIRTUAL)], axis=0))
 

time: 552 us -> 566 us (1.025)
  starting transfers between devices: 69.2 us -> 53.2 us
  local copies, waits for them, and re-layouts: 36.2 us -> 45.4 us
  waiting for transfers between devices: 226 us -> 235 us
  other arithmetic: 18.5 us -> 24.6 us
    ppermute x34 -> x32, waiting for transfers between devices: 75.6 us -> 91.2 us  [dp_swap(): return lax.ppermute(value, 'dp', [(i, i ^ bit) for i in range(VIRTUAL)])]
    ppermute x24 -> x18, starting transfers between devices: 38.9 us -> 23.5 us  [the longest x12 13.6 us: seq_send(): lax.ppermute(pick(value, me + k, parts), 'seq', [(i, (i + k) % parts) for...]
    dynamic_update_slice x26 -> x12, local copies, waits for them, and re-layouts: 4.86 us -> 12.2 us  [seq_place(): out = lax.dynamic_update_index_in_dim(out, arrived, (me - k) % parts, 0)]
    convert_element_type x9 -> x14, other arithmetic: 6.25 us -> 12.5 us  [the longest x1 2.69 us: shards(): one_up = add(half_up[0::2], far_up).astype(BF16)]
    ppermute x24 -> x18, waiting for transfers between devices: 125 us -> 122 us  [the longest x6 67.5 us: seq_move(): return lax.ppermute(value, 'seq', moves)]
    pallas_call x1 -> x2, Pallas kernels: 51.9 us -> 53.9 us  [attention_backward(): pl.pallas_call(functools.partial(attention_backward_kernel, q_tiles), gri...]
    unnamed x105 -> x113, local copies, waits for them, and re-layouts: 17.4 us -> 16 us
    pallas_call x1 -> x2, Pallas kernels: 47.4 us -> 46.9 us  [attention_forward(): pl.pallas_call(attention_forward_kernel, grid=(pairs, tokens // tile), in...]
  transfers between devices with their start and end apart: 62 -> 54, of which waited for: 34 -> 27; matrix products, arithmetic and copies ran while one was open for 5% -> 8% of each run, Pallas kernels for 25% -> 18%
where the time goes in v2:
time: 566 us; the launch traced here: 558 us
  waiting for transfers between devices  235 us (42%)
  Pallas kernels  197 us (35%)
  starting transfers between devices  53.2 us (9%)
  local copies, waits for them, and re-layouts  45.4 us (8%)
  other arithmetic  24.6 us (4%)
    ppermute x32, waiting for transfers between devices, dp_swap(): return lax.ppermute(value, 'dp', [(i, i ^ bit) for i in range(VIRTUAL)])  91.2 us
    ppermute x6, waiting for transfers between devices, seq_move(): return lax.ppermute(value, 'seq', moves)  67.5 us
    ppermute x12, waiting for transfers between devices, seq_send(): lax.ppermute(pick(value, me + k, parts), 'seq', [(i, (i + k) % parts) for...  54.4 us
    pallas_call x2, Pallas kernels, attention_backward(): pl.pallas_call(functools.partial(attention_backward_kernel, q_tiles), gri...  53.9 us
    pallas_call x1, Pallas kernels, mlp(): pl.pallas_call(functools.partial(mlp_kernel, rows, tiles, block, images),...  48 us
    pallas_call x2, Pallas kernels, attention_forward(): pl.pallas_call(attention_forward_kernel, grid=(pairs, tokens // tile), in...  46.9 us
    ppermute x32, starting transfers between devices, dp_swap(): return lax.ppermute(value, 'dp', [(i, i ^ bit) for i in range(VIRTUAL)])  23 us
    ppermute x4, waiting for transfers between devices, sum_everywhere(): lax.ppermute(value, 'seq', [(i, i ^ bit) for i in range(parts)])  21.8 us
  transfers between devices with their start and end apart: 54, of which 27 were waited for; matrix products, arithmetic and copies ran while one was open for 8% of the time, Pallas kernels for 18%

profile of v2, /device:TPU:0, one launch (start us, length us, event | category | flops | bytes accessed | tf_op | source)
XLA Modules:
  0.0 557.5 jit_solution(17867928600565026768)
XLA Ops:
  7.4 3.0 collective-permute-start.4
  10.4 1.5 collective-permute-start.6
  12.9 2.6 collective-permute-start
  15.5 1.6 collective-permute-start.1
  17.5 25.1 %collective-permute-done = bf16[256,768]{1,0:T(8,128)(2,1)} collective-permute-done((bf16[256,768]{1,0:T(8,128)(2,1)}, bf16[256,768]{1,0:T(8,128)(2,1)}, u32[]{:S(2)}, u32[]{:S(2)}) %collective-permute-start) | collective-permute-done | bytes 393248 | tf_op jit(solution)/shard_map/ppermute | solution.py:626
  42.5 1.8 bitcast_dynamic-update-slice_fusion.11
  44.3 1.9 bitcast_dynamic-update-slice_fusion.10
  46.2 7.0 %collective-permute-done.2 = bf16[256,768]{1,0:T(8,128)(2,1)S(1)} collective-permute-done((bf16[256,768]{1,0:T(8,128)(2,1)S(1)}, bf16[256,768]{1,0:T(8,128)(2,1)S(1)}, u32[]{:S(2)}, u32[]{:S(2)}) %collective-permute-start.2) | collective-permute-done | bytes 393248 | tf_op jit(solution)/shard_map/ppermute | solution.py:626
  55.7 2.7 collective-permute-start.13
  59.0 7.5 %collective-permute-done.8.refs_6_ = bf16[112,2304]{1,0:T(8,128)(2,1)} collective-permute-done((bf16[112,2304]{1,0:T(8,128)(2,1)S(1)}, bf16[112,2304]{1,0:T(8,128)(2,1)}, u32[]{:S(2)}, u32[]{:S(2)}) %collective-permute-start.8) | collective-permute-done | bytes 516128 | tf_op jit(solution)/shard_map/ppermute | solution.py:615
  69.0 13.9 %collective-permute-done.12 = bf16[256,768]{1,0:T(8,128)(2,1)} collective-permute-done((bf16[256,768]{1,0:T(8,128)(2,1)}, bf16[256,768]{1,0:T(8,128)(2,1)}, u32[]{:S(2)}, u32[]{:S(2)}) %collective-permute-start.12) | collective-permute-done | bytes 393248 | tf_op jit(solution)/shard_map/ppermute | solution.py:626
  82.9 1.8 bitcast_dynamic-update-slice_fusion.8
  84.7 1.8 bitcast_dynamic-update-slice_fusion.7
  86.9 1.7 collective-permute-start.11
  88.6 1.4 collective-permute-start.18
  90.0 3.9 collective-permute-done.14
  99.2 10.7 %joint_forward.1 = (bf16[1024,2304]{1,0:T(8,128)(2,1)}, bf16[768,1024]{1,0:T(8,128)(2,1)S(1)}, bf16[768,2304]{1,0:T(8,128)(2,1)}) custom-call(s32[1]{0:T(128)} %bitcast.place_ref, bf16[1024,768]{1,0:T(8,128)(2,1)} %bitcast.108, f32[1,768]{1,0:T(1,128)S(1)} %reshape.173.gain_ref.refs_9_, f32[1,768]{1,0:T(1,128)S(1)} %reshape.174.shift_ref, ...), custom_call_target="tpu_custom_call" | custom-call | flops 3623878656 | bytes 14680064 | tf_op jit(solution)/shard_map/joint_forward/pallas_call | solution.py:103
  110.0 1.2 copy-done.19
  111.2 7.4 %collective-permute-done.10.refs_2_ = bf16[96,6912]{1,0:T(8,128)(2,1)} collective-permute-done((bf16[96,6912]{1,0:T(8,128)(2,1)S(1)}, bf16[96,6912]{1,0:T(8,128)(2,1)}, u32[]{:S(2)}, u32[]{:S(2)}) %collective-permute-start.10) | collective-permute-done | bytes 1327136 | tf_op jit(solution)/shard_map/ppermute | solution.py:615
  118.6 26.7 %collective-permute-done.11.refs_4_ = bf16[96,6912]{1,0:T(8,128)(2,1)} collective-permute-done((bf16[96,6912]{1,0:T(8,128)(2,1)S(1)}, bf16[96,6912]{1,0:T(8,128)(2,1)}, u32[]{:S(2)}, u32[]{:S(2)}) %collective-permute-start.11) | collective-permute-done | bytes 1327136 | tf_op jit(solution)/shard_map/ppermute | solution.py:615
  145.4 1.7 collective-permute-done.18.refs_6_
  147.8 2.3 copy-done.21
  150.1 23.4 %attention_forward.2 = (bf16[1024,384]{1,0:T(8,128)(2,1)S(1)}, f32[3,8,1024]{2,1,0:T(8,128)S(1)}) custom-call(bf16[1024,2304]{1,0:T(8,128)(2,1)S(1)} %copy-done.21, bf16[1024,2304]{1,0:T(8,128)(2,1)S(1)} %copy-done.21, bf16[1024,2304]{1,0:T(8,128)(2,1)S(1)} %copy-done.21, s32[1,1024]{1,0:T(1,128)S(1)} %constant_dynamic-slice_fusion.segq_ref, ...), custom_call_target="tpu_custom_call" | custom-call | flops 6442450944 | bytes 8388608 | tf_op jit(solution)/shard_map/attention_forward/pallas_call | solution.py:160
  174.2 23.5 %attention_forward.3 = (bf16[1024,384]{1,0:T(8,128)(2,1)S(1)}, f32[3,8,1024]{2,1,0:T(8,128)S(1)}) custom-call(bf16[1024,2304]{1,0:T(8,128)(2,1)S(1)} %copy-done.21, bf16[1024,2304]{1,0:T(8,128)(2,1)S(1)} %copy-done.21, bf16[1024,2304]{1,0:T(8,128)(2,1)S(1)} %copy-done.21, s32[1,1024]{1,0:T(1,128)S(1)} %constant_dynamic-slice_fusion.segq_ref, ...), custom_call_target="tpu_custom_call" | custom-call | flops 6442450944 | bytes 8388608 | tf_op jit(solution)/shard_map/attention_forward/pallas_call | solution.py:160
  199.7 8.1 %middle_forward.1 = (f32[1024,768]{1,0:T(8,128)}, bf16[1024,768]{1,0:T(8,128)(2,1)}, bf16[768,1024]{1,0:T(8,128)(2,1)}, bf16[1024,768]{1,0:T(8,128)(2,1)}, bf16[768,768]{1,0:T(8,128)(2,1)S(1)}) custom-call(s32[1]{0:T(128)} %bitcast.place_ref, s32[8]{0:T(128)S(1)} %fusion.5.flags_ref, bf16[1024,384]{1,0:T(8,128)(2,1)S(1)} %get-tuple-element.59.mixed0_ref, ...), custom_call_target="tpu_custom_call" | custom-call | flops 1207959552 | bytes 16777216 | tf_op jit(solution)/shard_map/middle_forward/pallas_call | solution.py:296
  208.8 48.0 %mlp.1 = (bf16[1024,768]{1,0:T(8,128)(2,1)}, f32[1024,768]{1,0:T(8,128)}, bf16[4,96,3072]{2,1,0:T(8,128)(2,1)}, bf16[4,96,3072]{2,1,0:T(8,128)(2,1)}, bf16[4,96,...) custom-call(s32[1]{0:T(128)} %bitcast.place_ref, s32[8]{0:T(128)} %copy-done.9, ...), custom_call_target="tpu_custom_call" | custom-call | flops 28991029248 | bytes 31457280 | tf_op jit(solution)/shard_map/mlp/pallas_call | solution.py:431
  257.4 12.6 %output_backward.1 = (f32[1024,768]{1,0:T(8,128)}, bf16[1024,768]{1,0:T(8,128)(2,1)}, bf16[4,96,768]{2,1,0:T(8,128)(2,1)}, bf16[4,96,768]{2,1,0:T(8,128)(2,1)}, f32[8,768]{1,0:T(8,128)}) custom-call(s32[1]{0:T(128)} %bitcast.place_ref, s32[8]{0:T(128)} %copy-done.9, f32[1024,768]{1,0:T(8,128)} %get-tuple-element.67.middle_ref, ...), custom_call_target="tpu_custom_call" | custom-call | flops 2415919104 | bytes 23068672 | tf_op jit(solution)/shard_map/output_backward/pallas_call | solution.py:515
  273.3 2.8 collective-permute-done.47
  278.5 1.5 collective-permute-done.48
  280.0 1.7 collective-permute-start.49
  281.8 5.1 collective-permute-done.49
  287.4 4.8 collective-permute-start.50
  292.3 15.8 %collective-permute-done.50 = f32[48,128]{1,0:T(8,128)} collective-permute-done((f32[48,128]{1,0:T(8,128)}, f32[48,128]{1,0:T(8,128)}, u32[]{:S(2)}, u32[]{:S(2)}) %collective-permute-start.50) | collective-permute-done | bytes 24608 | tf_op jit(solution)/shard_map/ppermute | solution.py:671
  310.2 1.8 bitcast_dynamic-update-slice_fusion.5
  312.7 4.5 collective-permute-done.22
  318.0 2.5 add_convert_fusion.1
  321.6 1.5 collective-permute-start.25
  323.1 2.6 add_convert_fusion
  327.3 27.1 %attention_backward.2 = (bf16[1024,384]{1,0:T(8,128)(2,1)}, bf16[1024,384]{1,0:T(8,128)(2,1)}, bf16[1024,384]{1,0:T(8,128)(2,1)}) custom-call(bf16[1024,2304]{1,0:T(8,128)(2,1)} %get-tuple-element.61.q_ref.k_ref.v_ref, bf16[1024,2304]{1,0:T(8,128)(2,1)} %get-tuple-element.61.q_ref.k_ref.v_ref, bf16[1024,2304]{1,0:T(8,128)(2,1)} %get-tuple-element.61.q_ref.k_ref.v_ref, ...), custom_call_target="tpu_custom_call" | custom-call | flops 9663676416 | bytes 14680064 | tf_op jit(solution)/shard_map/attention_backward/pallas_call | solution.py:227
  357.8 3.4 joint_weight_grad.2
  361.3 2.7 add_convert_fusion.6
  363.9 2.7 add_convert_fusion.5
  366.6 26.8 %attention_backward.3 = (bf16[1024,384]{1,0:T(8,128)(2,1)}, bf16[1024,384]{1,0:T(8,128)(2,1)}, bf16[1024,384]{1,0:T(8,128)(2,1)}) custom-call(bf16[1024,2304]{1,0:T(8,128)(2,1)} %get-tuple-element.61.q_ref.k_ref.v_ref, bf16[1024,2304]{1,0:T(8,128)(2,1)} %get-tuple-element.61.q_ref.k_ref.v_ref, bf16[1024,2304]{1,0:T(8,128)(2,1)} %get-tuple-element.61.q_ref.k_ref.v_ref, ...), custom_call_target="tpu_custom_call" | custom-call | flops 9663676416 | bytes 14680064 | tf_op jit(solution)/shard_map/attention_backward/pallas_call | solution.py:227
  396.9 3.4 joint_weight_grad.3
  400.3 10.1 %joint_backward.1 = (bf16[1024,768]{1,0:T(8,128)(2,1)}, f32[8,768]{1,0:T(8,128)S(1)}) custom-call(bf16[1024,384]{1,0:T(8,128)(2,1)S(1)} %copy-done.11, bf16[1024,384]{1,0:T(8,128)(2,1)S(1)} %copy-done.13, bf16[1024,384]{1,0:T(8,128)(2,1)S(1)} %copy-done.15, bf16[1024,384]{1,0:T(8,128)(2,1)S(1)} %copy-done.16, bf16[1024,384]{1,0:T(8,128)(2,1)S(1)} %copy-done.17, ...), custom_call_target="tpu_custom_call" | custom-call | flops 3623878656 | bytes 15728640 | tf_op jit(solution)/shard_map/joint_backward/pallas_call | solution.py:596
  412.9 2.6 collective-permute-done.31
  415.5 1.5 collective-permute-start.32
  419.6 2.7 collective-permute-start.27
  423.5 3.8 collective-permute-start.29
  427.7 3.6 collective-permute-done.38
  432.7 15.0 %collective-permute-done.36 = bf16[2,96,1920]{2,1,0:T(8,128)(2,1)S(1)} collective-permute-done((bf16[2,96,1920]{2,1,0:T(8,128)(2,1)S(1)}, bf16[2,96,1920]{2,1,0:T(8,128)(2,1)S(1)}, u32[]{:S(2)}, u32[]{:S(2)}) %collective-permute-start.36) | collective-permute-done | bytes 737312 | tf_op jit(solution)/shard_map/ppermute | solution.py:615
  449.3 9.0 %collective-permute-done.41 = bf16[2,96,1152]{2,1,0:T(8,128)(2,1)S(1)} collective-permute-done((bf16[2,96,1152]{2,1,0:T(8,128)(2,1)S(1)}, bf16[2,96,1152]{2,1,0:T(8,128)(2,1)S(1)}, u32[]{:S(2)}, u32[]{:S(2)}) %collective-permute-start.41) | collective-permute-done | bytes 442400 | tf_op jit(solution)/shard_map/ppermute | solution.py:615
  458.3 1.3 collective-permute-start.37
  459.7 6.1 %collective-permute-done.37 = bf16[96,1920]{1,0:T(8,128)(2,1)S(1)} collective-permute-done((bf16[96,1920]{1,0:T(8,128)(2,1)S(1)}, bf16[96,1920]{1,0:T(8,128)(2,1)S(1)}, u32[]{:S(2)}, u32[]{:S(2)}) %collective-permute-start.37) | collective-permute-done | bytes 368672 | tf_op jit(solution)/shard_map/ppermute | solution.py:615
  466.9 4.8 collective-permute-done.42
  471.9 4.6 collective-permute-start.43
  476.5 1.4 collective-permute-start.51
  479.2 10.9 %collective-permute-done.43 = bf16[96,3072]{1,0:T(8,128)(2,1)S(1)} collective-permute-done((bf16[96,3072]{1,0:T(8,128)(2,1)S(1)}, bf16[96,3072]{1,0:T(8,128)(2,1)S(1)}, u32[]{:S(2)}, u32[]{:S(2)}) %collective-permute-start.43) | collective-permute-done | bytes 589856 | tf_op jit(solution)/shard_map/ppermute | solution.py:652
  491.0 17.6 %collective-permute-done.51 = bf16[96,6144]{1,0:T(8,128)(2,1)S(1)} collective-permute-done((bf16[96,6144]{1,0:T(8,128)(2,1)S(1)}, bf16[96,6144]{1,0:T(8,128)(2,1)S(1)}, u32[]{:S(2)}, u32[]{:S(2)}) %collective-permute-start.51) | collective-permute-done | bytes 1179680 | tf_op jit(solution)/shard_map/ppermute | solution.py:652
  509.7 1.9 convert_element_type.227
  511.8 1.3 collective-permute-start.45
  513.4 1.3 collective-permute-start.53
  514.7 10.7 %collective-permute-done.45 = bf16[96,3072]{1,0:T(8,128)(2,1)S(1)} collective-permute-done((bf16[96,3072]{1,0:T(8,128)(2,1)S(1)}, bf16[96,3072]{1,0:T(8,128)(2,1)S(1)}, u32[]{:S(2)}, u32[]{:S(2)}) %collective-permute-start.45) | collective-permute-done | bytes 589856 | tf_op jit(solution)/shard_map/ppermute | solution.py:652
  526.4 28.2 %collective-permute-done.53 = bf16[96,6144]{1,0:T(8,128)(2,1)S(1)} collective-permute-done((bf16[96,6144]{1,0:T(8,128)(2,1)S(1)}, bf16[96,6144]{1,0:T(8,128)(2,1)S(1)}, u32[]{:S(2)}, u32[]{:S(2)}) %collective-permute-start.53) | collective-permute-done | bytes 1179680 | tf_op jit(solution)/shard_map/ppermute | solution.py:652
  (293 shorter events, 61.0 us)
Async XLA Ops:
  0.6 55.1 %copy-start = (s32[4,1024]{1,0:T(4,128)S(1)}, s32[4,1024]{1,0:T(4,128)}, u32[]{:S(2)}) copy-start(s32[4,1024]{1,0:T(4,128)} %param.18) | copy-start | bytes 49156
  6.1 61.2 %copy-start.43 = (bf16[1,2304]{1,0:T(2,128)(2,1)}, bf16[1,2304]{1,0:T(2,128)(2,1)S(1)}, u32[]{:S(2)}) copy-start(bf16[1,2304]{1,0:T(2,128)(2,1)S(1)} %reshape.172) | copy-start | bytes 13828
  7.4 46.6 %collective-permute-start.4 = (bf16[112,2304]{1,0:T(8,128)(2,1)S(1)}, bf16[112,2304]{1,0:T(8,128)(2,1)S(1)}, u32[]{:S(2)}, u32[]{:S(2)}) collective-permute-start(bf16[112,2304]{1,0:T(8,128)(2,1)S(1)} %fusion.2.refs_0_), channel_id=1, source_target_pairs={{0,8},{4,12},{8,0},{12,4},{16,24},{20,28},{24,16},{28,20},{1,9},{5... | collective-permute-start | bytes 1548296 | tf_op jit(solution)/shard_map/ppermute | solution.py:615
  10.4 48.0 %collective-permute-start.6 = (bf16[112,2304]{1,0:T(8,128)(2,1)S(1)}, bf16[112,2304]{1,0:T(8,128)(2,1)}, u32[]{:S(2)}, u32[]{:S(2)}) collective-permute-start(bf16[112,2304]{1,0:T(8,128)(2,1)S(1)} %fusion.2.refs_0_), channel_id=1, source_target_pairs={{0,16},{4,20},{8,24},{12,28},{16,0},{20,4},{24,8},{28,12},{1,17},{... | collective-permute-start | bytes 1548296 | tf_op jit(solution)/shard_map/ppermute | solution.py:615
  11.9 46.6 %collective-permute-start.3 = (bf16[112,2304]{1,0:T(8,128)(2,1)S(1)}, bf16[112,2304]{1,0:T(8,128)(2,1)}, u32[]{:S(2)}, u32[]{:S(2)}) collective-permute-start(bf16[112,2304]{1,0:T(8,128)(2,1)S(1)} %fusion.2.refs_0_), channel_id=1, source_target_pairs={{0,4},{4,0},{8,12},{12,8},{16,20},{20,16},{24,28},{28,24},{1,5},{5... | collective-permute-start | bytes 1548296 | tf_op jit(solution)/shard_map/ppermute | solution.py:615
  12.9 29.6 %collective-permute-start = (bf16[256,768]{1,0:T(8,128)(2,1)}, bf16[256,768]{1,0:T(8,128)(2,1)}, u32[]{:S(2)}, u32[]{:S(2)}) collective-permute-start(bf16[256,768]{1,0:T(8,128)(2,1)} %get-tuple-element.129), channel_id=1, source_target_pairs={{0,2},{1,3},{2,0},{3,1},{4,6},{5,7},{6,4},{7,5},{8,10},{9,11},{10,... | collective-permute-start | bytes 1179656 | tf_op jit(solution)/shard_map/ppermute | solution.py:626
  15.5 28.8 %collective-permute-start.1 = (bf16[256,768]{1,0:T(8,128)(2,1)S(1)}, bf16[256,768]{1,0:T(8,128)(2,1)}, u32[]{:S(2)}, u32[]{:S(2)}) collective-permute-start(bf16[256,768]{1,0:T(8,128)(2,1)S(1)} %get-tuple-element.131), channel_id=1, source_target_pairs={{0,1},{1,2},{2,3},{3,0},{4,5},{5,6},{6,7},{7,4},{8,9},{9,10},{10,1... | collective-permute-start | bytes 1179656 | tf_op jit(solution)/shard_map/ppermute | solution.py:626
  17.4 180.4 %copy-start.5 = (bf16[96,6912]{1,0:T(8,128)(2,1)}, bf16[96,6912]{1,0:T(8,128)(2,1)S(1)}, u32[]{:S(2)}) copy-start(bf16[96,6912]{1,0:T(8,128)(2,1)S(1)} %slice_dynamic-update-slice_fusion.6.refs_0_) | copy-start | bytes 3981316
  42.5 10.7 %collective-permute-start.2 = (bf16[256,768]{1,0:T(8,128)(2,1)S(1)}, bf16[256,768]{1,0:T(8,128)(2,1)S(1)}, u32[]{:S(2)}, u32[]{:S(2)}) collective-permute-start(bf16[256,768]{1,0:T(8,128)(2,1)S(1)} %get-tuple-element.128), channel_id=1, source_target_pairs={{0,3},{1,0},{2,1},{3,2},{4,7},{5,4},{6,5},{7,6},{8,11},{9,8},{10,9... | collective-permute-start | bytes 1179656 | tf_op jit(solution)/shard_map/ppermute | solution.py:626
  54.0 12.6 %collective-permute-start.8 = (bf16[112,2304]{1,0:T(8,128)(2,1)S(1)}, bf16[112,2304]{1,0:T(8,128)(2,1)}, u32[]{:S(2)}, u32[]{:S(2)}) collective-permute-start(bf16[112,2304]{1,0:T(8,128)(2,1)S(1)} %collective-permute-done.4.refs_2_), channel_id=1, source_target_pairs={{0,16},{4,20},{8,24},{12,28},{16,0},{20,4},{24,8},{28,12},{1,17},{... | collective-permute-start | bytes 1548296 | tf_op jit(solution)/shard_map/ppermute | solution.py:615
  55.6 27.3 %collective-permute-start.12 = (bf16[256,768]{1,0:T(8,128)(2,1)}, bf16[256,768]{1,0:T(8,128)(2,1)}, u32[]{:S(2)}, u32[]{:S(2)}) collective-permute-start(bf16[256,768]{1,0:T(8,128)(2,1)} %get-tuple-element.126), channel_id=1, source_target_pairs={{0,2},{1,3},{2,0},{3,1},{4,6},{5,7},{6,4},{7,5},{8,10},{9,11},{10,... | collective-permute-start | bytes 1179656 | tf_op jit(solution)/shard_map/ppermute | solution.py:626
  55.7 29.0 %collective-permute-start.13 = (bf16[256,768]{1,0:T(8,128)(2,1)}, bf16[256,768]{1,0:T(8,128)(2,1)}, u32[]{:S(2)}, u32[]{:S(2)}) collective-permute-start(bf16[256,768]{1,0:T(8,128)(2,1)} %get-tuple-element.125), channel_id=1, source_target_pairs={{0,1},{1,2},{2,3},{3,0},{4,5},{5,6},{6,7},{7,4},{8,9},{9,10},{10,1... | collective-permute-start | bytes 1179656 | tf_op jit(solution)/shard_map/ppermute | solution.py:626
  58.4 115.8 %copy-start.8 = (s32[1,1024]{1,0:T(1,128)}, s32[1,1024]{1,0:T(1,128)S(1)}, u32[]{:S(2)}) copy-start(s32[1,1024]{1,0:T(1,128)S(1)} %constant_dynamic-slice_fusion.segq_ref) | copy-start | bytes 12292
  58.4 28.0 %collective-permute-start.5 = (bf16[112,2304]{1,0:T(8,128)(2,1)S(1)}, bf16[112,2304]{1,0:T(8,128)(2,1)}, u32[]{:S(2)}, u32[]{:S(2)}) collective-permute-start(bf16[112,2304]{1,0:T(8,128)(2,1)S(1)} %collective-permute-done.4.refs_2_), channel_id=1, source_target_pairs={{0,4},{4,0},{8,12},{12,8},{16,20},{20,16},{24,28},{28,24},{1,5},{5... | collective-permute-start | bytes 1548296 | tf_op jit(solution)/shard_map/ppermute | solution.py:615
  58.5 28.0 %collective-permute-start.7 = (bf16[112,2304]{1,0:T(8,128)(2,1)}, bf16[112,2304]{1,0:T(8,128)(2,1)}, u32[]{:S(2)}, u32[]{:S(2)}) collective-permute-start(bf16[112,2304]{1,0:T(8,128)(2,1)} %collective-permute-done.6.refs_4_), channel_id=1, source_target_pairs={{0,4},{4,0},{8,12},{12,8},{16,20},{20,16},{24,28},{28,24},{1,5},{5... | collective-permute-start | bytes 1548296 | tf_op jit(solution)/shard_map/ppermute | solution.py:615
  66.5 19.9 %collective-permute-start.9 = (bf16[112,2304]{1,0:T(8,128)(2,1)}, bf16[112,2304]{1,0:T(8,128)(2,1)}, u32[]{:S(2)}, u32[]{:S(2)}) collective-permute-start(bf16[112,2304]{1,0:T(8,128)(2,1)} %collective-permute-done.8.refs_6_), channel_id=1, source_target_pairs={{0,4},{4,0},{8,12},{12,8},{16,20},{20,16},{24,28},{28,24},{1,5},{5... | collective-permute-start | bytes 1548296 | tf_op jit(solution)/shard_map/ppermute | solution.py:615
  67.2 130.5 %copy-start.9 = (s32[8]{0:T(128)}, s32[8]{0:T(128)S(1)}, u32[]{:S(2)}) copy-start(s32[8]{0:T(128)S(1)} %fusion.5.flags_ref) | copy-start | bytes 100
  67.2 30.4 %slice-start = ((bf16[1,2304]{1,0:T(2,128)(2,1)}), bf16[1,1152]{1,0:T(2,128)(2,1)S(1)}, s32[]{:S(2)}) async-start(bf16[1,2304]{1,0:T(2,128)(2,1)} %copy-done.43), calls=%async_computation | async-start | bytes 9216 | tf_op jit(solution)/shard_map/slice | solution.py:729
  67.5 130.3 %copy-start.2 = (s32[1024,1]{1,0:T(8,128)}, s32[1024,1]{1,0:T(8,128)S(1)}, u32[]{:S(2)}) copy-start(s32[1024,1]{1,0:T(8,128)S(1)} %copy.37.segk_ref.seg_ref) | copy-start | bytes 12292
  82.9 11.0 %collective-permute-start.14 = (bf16[256,768]{1,0:T(8,128)(2,1)S(1)}, bf16[256,768]{1,0:T(8,128)(2,1)S(1)}, u32[]{:S(2)}, u32[]{:S(2)}) collective-permute-start(bf16[256,768]{1,0:T(8,128)(2,1)S(1)} %get-tuple-element.124), channel_id=1, source_target_pairs={{0,3},{1,0},{2,1},{3,2},{4,7},{5,4},{6,5},{7,6},{8,11},{9,8},{10,9... | collective-permute-start | bytes 1179656 | tf_op jit(solution)/shard_map/ppermute | solution.py:626
  86.5 32.2 %collective-permute-start.10 = (bf16[96,6912]{1,0:T(8,128)(2,1)S(1)}, bf16[96,6912]{1,0:T(8,128)(2,1)}, u32[]{:S(2)}, u32[]{:S(2)}) collective-permute-start(bf16[96,6912]{1,0:T(8,128)(2,1)S(1)} %slice_dynamic-update-slice_fusion.6.refs_0_), channel_id=1, source_target_pairs={{0,8},{4,12},{8,0},{12,4},{16,24},{20,28},{24,16},{28,20},{1,9},{5... | collective-permute-start | bytes 3981320 | tf_op jit(solution)/shard_map/ppermute | solution.py:615
  86.9 58.5 %collective-permute-start.11 = (bf16[96,6912]{1,0:T(8,128)(2,1)S(1)}, bf16[96,6912]{1,0:T(8,128)(2,1)}, u32[]{:S(2)}, u32[]{:S(2)}) collective-permute-start(bf16[96,6912]{1,0:T(8,128)(2,1)S(1)} %slice_dynamic-update-slice_fusion.6.refs_0_), channel_id=1, source_target_pairs={{0,16},{4,20},{8,24},{12,28},{16,0},{20,4},{24,8},{28,12},{1,17},{... | collective-permute-start | bytes 3981320 | tf_op jit(solution)/shard_map/ppermute | solution.py:615
  88.6 58.5 %collective-permute-start.18 = (bf16[96,6912]{1,0:T(8,128)(2,1)S(1)}, bf16[96,6912]{1,0:T(8,128)(2,1)}, u32[]{:S(2)}, u32[]{:S(2)}) collective-permute-start(bf16[96,6912]{1,0:T(8,128)(2,1)S(1)} %slice_dynamic-update-slice_fusion.6.refs_0_), channel_id=1, source_target_pairs={{0,24},{4,28},{8,16},{12,20},{16,8},{20,12},{24,0},{28,4},{1,25},{... | collective-permute-start | bytes 3981320 | tf_op jit(solution)/shard_map/ppermute | solution.py:615
  96.9 100.8 %collective-permute-start.15 = (bf16[96,6912]{1,0:T(8,128)(2,1)S(1)}, bf16[96,6912]{1,0:T(8,128)(2,1)}, u32[]{:S(2)}, u32[]{:S(2)}) collective-permute-start(bf16[96,6912]{1,0:T(8,128)(2,1)S(1)} %slice_dynamic-update-slice_fusion.6.refs_0_), channel_id=1, source_target_pairs={{0,4},{4,0},{8,12},{12,8},{16,20},{20,16},{24,28},{28,24},{1,5},{5... | collective-permute-start | bytes 3981320 | tf_op jit(solution)/shard_map/ppermute | solution.py:615
  98.4 99.4 %copy-start.7 = (f32[1,768]{1,0:T(1,128)}, f32[1,768]{1,0:T(1,128)S(1)}, u32[]{:S(2)}) copy-start(f32[1,768]{1,0:T(1,128)S(1)} %reshape.179.gain_ref) | copy-start | bytes 9220
  118.6 79.1 %collective-permute-start.16 = (bf16[96,6912]{1,0:T(8,128)(2,1)}, bf16[96,6912]{1,0:T(8,128)(2,1)S(1)}, u32[]{:S(2)}, u32[]{:S(2)}) collective-permute-start(bf16[96,6912]{1,0:T(8,128)(2,1)} %collective-permute-done.10.refs_2_), channel_id=1, source_target_pairs={{0,4},{4,0},{8,12},{12,8},{16,20},{20,16},{24,28},{28,24},{1,5},{5... | collective-permute-start | bytes 3981320 | tf_op jit(solution)/shard_map/ppermute | solution.py:615
  145.4 52.4 %collective-permute-start.17 = (bf16[96,6912]{1,0:T(8,128)(2,1)}, bf16[96,6912]{1,0:T(8,128)(2,1)S(1)}, u32[]{:S(2)}, u32[]{:S(2)}) collective-permute-start(bf16[96,6912]{1,0:T(8,128)(2,1)} %collective-permute-done.11.refs_4_), channel_id=1, source_target_pairs={{0,4},{4,0},{8,12},{12,8},{16,20},{20,16},{24,28},{28,24},{1,5},{5... | collective-permute-start | bytes 3981320 | tf_op jit(solution)/shard_map/ppermute | solution.py:615
  147.1 50.7 %collective-permute-start.19 = (bf16[96,6912]{1,0:T(8,128)(2,1)}, bf16[96,6912]{1,0:T(8,128)(2,1)S(1)}, u32[]{:S(2)}, u32[]{:S(2)}) collective-permute-start(bf16[96,6912]{1,0:T(8,128)(2,1)} %collective-permute-done.18.refs_6_), channel_id=1, source_target_pairs={{0,4},{4,0},{8,12},{12,8},{16,20},{20,16},{24,28},{28,24},{1,5},{5... | collective-permute-start | bytes 3981320 | tf_op jit(solution)/shard_map/ppermute | solution.py:615
  256.8 61.2 %collective-permute-start.23 = (bf16[4,96,3072]{2,1,0:T(8,128)(2,1)}, bf16[4,96,3072]{2,1,0:T(8,128)(2,1)}, u32[]{:S(2)}, u32[]{:S(2)}) collective-permute-start(bf16[4,96,3072]{2,1,0:T(8,128)(2,1)} %get-tuple-element.73), channel_id=1, source_target_pairs={{0,4},{4,0},{8,12},{12,8},{16,20},{20,16},{24,28},{28,24},{1,5},{5... | collective-permute-start | bytes 7077896 | tf_op jit(solution)/shard_map/ppermute | solution.py:615
  271.1 1.3 collective-permute-start.46
  272.3 3.8 collective-permute-start.47
  273.3 49.9 %collective-permute-start.24 = (bf16[4,96,3072]{2,1,0:T(8,128)(2,1)}, bf16[4,96,3072]{2,1,0:T(8,128)(2,1)}, u32[]{:S(2)}, u32[]{:S(2)}) collective-permute-start(bf16[4,96,3072]{2,1,0:T(8,128)(2,1)} %get-tuple-element.75), channel_id=1, source_target_pairs={{0,4},{4,0},{8,12},{12,8},{16,20},{20,16},{24,28},{28,24},{1,5},{5... | collective-permute-start | bytes 7077896 | tf_op jit(solution)/shard_map/ppermute | solution.py:615
  276.2 3.8 collective-permute-start.48
  278.5 39.5 %copy-start.29 = (bf16[4,96,3072]{2,1,0:T(8,128)(2,1)S(1)}, bf16[4,96,3072]{2,1,0:T(8,128)(2,1)}, u32[]{:S(2)}) copy-start(bf16[4,96,3072]{2,1,0:T(8,128)(2,1)} %get-tuple-element.72) | copy-start | bytes 7077892
  278.5 31.6 %collective-permute-start.20 = (bf16[256,768]{1,0:T(8,128)(2,1)S(1)}, bf16[256,768]{1,0:T(8,128)(2,1)}, u32[]{:S(2)}, u32[]{:S(2)}) collective-permute-start(bf16[256,768]{1,0:T(8,128)(2,1)S(1)} %get-tuple-element.122), channel_id=1, source_target_pairs={{0,2},{1,3},{2,0},{3,1},{4,6},{5,7},{6,4},{7,5},{8,10},{9,11},{10,... | collective-permute-start | bytes 1179656 | tf_op jit(solution)/shard_map/ppermute | solution.py:626
  280.0 6.8 %collective-permute-start.49 = (f32[48,128]{1,0:T(8,128)S(1)}, f32[48,128]{1,0:T(8,128)S(1)}, u32[]{:S(2)}, u32[]{:S(2)}) collective-permute-start(f32[48,128]{1,0:T(8,128)S(1)} %add.290), channel_id=1, source_target_pairs={{0,1},{1,0},{2,3},{3,2},{4,5},{5,4},{6,7},{7,6},{8,9},{9,8},{10,11... | collective-permute-start | bytes 73736 | tf_op jit(solution)/shard_map/ppermute | solution.py:671
  287.4 20.7 %collective-permute-start.50 = (f32[48,128]{1,0:T(8,128)}, f32[48,128]{1,0:T(8,128)}, u32[]{:S(2)}, u32[]{:S(2)}) collective-permute-start(f32[48,128]{1,0:T(8,128)} %add.291), channel_id=1, source_target_pairs={{0,2},{1,3},{2,0},{3,1},{4,6},{5,7},{6,4},{7,5},{8,10},{9,11},{10,... | collective-permute-start | bytes 73736 | tf_op jit(solution)/shard_map/ppermute | solution.py:671
  292.3 19.6 %collective-permute-start.21 = (bf16[256,768]{1,0:T(8,128)(2,1)S(1)}, bf16[256,768]{1,0:T(8,128)(2,1)S(1)}, u32[]{:S(2)}, u32[]{:S(2)}) collective-permute-start(bf16[256,768]{1,0:T(8,128)(2,1)S(1)} %get-tuple-element.121), channel_id=1, source_target_pairs={{0,1},{1,2},{2,3},{3,0},{4,5},{5,6},{6,7},{7,4},{8,9},{9,10},{10,1... | collective-permute-start | bytes 1179656 | tf_op jit(solution)/shard_map/ppermute | solution.py:626
  308.1 9.1 %collective-permute-start.22 = (bf16[256,768]{1,0:T(8,128)(2,1)S(1)}, bf16[256,768]{1,0:T(8,128)(2,1)S(1)}, u32[]{:S(2)}, u32[]{:S(2)}) collective-permute-start(bf16[256,768]{1,0:T(8,128)(2,1)S(1)} %get-tuple-element.120), channel_id=1, source_target_pairs={{0,3},{1,0},{2,1},{3,2},{4,7},{5,4},{6,5},{7,6},{8,11},{9,8},{10,9... | collective-permute-start | bytes 1179656 | tf_op jit(solution)/shard_map/ppermute | solution.py:626
  321.6 39.6 %collective-permute-start.25 = (bf16[2,96,3072]{2,1,0:T(8,128)(2,1)}, bf16[2,96,3072]{2,1,0:T(8,128)(2,1)}, u32[]{:S(2)}, u32[]{:S(2)}) collective-permute-start(bf16[2,96,3072]{2,1,0:T(8,128)(2,1)} %slice.209), channel_id=1, source_target_pairs={{0,8},{4,12},{8,0},{12,4},{16,24},{20,28},{24,16},{28,20},{1,9},{5... | collective-permute-start | bytes 3538952 | tf_op jit(solution)/shard_map/ppermute | solution.py:615
  326.8 37.1 %collective-permute-start.26 = (bf16[2,96,3072]{2,1,0:T(8,128)(2,1)}, bf16[2,96,3072]{2,1,0:T(8,128)(2,1)}, u32[]{:S(2)}, u32[]{:S(2)}) collective-permute-start(bf16[2,96,3072]{2,1,0:T(8,128)(2,1)} %slice.269), channel_id=1, source_target_pairs={{0,16},{4,20},{8,24},{12,28},{16,0},{20,4},{24,8},{28,12},{1,17},{... | collective-permute-start | bytes 3538952 | tf_op jit(solution)/shard_map/ppermute | solution.py:615
  410.6 1.2 collective-permute-start.30
  410.8 12.6 %collective-permute-start.35 = (bf16[4,96,1920]{2,1,0:T(8,128)(2,1)S(1)}, bf16[4,96,1920]{2,1,0:T(8,128)(2,1)S(1)}, u32[]{:S(2)}, u32[]{:S(2)}) collective-permute-start(bf16[4,96,1920]{2,1,0:T(8,128)(2,1)S(1)} %pad_maximum_fusion), channel_id=1, source_target_pairs={{0,4},{4,0},{8,12},{12,8},{16,20},{20,16},{24,28},{28,24},{1,5},{5... | collective-permute-start | bytes 4423688 | tf_op jit(solution)/shard_map/ppermute | solution.py:615
  411.8 3.7 collective-permute-start.31
  415.5 3.8 collective-permute-start.32
  417.1 14.2 %collective-permute-start.38 = (bf16[96,3072]{1,0:T(8,128)(2,1)S(1)}, bf16[96,3072]{1,0:T(8,128)(2,1)S(1)}, u32[]{:S(2)}, u32[]{:S(2)}) collective-permute-start(bf16[96,3072]{1,0:T(8,128)(2,1)S(1)} %slice_bitcast_fusion.2), channel_id=1, source_target_pairs={{0,16},{4,20},{8,24},{12,28},{16,0},{20,4},{24,8},{28,12},{1,17},{... | collective-permute-start | bytes 1769480 | tf_op jit(solution)/shard_map/ppermute | solution.py:615
  417.7 14.8 %collective-permute-start.39 = (bf16[96,3072]{1,0:T(8,128)(2,1)S(1)}, bf16[96,3072]{1,0:T(8,128)(2,1)S(1)}, u32[]{:S(2)}, u32[]{:S(2)}) collective-permute-start(bf16[96,3072]{1,0:T(8,128)(2,1)S(1)} %slice_bitcast_fusion), channel_id=1, source_target_pairs={{0,8},{4,12},{8,0},{12,4},{16,24},{20,28},{24,16},{28,20},{1,9},{5... | collective-permute-start | bytes 1769480 | tf_op jit(solution)/shard_map/ppermute | solution.py:615
  419.4 3.8 collective-permute-start.33
  419.6 59.5 %collective-permute-start.27 = (bf16[256,768]{1,0:T(8,128)(2,1)S(1)}, bf16[256,768]{1,0:T(8,128)(2,1)S(1)}, u32[]{:S(2)}, u32[]{:S(2)}) collective-permute-start(bf16[256,768]{1,0:T(8,128)(2,1)S(1)} %get-tuple-element.118), channel_id=1, source_target_pairs={{0,2},{1,3},{2,0},{3,1},{4,6},{5,7},{6,4},{7,5},{8,10},{9,11},{10,... | collective-permute-start | bytes 1179656 | tf_op jit(solution)/shard_map/ppermute | solution.py:626
  423.2 86.4 %collective-permute-start.28 = (bf16[256,768]{1,0:T(8,128)(2,1)S(1)}, bf16[256,768]{1,0:T(8,128)(2,1)S(1)}, u32[]{:S(2)}, u32[]{:S(2)}) collective-permute-start(bf16[256,768]{1,0:T(8,128)(2,1)S(1)} %get-tuple-element.117), channel_id=1, source_target_pairs={{0,1},{1,2},{2,3},{3,0},{4,5},{5,6},{6,7},{7,4},{8,9},{9,10},{10,1... | collective-permute-start | bytes 1179656 | tf_op jit(solution)/shard_map/ppermute | solution.py:626
  423.5 86.2 %collective-permute-start.29 = (bf16[256,768]{1,0:T(8,128)(2,1)S(1)}, bf16[256,768]{1,0:T(8,128)(2,1)S(1)}, u32[]{:S(2)}, u32[]{:S(2)}) collective-permute-start(bf16[256,768]{1,0:T(8,128)(2,1)S(1)} %get-tuple-element.116), channel_id=1, source_target_pairs={{0,3},{1,0},{2,1},{3,2},{4,7},{5,4},{6,5},{7,6},{8,11},{9,8},{10,9... | collective-permute-start | bytes 1179656 | tf_op jit(solution)/shard_map/ppermute | solution.py:626
  431.3 16.4 %collective-permute-start.36 = (bf16[2,96,1920]{2,1,0:T(8,128)(2,1)S(1)}, bf16[2,96,1920]{2,1,0:T(8,128)(2,1)S(1)}, u32[]{:S(2)}, u32[]{:S(2)}) collective-permute-start(bf16[2,96,1920]{2,1,0:T(8,128)(2,1)S(1)} %slice.219), channel_id=1, source_target_pairs={{0,8},{4,12},{8,0},{12,4},{16,24},{20,28},{24,16},{28,20},{1,9},{5... | collective-permute-start | bytes 2211848 | tf_op jit(solution)/shard_map/ppermute | solution.py:615
  432.5 15.4 %collective-permute-start.40 = (bf16[4,96,1152]{2,1,0:T(8,128)(2,1)S(1)}, bf16[4,96,1152]{2,1,0:T(8,128)(2,1)S(1)}, u32[]{:S(2)}, u32[]{:S(2)}) collective-permute-start(bf16[4,96,1152]{2,1,0:T(8,128)(2,1)S(1)} %get-tuple-element.99), channel_id=1, source_target_pairs={{0,4},{4,0},{8,12},{12,8},{16,20},{20,16},{24,28},{28,24},{1,5},{5... | collective-permute-start | bytes 2654216 | tf_op jit(solution)/shard_map/ppermute | solution.py:615
  447.7 28.8 %collective-permute-start.34 = (f32[24,128]{1,0:T(8,128)S(1)}, f32[24,128]{1,0:T(8,128)S(1)}, u32[]{:S(2)}, u32[]{:S(2)}) collective-permute-start(f32[24,128]{1,0:T(8,128)S(1)} %add.271), channel_id=1, source_target_pairs={{0,2},{1,3},{2,0},{3,1},{4,6},{5,7},{6,4},{7,5},{8,10},{9,11},{10,... | collective-permute-start | bytes 36872 | tf_op jit(solution)/shard_map/ppermute | solution.py:671
  448.2 10.1 %collective-permute-start.41 = (bf16[2,96,1152]{2,1,0:T(8,128)(2,1)S(1)}, bf16[2,96,1152]{2,1,0:T(8,128)(2,1)S(1)}, u32[]{:S(2)}, u32[]{:S(2)}) collective-permute-start(bf16[2,96,1152]{2,1,0:T(8,128)(2,1)S(1)} %slice.277), channel_id=1, source_target_pairs={{0,16},{4,20},{8,24},{12,28},{16,0},{20,4},{24,8},{28,12},{1,17},{... | collective-permute-start | bytes 1327112 | tf_op jit(solution)/shard_map/ppermute | solution.py:615
  458.3 7.5 %collective-permute-start.37 = (bf16[96,1920]{1,0:T(8,128)(2,1)S(1)}, bf16[96,1920]{1,0:T(8,128)(2,1)S(1)}, u32[]{:S(2)}, u32[]{:S(2)}) collective-permute-start(bf16[96,1920]{1,0:T(8,128)(2,1)S(1)} %slice_bitcast_fusion.4), channel_id=1, source_target_pairs={{0,16},{4,20},{8,24},{12,28},{16,0},{20,4},{24,8},{28,12},{1,17},{... | collective-permute-start | bytes 1105928 | tf_op jit(solution)/shard_map/ppermute | solution.py:615
  465.8 5.9 %collective-permute-start.42 = (bf16[96,1152]{1,0:T(8,128)(2,1)S(1)}, bf16[96,1152]{1,0:T(8,128)(2,1)S(1)}, u32[]{:S(2)}, u32[]{:S(2)}) collective-permute-start(bf16[96,1152]{1,0:T(8,128)(2,1)S(1)} %slice_bitcast_fusion.6), channel_id=1, source_target_pairs={{0,8},{4,12},{8,0},{12,4},{16,24},{20,28},{24,16},{28,20},{1,9},{5... | collective-permute-start | bytes 663560 | tf_op jit(solution)/shard_map/ppermute | solution.py:615
  471.9 18.2 %collective-permute-start.43 = (bf16[96,3072]{1,0:T(8,128)(2,1)S(1)}, bf16[96,3072]{1,0:T(8,128)(2,1)S(1)}, u32[]{:S(2)}, u32[]{:S(2)}) collective-permute-start(bf16[96,3072]{1,0:T(8,128)(2,1)S(1)} %pad_maximum_fusion.3), channel_id=1, source_target_pairs={{0,1},{3,2},{4,5},{7,6},{8,9},{11,10},{12,13},{15,14},{16,17},{19,... | collective-permute-start | bytes 1769480 | tf_op jit(solution)/shard_map/ppermute | solution.py:652
  476.5 32.1 %collective-permute-start.51 = (bf16[96,6144]{1,0:T(8,128)(2,1)S(1)}, bf16[96,6144]{1,0:T(8,128)(2,1)S(1)}, u32[]{:S(2)}, u32[]{:S(2)}) collective-permute-start(bf16[96,6144]{1,0:T(8,128)(2,1)S(1)} %pad_maximum_fusion.1), channel_id=1, source_target_pairs={{0,1},{3,2},{4,5},{7,6},{8,9},{11,10},{12,13},{15,14},{16,17},{19,... | collective-permute-start | bytes 3538952 | tf_op jit(solution)/shard_map/ppermute | solution.py:652
  490.3 21.4 %collective-permute-start.44 = (bf16[96,3072]{1,0:T(8,128)(2,1)S(1)}, bf16[96,3072]{1,0:T(8,128)(2,1)S(1)}, u32[]{:S(2)}, u32[]{:S(2)}) collective-permute-start(bf16[96,3072]{1,0:T(8,128)(2,1)S(1)} %add_convert_fusion.10), channel_id=1, source_target_pairs={{1,2},{2,1},{5,6},{6,5},{9,10},{10,9},{13,14},{14,13},{17,18},{18,... | collective-permute-start | bytes 1769480 | tf_op jit(solution)/shard_map/ppermute | solution.py:652
  508.9 4.2 collective-permute-start.52
  511.8 13.6 %collective-permute-start.45 = (bf16[96,3072]{1,0:T(8,128)(2,1)S(1)}, bf16[96,3072]{1,0:T(8,128)(2,1)S(1)}, u32[]{:S(2)}, u32[]{:S(2)}) collective-permute-start(bf16[96,3072]{1,0:T(8,128)(2,1)S(1)} %add_convert_fusion.9), channel_id=1, source_target_pairs={{1,0},{2,3},{5,4},{6,7},{9,8},{10,11},{13,12},{14,15},{17,16},{18,... | collective-permute-start | bytes 1769480 | tf_op jit(solution)/shard_map/ppermute | solution.py:652
  513.4 41.2 %collective-permute-start.53 = (bf16[96,6144]{1,0:T(8,128)(2,1)S(1)}, bf16[96,6144]{1,0:T(8,128)(2,1)S(1)}, u32[]{:S(2)}, u32[]{:S(2)}) collective-permute-start(bf16[96,6144]{1,0:T(8,128)(2,1)S(1)} %add_convert_fusion.3), channel_id=1, source_target_pairs={{1,0},{2,3},{5,4},{6,7},{9,8},{10,11},{13,12},{14,15},{17,16},{18,... | collective-permute-start | bytes 3538952 | tf_op jit(solution)/shard_map/ppermute | solution.py:652
  526.4 28.4 %copy-start.45 = (f32[96,2304]{1,0:T(8,128)}, f32[96,2304]{1,0:T(8,128)S(1)}, u32[]{:S(2)}) copy-start(f32[96,2304]{1,0:T(8,128)S(1)} %slice_dynamic-update-slice_fusion) | copy-start | bytes 2654212
  (38 other events, 212.0 us)
